TPU v7x, 32 devices: a whole 2x2x4 slice. The times are simulated.
32 devices in a mesh: groups: 2 (over x), chan: 16 (over z, y, core).
Axes of the slice: x: 2, y: 2, z: 4, core: 2. Of those that a mesh axis runs over, the one named last changes fastest.
Arguments:
- spectra: bfloat16 [256, 8, 6144], P(('groups', 'chan')), parts along dimension 0
- bad_flag: int32 [256], P(('groups', 'chan')), parts along dimension 0, may hold values 0 or 1
- source_pick: int32 [32], P(('groups', 'chan')), parts along dimension 0, may hold values from 0 to 7
- lag_start: int32 [32], P(('groups', 'chan')), parts along dimension 0, may hold values from -1000 to -23
Outputs:
- correlations: float32 [16, 256, 1024], P(None, ('groups', 'chan')), parts along dimension 1
There are 2 independent parts, one for each index of `groups`. A program takes and returns all parts, laid end to end along the dimension named above; each array names one. Nothing has to cross between parts.
Inputs may be any that keep to these rules, and one draw needn't show every extreme that they name: Lag windows lie within -1000 to 1000: lag_start + 1023 <= 1000.
All inputs are finite; a program needn't handle non-finite values. No bound on the sum of `bad_flag` on one device may be relied on, other than what follows from the above.
Results may differ from a plain program's by a relative error of at most 0.0027.
Values may be sent and summed in bfloat16 or wider, within the bound.
No kernel may reach another device: no remote copies, remote signals or barrier semaphores. Data moves between devices by JAX's collectives and lax.ppermute only.
A program may use at most 64 MiB of HBM per device.

v0:
```python
import math

import jax
import jax.numpy as jnp
from jax import lax
from jax.sharding import PartitionSpec as P

SRC_DEV = 1
NFFT = 12000
LAGW = 1024
SMOOTH = 64


def broadcast(value, axis, source):
    kept = jnp.where(lax.axis_index(axis) == source, value, 0).astype(value.dtype)
    return lax.psum(kept, axis)


def build_table(bin_count):
    bin_index = jnp.arange(1, bin_count + 1, dtype=jnp.int32)
    lag_index = jnp.arange(LAGW, dtype=jnp.int32)
    turns = jnp.mod(bin_index[:, None] * lag_index[None, :], NFFT)
    angle = 2.0 * math.pi / NFFT * turns.astype(jnp.float32)
    return jnp.concatenate([jnp.cos(angle), -jnp.sin(angle)], axis=0).astype(jnp.bfloat16)


def pair_product(left_part, right_part):
    return jnp.einsum("swf,rwf->srf", left_part, right_part, preferred_element_type=jnp.float32)


def shards(spectra, bad_flag, source_pick, lag_start):
    receivers, windows, width_both = spectra.shape
    bin_count = width_both // 2
    owner_count = lax.axis_size("chan")
    channels = receivers * owner_count
    local_total = jnp.sum(spectra, axis=0, dtype=jnp.float32)
    channel_total = lax.psum(local_total, "chan")
    cleaned = spectra.astype(jnp.float32) - channel_total / channels
    blocks = cleaned.reshape(receivers, windows, 2, bin_count // SMOOTH, SMOOTH)
    block_level = jnp.mean(blocks[:, :, 0] ** 2 + blocks[:, :, 1] ** 2, axis=-1)
    keep = (1 - bad_flag).astype(jnp.float32)
    block_scale = keep[:, None, None] / jnp.sqrt(block_level + 1e-06)
    whitened = (
        (blocks * block_scale[:, :, None, :, None])
        .reshape(receivers, windows, width_both)
        .astype(jnp.bfloat16)
    )
    picked = jnp.take(whitened, source_pick, axis=0).astype(jnp.float32)
    bin_index = jnp.arange(1, bin_count + 1, dtype=jnp.int32)
    turns = jnp.mod(bin_index[None, :] * lag_start[:, None], NFFT)
    angle = 2.0 * math.pi / NFFT * turns.astype(jnp.float32)
    cosine = jnp.cos(angle)[:, None, :]
    sine_part = jnp.sin(angle)[:, None, :]
    real_src = picked[..., :bin_count]
    imag_src = picked[..., bin_count:]
    shifted = jnp.concatenate(
        [real_src * cosine + imag_src * sine_part, imag_src * cosine - real_src * sine_part],
        axis=-1,
    ).astype(jnp.bfloat16)
    real_rec = whitened[..., :bin_count]
    imag_rec = whitened[..., bin_count:]
    norm_factor = 1.0 / math.sqrt(windows * bin_count)

    def cross_rows(arrived):
        real_s = arrived[..., :bin_count]
        imag_s = arrived[..., bin_count:]
        cross_re = pair_product(real_s, real_rec) + pair_product(imag_s, imag_rec)
        cross_im = pair_product(real_s, imag_rec) - pair_product(imag_s, real_rec)
        return (jnp.concatenate([cross_re, cross_im], axis=-1) * norm_factor).astype(jnp.bfloat16)

    source_total = SRC_DEV * owner_count
    stacked = jnp.zeros((source_total, receivers, width_both), jnp.bfloat16)

    def owner_turn(owner_index, current):
        arrived = broadcast(shifted, "chan", owner_index)
        return lax.dynamic_update_slice_in_dim(
            current, cross_rows(arrived), owner_index * SRC_DEV, 0
        )

    stacked = lax.fori_loop(0, owner_count, owner_turn, stacked)
    lag_table = build_table(bin_count)
    flat = stacked.reshape(source_total * receivers, width_both)
    result = jnp.dot(flat, lag_table, preferred_element_type=jnp.float32)
    return result.reshape(source_total, receivers, LAGW)


def solution(mesh):
    in_specs = (
        P(("groups", "chan"), None, None),
        P(("groups", "chan")),
        P(("groups", "chan")),
        P(("groups", "chan")),
    )
    out_specs = P(None, ("groups", "chan"), None)
    return jax.shard_map(shards, mesh=mesh, in_specs=in_specs, out_specs=out_specs, check_vma=False)
```

profile of v0, /device:TPU:0, one launch (start us, length us, event | category | flops | bytes accessed | tf_op | source)
XLA Modules:
  0.0 1601.6 jit_solution(17770009232089719066)
XLA Ops:
  6.5 1.9 convert_reduce_fusion
  9.8 0.7 subtract_convert_fusion.1
  10.5 55.8 %cosine_convert_fusion = (bf16[3072,1024]{1,0:T(8,128)(2,1)}, bf16[3072,1024]{1,0:T(8,128)(2,1)}) fusion(s32[3072]{0:T(1024)S(1)} %iota_add_fusion), kind=kLoop, calls=%fused_computation.23 | loop fusion | flops 37748736 | bytes 12595200 | tf_op jit(solution)/shard_map/convert
  66.4 36.9 %all-reduce.3.cloned.1.call-done = f32[8,6144]{1,0:T(8,128)} async-done(((f32[8,6144]{1,0:T(8,128)}), f32[8,6144]{1,0:T(8,128)}) %all-reduce.3.cloned.1.call-update) | async-done | bytes 196624 | tf_op jit(solution)/shard_map/psum | solution.py:37
  103.2 0.9 broadcast_multiply_fusion
  104.2 1.3 convert_subtract_fusion
  105.5 2.4 reshape.194
  108.9 1.9 mul.121
  110.8 1.9 multiply_convert_fusion
  113.0 1475.7 %while.16 = (s32[]{:T(128)}, bf16[16,8,6144]{2,1,0:T(8,128)(2,1)S(1)}, bf16[1,8,6144]{2,1,0:T(8,128)(2,1)S(1)}, bf16[8,8,3072]{2,1,0:T(8,128)(2,1)S(1)}, bf16[8,...) while((s32[]{:T(128)}, bf16[16,8,6144]{2,1,0:T(8,128)(2,1)S(1)}, bf16[1,8,6144]{2,1,0:T(8,128)(2,1)S(1)}, ...), condition=%wide.region_5.6_spmd, body=%wide.region_3.0_spmd.sunk | while | flops 2211845 | bytes 3342495 | solution.py:80
  113.0 0.7 broadcast_select_fusion.2
  113.7 89.7 %all-reduce.5.cloned.1.call-done = bf16[1,8,6144]{2,1,0:T(8,128)(2,1)} async-done(((bf16[1,8,6144]{2,1,0:T(8,128)(2,1)}), bf16[1,8,6144]{2,1,0:T(8,128)(2,1)}) %all-reduce.5.cloned.1.call-update) | async-done | bytes 98320 | tf_op jit(solution)/shard_map/while/body/eval_jaxpr/psum | solution.py:16
  203.4 0.8 fusion.27
  204.3 1.0 fusion.28
  205.4 0.7 broadcast_select_fusion.2
  206.1 89.7 %all-reduce.5.cloned.1.call-done = bf16[1,8,6144]{2,1,0:T(8,128)(2,1)} async-done(((bf16[1,8,6144]{2,1,0:T(8,128)(2,1)}), bf16[1,8,6144]{2,1,0:T(8,128)(2,1)}) %all-reduce.5.cloned.1.call-update) | async-done | bytes 98320 | tf_op jit(solution)/shard_map/while/body/eval_jaxpr/psum | solution.py:16
  295.9 0.8 fusion.27
  296.7 1.0 fusion.28
  297.8 0.7 broadcast_select_fusion.2
  298.5 89.4 %all-reduce.5.cloned.1.call-done = bf16[1,8,6144]{2,1,0:T(8,128)(2,1)} async-done(((bf16[1,8,6144]{2,1,0:T(8,128)(2,1)}), bf16[1,8,6144]{2,1,0:T(8,128)(2,1)}) %all-reduce.5.cloned.1.call-update) | async-done | bytes 98320 | tf_op jit(solution)/shard_map/while/body/eval_jaxpr/psum | solution.py:16
  387.9 0.8 fusion.27
  388.8 1.0 fusion.28
  390.6 89.4 %all-reduce.5.cloned.1.call-done = bf16[1,8,6144]{2,1,0:T(8,128)(2,1)} async-done(((bf16[1,8,6144]{2,1,0:T(8,128)(2,1)}), bf16[1,8,6144]{2,1,0:T(8,128)(2,1)}) %all-reduce.5.cloned.1.call-update) | async-done | bytes 98320 | tf_op jit(solution)/shard_map/while/body/eval_jaxpr/psum | solution.py:16
  480.0 0.8 fusion.27
  480.9 1.0 fusion.28
  482.7 89.4 %all-reduce.5.cloned.1.call-done = bf16[1,8,6144]{2,1,0:T(8,128)(2,1)} async-done(((bf16[1,8,6144]{2,1,0:T(8,128)(2,1)}), bf16[1,8,6144]{2,1,0:T(8,128)(2,1)}) %all-reduce.5.cloned.1.call-update) | async-done | bytes 98320 | tf_op jit(solution)/shard_map/while/body/eval_jaxpr/psum | solution.py:16
  572.1 0.8 fusion.27
  573.0 1.0 fusion.28
  574.8 89.7 %all-reduce.5.cloned.1.call-done = bf16[1,8,6144]{2,1,0:T(8,128)(2,1)} async-done(((bf16[1,8,6144]{2,1,0:T(8,128)(2,1)}), bf16[1,8,6144]{2,1,0:T(8,128)(2,1)}) %all-reduce.5.cloned.1.call-update) | async-done | bytes 98320 | tf_op jit(solution)/shard_map/while/body/eval_jaxpr/psum | solution.py:16
  664.6 0.8 fusion.27
  665.4 1.0 fusion.28
  667.2 89.7 %all-reduce.5.cloned.1.call-done = bf16[1,8,6144]{2,1,0:T(8,128)(2,1)} async-done(((bf16[1,8,6144]{2,1,0:T(8,128)(2,1)}), bf16[1,8,6144]{2,1,0:T(8,128)(2,1)}) %all-reduce.5.cloned.1.call-update) | async-done | bytes 98320 | tf_op jit(solution)/shard_map/while/body/eval_jaxpr/psum | solution.py:16
  757.0 0.8 fusion.27
  757.8 1.0 fusion.28
  759.6 89.7 %all-reduce.5.cloned.1.call-done = bf16[1,8,6144]{2,1,0:T(8,128)(2,1)} async-done(((bf16[1,8,6144]{2,1,0:T(8,128)(2,1)}), bf16[1,8,6144]{2,1,0:T(8,128)(2,1)}) %all-reduce.5.cloned.1.call-update) | async-done | bytes 98320 | tf_op jit(solution)/shard_map/while/body/eval_jaxpr/psum | solution.py:16
  849.4 0.8 fusion.27
  850.2 1.0 fusion.28
  852.0 89.4 %all-reduce.5.cloned.1.call-done = bf16[1,8,6144]{2,1,0:T(8,128)(2,1)} async-done(((bf16[1,8,6144]{2,1,0:T(8,128)(2,1)}), bf16[1,8,6144]{2,1,0:T(8,128)(2,1)}) %all-reduce.5.cloned.1.call-update) | async-done | bytes 98320 | tf_op jit(solution)/shard_map/while/body/eval_jaxpr/psum | solution.py:16
  941.5 0.8 fusion.27
  942.3 1.0 fusion.28
  944.1 89.7 %all-reduce.5.cloned.1.call-done = bf16[1,8,6144]{2,1,0:T(8,128)(2,1)} async-done(((bf16[1,8,6144]{2,1,0:T(8,128)(2,1)}), bf16[1,8,6144]{2,1,0:T(8,128)(2,1)}) %all-reduce.5.cloned.1.call-update) | async-done | bytes 98320 | tf_op jit(solution)/shard_map/while/body/eval_jaxpr/psum | solution.py:16
  1033.9 0.8 fusion.27
  1034.7 1.0 fusion.28
  1035.8 0.7 broadcast_select_fusion.2
  1036.5 89.4 %all-reduce.5.cloned.1.call-done = bf16[1,8,6144]{2,1,0:T(8,128)(2,1)} async-done(((bf16[1,8,6144]{2,1,0:T(8,128)(2,1)}), bf16[1,8,6144]{2,1,0:T(8,128)(2,1)}) %all-reduce.5.cloned.1.call-update) | async-done | bytes 98320 | tf_op jit(solution)/shard_map/while/body/eval_jaxpr/psum | solution.py:16
  1126.0 0.8 fusion.27
  1126.8 1.0 fusion.28
  1128.6 89.7 %all-reduce.5.cloned.1.call-done = bf16[1,8,6144]{2,1,0:T(8,128)(2,1)} async-done(((bf16[1,8,6144]{2,1,0:T(8,128)(2,1)}), bf16[1,8,6144]{2,1,0:T(8,128)(2,1)}) %all-reduce.5.cloned.1.call-update) | async-done | bytes 98320 | tf_op jit(solution)/shard_map/while/body/eval_jaxpr/psum | solution.py:16
  1218.4 0.8 fusion.27
  1219.2 1.0 fusion.28
  1221.0 89.4 %all-reduce.5.cloned.1.call-done = bf16[1,8,6144]{2,1,0:T(8,128)(2,1)} async-done(((bf16[1,8,6144]{2,1,0:T(8,128)(2,1)}), bf16[1,8,6144]{2,1,0:T(8,128)(2,1)}) %all-reduce.5.cloned.1.call-update) | async-done | bytes 98320 | tf_op jit(solution)/shard_map/while/body/eval_jaxpr/psum | solution.py:16
  1310.5 0.8 fusion.27
  1311.3 1.0 fusion.28
  1313.1 89.4 %all-reduce.5.cloned.1.call-done = bf16[1,8,6144]{2,1,0:T(8,128)(2,1)} async-done(((bf16[1,8,6144]{2,1,0:T(8,128)(2,1)}), bf16[1,8,6144]{2,1,0:T(8,128)(2,1)}) %all-reduce.5.cloned.1.call-update) | async-done | bytes 98320 | tf_op jit(solution)/shard_map/while/body/eval_jaxpr/psum | solution.py:16
  1402.6 0.8 fusion.27
  1403.4 1.0 fusion.28
  1404.6 0.7 broadcast_select_fusion.2
  1405.2 89.4 %all-reduce.5.cloned.1.call-done = bf16[1,8,6144]{2,1,0:T(8,128)(2,1)} async-done(((bf16[1,8,6144]{2,1,0:T(8,128)(2,1)}), bf16[1,8,6144]{2,1,0:T(8,128)(2,1)}) %all-reduce.5.cloned.1.call-update) | async-done | bytes 98320 | tf_op jit(solution)/shard_map/while/body/eval_jaxpr/psum | solution.py:16
  1494.7 0.8 fusion.27
  1495.5 1.0 fusion.28
  1497.3 89.4 %all-reduce.5.cloned.1.call-done = bf16[1,8,6144]{2,1,0:T(8,128)(2,1)} async-done(((bf16[1,8,6144]{2,1,0:T(8,128)(2,1)}), bf16[1,8,6144]{2,1,0:T(8,128)(2,1)}) %all-reduce.5.cloned.1.call-update) | async-done | bytes 98320 | tf_op jit(solution)/shard_map/while/body/eval_jaxpr/psum | solution.py:16
  1586.8 0.8 fusion.27
  1587.6 1.0 fusion.28
  1588.7 6.4 fusion.12
  (91 shorter events, 10.2 us)
Async XLA Ops:
  6.5 96.7 %all-reduce.3.cloned.1.call-start = ((), (), s32[]{:S(2)}) async-start(), calls=%async_computation | async-start | bytes 393216 | tf_op jit(solution)/shard_map/psum | solution.py:37
  10.5 93.7 %copy-start = (bf16[8,8,6144]{2,1,0:T(8,128)(2,1)S(1)}, bf16[8,8,6144]{2,1,0:T(8,128)(2,1)}, u32[]{:S(2)}) copy-start(bf16[8,8,6144]{2,1,0:T(8,128)(2,1)} %param.6) | copy-start | bytes 2359300
  110.8 2.1 copy-start.1
  113.0 90.5 %all-reduce.5.cloned.1.call-start = ((), (), s32[]{:S(2)}) async-start(), calls=%async_computation.1 | async-start | bytes 196608 | tf_op jit(solution)/shard_map/while/body/eval_jaxpr/psum | solution.py:16
  205.4 90.5 %all-reduce.5.cloned.1.call-start = ((), (), s32[]{:S(2)}) async-start(), calls=%async_computation.1 | async-start | bytes 196608 | tf_op jit(solution)/shard_map/while/body/eval_jaxpr/psum | solution.py:16
  297.8 90.2 %all-reduce.5.cloned.1.call-start = ((), (), s32[]{:S(2)}) async-start(), calls=%async_computation.1 | async-start | bytes 196608 | tf_op jit(solution)/shard_map/while/body/eval_jaxpr/psum | solution.py:16
  389.9 90.2 %all-reduce.5.cloned.1.call-start = ((), (), s32[]{:S(2)}) async-start(), calls=%async_computation.1 | async-start | bytes 196608 | tf_op jit(solution)/shard_map/while/body/eval_jaxpr/psum | solution.py:16
  482.0 90.2 %all-reduce.5.cloned.1.call-start = ((), (), s32[]{:S(2)}) async-start(), calls=%async_computation.1 | async-start | bytes 196608 | tf_op jit(solution)/shard_map/while/body/eval_jaxpr/psum | solution.py:16
  574.1 90.5 %all-reduce.5.cloned.1.call-start = ((), (), s32[]{:S(2)}) async-start(), calls=%async_computation.1 | async-start | bytes 196608 | tf_op jit(solution)/shard_map/while/body/eval_jaxpr/psum | solution.py:16
  666.5 90.5 %all-reduce.5.cloned.1.call-start = ((), (), s32[]{:S(2)}) async-start(), calls=%async_computation.1 | async-start | bytes 196608 | tf_op jit(solution)/shard_map/while/body/eval_jaxpr/psum | solution.py:16
  758.9 90.5 %all-reduce.5.cloned.1.call-start = ((), (), s32[]{:S(2)}) async-start(), calls=%async_computation.1 | async-start | bytes 196608 | tf_op jit(solution)/shard_map/while/body/eval_jaxpr/psum | solution.py:16
  851.3 90.2 %all-reduce.5.cloned.1.call-start = ((), (), s32[]{:S(2)}) async-start(), calls=%async_computation.1 | async-start | bytes 196608 | tf_op jit(solution)/shard_map/while/body/eval_jaxpr/psum | solution.py:16
  943.4 90.5 %all-reduce.5.cloned.1.call-start = ((), (), s32[]{:S(2)}) async-start(), calls=%async_computation.1 | async-start | bytes 196608 | tf_op jit(solution)/shard_map/while/body/eval_jaxpr/psum | solution.py:16
  1035.8 90.2 %all-reduce.5.cloned.1.call-start = ((), (), s32[]{:S(2)}) async-start(), calls=%async_computation.1 | async-start | bytes 196608 | tf_op jit(solution)/shard_map/while/body/eval_jaxpr/psum | solution.py:16
  1127.9 90.5 %all-reduce.5.cloned.1.call-start = ((), (), s32[]{:S(2)}) async-start(), calls=%async_computation.1 | async-start | bytes 196608 | tf_op jit(solution)/shard_map/while/body/eval_jaxpr/psum | solution.py:16
  1220.3 90.2 %all-reduce.5.cloned.1.call-start = ((), (), s32[]{:S(2)}) async-start(), calls=%async_computation.1 | async-start | bytes 196608 | tf_op jit(solution)/shard_map/while/body/eval_jaxpr/psum | solution.py:16
  1312.4 90.2 %all-reduce.5.cloned.1.call-start = ((), (), s32[]{:S(2)}) async-start(), calls=%async_computation.1 | async-start | bytes 196608 | tf_op jit(solution)/shard_map/while/body/eval_jaxpr/psum | solution.py:16
  1404.5 90.2 %all-reduce.5.cloned.1.call-start = ((), (), s32[]{:S(2)}) async-start(), calls=%async_computation.1 | async-start | bytes 196608 | tf_op jit(solution)/shard_map/while/body/eval_jaxpr/psum | solution.py:16
  1496.6 90.2 %all-reduce.5.cloned.1.call-start = ((), (), s32[]{:S(2)}) async-start(), calls=%async_computation.1 | async-start | bytes 196608 | tf_op jit(solution)/shard_map/while/body/eval_jaxpr/psum | solution.py:16
Sparse Core Ops, SparseCore 0:
  10.8 92.4 all-reduce.2
  117.2 86.1 all-reduce.4
  209.6 86.1 all-reduce.4
  301.7 86.1 all-reduce.4
  393.8 86.1 all-reduce.4
  485.9 86.1 all-reduce.4
  578.3 86.1 all-reduce.4
  670.7 86.1 all-reduce.4
  763.2 86.1 all-reduce.4
  855.2 86.1 all-reduce.4
  947.7 86.1 all-reduce.4
  1039.7 86.1 all-reduce.4
  1132.2 86.1 all-reduce.4
  1224.3 86.1 all-reduce.4
  1316.4 86.1 all-reduce.4
  1408.5 86.1 all-reduce.4
  1500.5 86.1 all-reduce.4
where the time goes:
time: 1600 us
  waiting for transfers between devices  1470 us (92%)
  other arithmetic  104 us (6%)
    psum x16, waiting for transfers between devices, broadcast(): return lax.psum(kept, axis)  1430 us
    another operation x2, other arithmetic  55.8 us
    psum x1, waiting for transfers between devices, shards(): channel_total = lax.psum(local_total, 'chan')  36.9 us
  transfers between devices with their start and end apart: 17, of which 17 were waited for; matrix products, arithmetic and copies ran while one was open for 4% of the time, Pallas kernels for 0%

commit v1 on v0

v1 whole, which is shorter than its diff:
```python
import functools
import math

import jax
import jax.numpy as jnp
import ml_dtypes
import numpy as np
from jax import lax
from jax.experimental import pallas as pl
from jax.experimental.pallas import tpu as pltpu
from jax.sharding import PartitionSpec as P

NFFT = 12000
LAGW = 1024
SMOOTH = 64
LANES = 128
SPLIT = 4
LAGS = LAGW // SPLIT
VMEM = pl.BlockSpec(memory_space=pltpu.VMEM)
SMEM = pl.BlockSpec(memory_space=pltpu.SMEM)
f32 = jnp.float32
bf16 = jnp.bfloat16


def lag_tables(bins):
    k = np.arange(1, bins + 1, dtype=np.int64)
    angle = 2.0 * np.pi / NFFT * np.mod(k[:, None] * np.arange(LAGS)[None, :], NFFT)
    both = np.stack([np.cos(angle), -np.sin(angle)]).reshape(2, bins // LANES, LANES, LAGS)
    table = both.transpose(1, 0, 2, 3).reshape(2 * bins, LAGS).astype(ml_dtypes.bfloat16)
    turn = 2.0 * np.pi / NFFT * np.mod(k[None, :] * (LAGS * np.arange(SPLIT))[:, None], NFFT)
    return table, np.stack([np.cos(turn), np.sin(turn)]).astype(np.float32)


def orders(owners):
    bits = [1 << i for i in range(owners.bit_length() - 1)]
    far = bits[:0:-1]
    other = far[:-2] + far[-2:][::-1]
    return bits[1:], far + [1], other + [1]


def masks(order):
    out = [0]
    for bit in order:
        out = out + [m ^ bit for m in out]
    return out


def swap(value, bit):
    owners = lax.axis_size("chan")
    return lax.ppermute(value, "chan", [(i, i ^ bit) for i in range(owners)])


def prepare(bins, info, spectra, own, other, first, second):
    core, pick, lag = info[0], info[1], info[2]
    half = bins // 2
    keep = (1 - info[3 + pick]).astype(f32)
    for h, dest in ((0, first), (1, second)):
        for part in range(2):
            src = pl.ds(part * bins + h * half, half)
            total = spectra[0, :, src].astype(f32)
            for r in range(1, spectra.shape[0]):
                total = total + spectra[r, :, src].astype(f32)
            cols = pl.ds(part * half, half)

            @pl.when(core == h)
            def _():
                own[:, cols] = total

            @pl.when(core != h)
            def _():
                other[:, cols] = total

            dest[:, cols] = spectra[pick, :, src]
    row = lax.broadcasted_iota(jnp.int32, (8, LANES), 0)
    high = lax.shift_right_arithmetic(lag, 5)
    low = lag - high * 32
    extra = jnp.where(
        row == 0, high.astype(f32), jnp.where(row == 1, low.astype(f32), keep)
    )
    first[:, pl.ds(bins, LANES)] = extra.astype(bf16)


def cos_sin(turns):
    whole = jnp.floor(turns * (1.0 / NFFT) + 0.5)
    rest = turns - whole * NFFT
    quarter = jnp.floor(rest * (4.0 / NFFT) + 0.5)
    phi = (rest - quarter * (NFFT / 4)) * (2.0 * math.pi / NFFT)
    sq = phi * phi
    s = phi * (1.0 + sq * (-1 / 6 + sq * (1 / 120 + sq * (-1 / 5040))))
    c = 1.0 + sq * (-0.5 + sq * (1 / 24 + sq * (-1 / 720 + sq * (1 / 40320))))
    swapped = jnp.abs(quarter) == 1.0
    cos_neg = (quarter == 1.0) | (jnp.abs(quarter) == 2.0)
    sin_neg = (quarter == -1.0) | (jnp.abs(quarter) == 2.0)
    cosine = jnp.where(swapped, s, c)
    sine = jnp.where(swapped, c, s)
    return jnp.where(cos_neg, -cosine, cosine), jnp.where(sin_neg, -sine, sine)


def correlate(
    bins, order_a, order_b, channels, info, spectra, keep, own, other, got_a, got_b, table, turn,
    out, rec, src, ang, cross,
):
    core, me = info[0], info[11]
    receivers, windows = spectra.shape[0], spectra.shape[1]
    sources = got_a.shape[0]
    half = bins // 2
    chunks = half // LANES
    norm = 1.0 / math.sqrt(windows * bins)
    rows = receivers * windows + sources * windows
    block_i = lax.broadcasted_iota(jnp.int32, (LANES, LANES), 0) // SMOOTH
    block_j = lax.broadcasted_iota(jnp.int32, (LANES, LANES), 1) // SMOOTH
    same = jnp.where(block_i == block_j, 1.0, 0.0).astype(bf16)
    masks_a, masks_b = masks(order_a), masks(order_b)
    place_b = [masks_a.index(m) for m in masks_b]
    lane = lax.broadcasted_iota(jnp.int32, (1, LANES), 1)
    inv = 1.0 / channels

    def whiten(re, im, keeps):
        count = re.shape[0]
        power = (re * re + im * im).reshape(count * windows, LANES)
        high = power.astype(bf16)
        low = (power - high.astype(f32)).astype(bf16)
        level = jnp.dot(high, same, preferred_element_type=f32) + jnp.dot(
            low, same, preferred_element_type=f32
        )
        scale = lax.rsqrt(level * (1.0 / SMOOTH) + 1e-6).reshape(count, windows, LANES) * keeps
        return (re * scale).astype(bf16).astype(f32), (im * scale).astype(bf16).astype(f32)

    tail = got_a[:, :, pl.ds(bins, LANES)].astype(f32)
    lags = tail[:, 0:1, :] * 32.0 + tail[:, 1:2, :]
    keep_src = jnp.broadcast_to(tail[:, 2:3, :], (sources, windows, LANES))

    for h, got, where in ((0, got_a, list(range(sources))), (1, got_b, place_b)):
        if h == 0:
            lag_rows, keep_rows = lags, keep_src
        else:
            lag_rows = jnp.concatenate([lags[p : p + 1] for p in where], 0)
            keep_rows = jnp.concatenate([keep_src[p : p + 1] for p in where], 0)

        def chunk(c, _):
            off = pl.multiple_of(c * LANES, LANES)
            re_at = pl.ds(off, LANES)
            im_at = pl.ds(pl.multiple_of(half + c * LANES, LANES), LANES)
            mean = []
            for at in (re_at, im_at):
                mean.append(
                    jnp.where(core == h, own[:, at], other[:, at]) * inv
                )
            x_re = spectra[:, :, pl.ds(pl.multiple_of(h * half + c * LANES, LANES), LANES)]
            x_im = spectra[:, :, pl.ds(pl.multiple_of(bins + h * half + c * LANES, LANES), LANES)]
            r_re, r_im = whiten(
                x_re.astype(f32) - mean[0][None], x_im.astype(f32) - mean[1][None], keep[...]
            )
            rec[0] = r_re
            rec[1] = r_im
            s_re, s_im = whiten(
                got[:, :, re_at].astype(f32) - mean[0][None],
                got[:, :, im_at].astype(f32) - mean[1][None],
                keep_rows,
            )
            k = (lane + (h * half + 1) + c * LANES).astype(f32)
            cosine, sine = cos_sin(lag_rows * k[None])
            src[0] = (s_re * cosine + s_im * sine).astype(bf16).astype(f32)
            src[1] = (s_im * cosine - s_re * sine).astype(bf16).astype(f32)
            a = [rec[0, :, w, :] for w in range(windows)]
            b = [rec[1, :, w, :] for w in range(windows)]
            turns = [
                (turn[0, q : q + 1, pl.ds(pl.multiple_of(h * half + c * LANES, LANES), LANES)],
                 turn[1, q : q + 1, pl.ds(pl.multiple_of(h * half + c * LANES, LANES), LANES)])
                for q in range(SPLIT)
            ]
            col = pl.multiple_of(c * 2 * LANES, LANES)
            for p in range(0, sources, 2):
                pair = []
                for i in (p, p + 1):
                    c_re = c_im = None
                    for w in range(windows):
                        g = jnp.broadcast_to(src[0, i, w : w + 1, :], (receivers, LANES))
                        e = jnp.broadcast_to(src[1, i, w : w + 1, :], (receivers, LANES))
                        t_re = g * a[w] + e * b[w]
                        t_im = g * b[w] - e * a[w]
                        c_re = t_re if c_re is None else c_re + t_re
                        c_im = t_im if c_im is None else c_im + t_im
                    pair.append((c_re * norm, c_im * norm))
                for q in range(SPLIT):
                    done = []
                    for c_re, c_im in pair:
                        if q == 0:
                            done.append((c_re, c_im))
                        else:
                            ct, st = turns[q]
                            done.append((c_re * ct - c_im * st, c_re * st + c_im * ct))
                    for part in range(2):
                        for j, i in enumerate((p, p + 1)):
                            at = q * sources * receivers + where[i] * receivers
                            cross[at : at + receivers, pl.ds(pl.multiple_of(col + part * LANES, LANES), LANES)] = done[j][part]
            return 0

        lax.fori_loop(0, chunks, chunk, 0)
        for q in range(SPLIT):
            span = sources * receivers
            part = jnp.dot(
                cross[q * span : (q + 1) * span, :].astype(bf16),
                table[h * bins : (h + 1) * bins, :],
                preferred_element_type=f32,
            )
            for p in range(sources):
                source = jnp.bitwise_xor(me, masks_a[p])
                rows_p = part[p * receivers : (p + 1) * receivers, :]
                cols = pl.ds(q * LAGS, LAGS)
                if h == 0:
                    out[source, :, cols] = rows_p
                else:
                    out[source, :, cols] = out[source, :, cols] + rows_p


def shards(spectra, bad_flag, source_pick, lag_start):
    receivers, windows, width_both = spectra.shape
    bins = width_both // 2
    owners = lax.axis_size("chan")
    half = bins // 2
    me = lax.axis_index("chan").astype(jnp.int32)
    info = jnp.concatenate(
        [jnp.stack([me & 1, source_pick[0], lag_start[0]]), bad_flag, me[None]]
    )
    keep = jnp.broadcast_to(
        (1 - bad_flag).astype(f32)[:, None, None], (receivers, windows, LANES)
    )
    own, other, first, second = pl.pallas_call(
        functools.partial(prepare, bins),
        out_shape=(
            jax.ShapeDtypeStruct((windows, bins), f32),
            jax.ShapeDtypeStruct((windows, bins), f32),
            jax.ShapeDtypeStruct((windows, bins + LANES), bf16),
            jax.ShapeDtypeStruct((windows, bins), bf16),
        ),
        in_specs=[SMEM, VMEM],
        out_specs=(VMEM,) * 4,
        compiler_params=pltpu.CompilerParams(vmem_limit_bytes=16 << 20),
        name="prepare",
    )(info, spectra)
    near, order_a, order_b = orders(owners)
    total = own + swap(other, 1)
    got_a, got_b = first[None], second[None]
    for i in range(len(order_a)):
        got_a = jnp.concatenate([got_a, swap(got_a, order_a[i])], 0)
        got_b = jnp.concatenate([got_b, swap(got_b, order_b[i])], 0)
    for bit in near:
        total = total + swap(total, bit)
    rest = swap(total, 1)
    table, turn = lag_tables(bins)
    sources = owners
    return pl.pallas_call(
        functools.partial(correlate, bins, order_a, order_b, receivers * owners),
        out_shape=jax.ShapeDtypeStruct((sources, receivers, LAGW), f32),
        in_specs=[SMEM] + [VMEM] * 8,
        out_specs=VMEM,
        scratch_shapes=[
            pltpu.VMEM((2, receivers, windows, LANES), f32),
            pltpu.VMEM((2, sources, windows, LANES), f32),
            pltpu.VMEM((8, LANES), f32),
            pltpu.VMEM((SPLIT * sources * receivers, bins), f32),
        ],
        compiler_params=pltpu.CompilerParams(vmem_limit_bytes=56 << 20),
        name="correlate",
    )(info, spectra, keep, total, rest, got_a, got_b, jnp.asarray(table), jnp.asarray(turn))


def solution(mesh):
    in_specs = (
        P(("groups", "chan"), None, None),
        P(("groups", "chan")),
        P(("groups", "chan")),
        P(("groups", "chan")),
    )
    out_specs = P(None, ("groups", "chan"), None)
    return jax.shard_map(shards, mesh=mesh, in_specs=in_specs, out_specs=out_specs, check_vma=False)
```

time: 1600 us -> 54.2 us (0.03)
  waiting for transfers between devices: 1470 us -> 16.7 us
  other arithmetic: 104 us -> 0.89 us
  Pallas kernels: 0 us -> 18.8 us
    psum x17 -> x0, waiting for transfers between devices: 1470 us -> none  [the longest x16 1430 us: broadcast(): return lax.psum(kept, axis)]
    another operation x2 -> x0, other arithmetic: 55.8 us -> none
    pallas_call x0 -> x2, Pallas kernels: none -> 18.8 us  [the longest x1 18.1 us: shards(): pl.pallas_call(functools.partial(correlate, bins, order_a, order_b, recei...]
    ppermute x0 -> x13, waiting for transfers between devices: none -> 16.7 us  [swap(): return lax.ppermute(value, 'chan', [(i, i ^ bit) for i in range(owners)])]
  transfers between devices with their start and end apart: 17 -> 13, of which waited for: 17 -> 6; matrix products, arithmetic and copies ran while one was open for 4% -> 2% of each run, Pallas kernels for 0% -> 0%
where the time goes in v1:
time: 54.2 us; the launch traced here: 54 us
  Pallas kernels  18.8 us (35%)
  waiting for transfers between devices  16.7 us (31%)
  starting transfers between devices  13.5 us (25%)
  local copies, waits for them, and re-layouts  2.72 us (5%)
  between operations  1.47 us (3%)
  other arithmetic  0.89 us (2%)
    pallas_call x1, Pallas kernels, shards(): pl.pallas_call(functools.partial(correlate, bins, order_a, order_b, recei...  18.1 us
    ppermute x13, waiting for transfers between devices, swap(): return lax.ppermute(value, 'chan', [(i, i ^ bit) for i in range(owners)])  16.7 us
    ppermute x13, starting transfers between devices, swap(): return lax.ppermute(value, 'chan', [(i, i ^ bit) for i in range(owners)])  13.5 us
    unnamed x20, local copies, waits for them, and re-layouts  1.24 us
  transfers between devices with their start and end apart: 13, of which 6 were waited for; matrix products, arithmetic and copies ran while one was open for 2% of the time, Pallas kernels for 0%

profile of v1, /device:TPU:0, one launch (start us, length us, event | category | flops | bytes accessed | tf_op | source)
XLA Modules:
  0.0 54.0 jit_solution(13595619982073627375)
XLA Ops:
  1.3 0.7 %concatenate.33.info = s32[12]{0:T(128)S(1)} concatenate(s32[1]{0:T(128)} %bitcast, s32[1]{0:T(128)S(6)} %copy.15, s32[1]{0:T(128)S(6)} %copy.16, s32[8]{0:T(128)} %param.7, s32[1]{0:T(128)} %bitcast.1), dimensions={0} | concatenate | bytes 96 | tf_op jit(solution)/shard_map/concatenate | solution.py:223
  2.0 0.0 copy-start
  2.0 1.1 %copy-done = bf16[8,8,6144]{2,1,0:T(8,128)(2,1)S(1)} copy-done((bf16[8,8,6144]{2,1,0:T(8,128)(2,1)S(1)}, bf16[8,8,6144]{2,1,0:T(8,128)(2,1)}, u32[]{:S(2)}) %copy-start) | copy-done | bytes 786456
  3.2 0.0 copy-start.1
  3.2 0.7 %prepare.1 = (f32[8,3072]{1,0:T(8,128)S(1)}, f32[8,3072]{1,0:T(8,128)S(1)}, bf16[8,3200]{1,0:T(8,128)(2,1)S(1)}, bf16[8,3072]{1,0:T(8,128)(2,1)S(1)}) custom-call(s32[12]{0:T(128)S(1)} %concatenate.33.info, bf16[8,8,6144]{2,1,0:T(8,128)(2,1)S(1)} %copy-done), custom_call_target="tpu_custom_call" | custom-call | tf_op jit(solution)/shard_map/prepare/pallas_call | solution.py:229
  3.8 0.5 collective-permute-start
  4.4 3.7 %collective-permute-start.5 = (bf16[1,8,3200]{2,1,0:T(8,128)(2,1)S(1)}, bf16[1,8,3200]{2,1,0:T(8,128)(2,1)S(1)}, u32[]{:S(2)}, u32[]{:S(2)}) collective-permute-start(bf16[1,8,3200]{2,1,0:T(8,128)(2,1)S(1)} %bitcast.6), channel_id=1, source_target_pairs={{0,8},{1,9},{2,10},{3,11},{4,12},{5,13},{6,14},{7,15},{8,0},{9,1},... | collective-permute-start | bytes 153608 | tf_op jit(solution)/shard_map/ppermute | solution.py:50
  8.0 0.1 collective-permute-start.9
  8.1 0.7 %subtract_convert_fusion = f32[8]{0:T(128)S(1)} fusion(s32[8]{0:T(128)} %param.7), kind=kLoop, calls=%fused_computation.16 | loop fusion | flops 16 | bytes 64 | tf_op jit(solution)/shard_map/convert_element_type | solution.py:227
  8.8 5.3 %collective-permute-done.9 = bf16[1,8,3072]{2,1,0:T(8,128)(2,1)S(1)} collective-permute-done((bf16[1,8,3072]{2,1,0:T(8,128)(2,1)S(1)}, bf16[1,8,3072]{2,1,0:T(8,128)(2,1)S(1)}, u32[]{:S(2)}, u32[]{:S(2)}) %collective-permute-start.9) | collective-permute-done | bytes 49184 | tf_op jit(solution)/shard_map/ppermute | solution.py:50
  14.1 1.6 %collective-permute-start.10 = (bf16[2,8,3072]{2,1,0:T(8,128)(2,1)S(1)}, bf16[2,8,3072]{2,1,0:T(8,128)(2,1)S(1)}, u32[]{:S(2)}, u32[]{:S(2)}) collective-permute-start(bf16[2,8,3072]{2,1,0:T(8,128)(2,1)S(1)} %pad_maximum_fusion.5), channel_id=1, source_target_pairs={{0,2},{1,3},{2,0},{3,1},{4,6},{5,7},{6,4},{7,5},{8,10},{9,11},{10,... | collective-permute-start | bytes 294920 | tf_op jit(solution)/shard_map/ppermute | solution.py:50
  15.7 0.0 collective-permute-done.5
  15.7 0.6 %collective-permute-start.6 = (bf16[2,8,3200]{2,1,0:T(8,128)(2,1)S(1)}, bf16[2,8,3200]{2,1,0:T(8,128)(2,1)S(1)}, u32[]{:S(2)}, u32[]{:S(2)}) collective-permute-start(bf16[2,8,3200]{2,1,0:T(8,128)(2,1)S(1)} %pad_maximum_fusion.4), channel_id=1, source_target_pairs={{0,4},{1,5},{2,6},{3,7},{4,0},{5,1},{6,2},{7,3},{8,12},{9,13},{10,... | collective-permute-start | bytes 307208 | tf_op jit(solution)/shard_map/ppermute | solution.py:50
  16.3 0.0 collective-permute-done
  16.3 0.6 %collective-permute-start.1 = (f32[8,3072]{1,0:T(8,128)S(1)}, f32[8,3072]{1,0:T(8,128)S(1)}, u32[]{:S(2)}, u32[]{:S(2)}) collective-permute-start(f32[8,3072]{1,0:T(8,128)S(1)} %add.12), channel_id=1, source_target_pairs={{0,2},{1,3},{2,0},{3,1},{4,6},{5,7},{6,4},{7,5},{8,10},{9,11},{10,... | collective-permute-start | bytes 294920 | tf_op jit(solution)/shard_map/ppermute | solution.py:50
  16.9 2.5 %collective-permute-done.10 = bf16[2,8,3072]{2,1,0:T(8,128)(2,1)S(1)} collective-permute-done((bf16[2,8,3072]{2,1,0:T(8,128)(2,1)S(1)}, bf16[2,8,3072]{2,1,0:T(8,128)(2,1)S(1)}, u32[]{:S(2)}, u32[]{:S(2)}) %collective-permute-start.10) | collective-permute-done | bytes 98336 | tf_op jit(solution)/shard_map/ppermute | solution.py:50
  19.4 0.7 %collective-permute-start.11 = (bf16[4,8,3072]{2,1,0:T(8,128)(2,1)S(1)}, bf16[4,8,3072]{2,1,0:T(8,128)(2,1)S(1)}, u32[]{:S(2)}, u32[]{:S(2)}) collective-permute-start(bf16[4,8,3072]{2,1,0:T(8,128)(2,1)S(1)} %pad_maximum_fusion.3), channel_id=1, source_target_pairs={{0,4},{1,5},{2,6},{3,7},{4,0},{5,1},{6,2},{7,3},{8,12},{9,13},{10,... | collective-permute-start | bytes 589832 | tf_op jit(solution)/shard_map/ppermute | solution.py:50
  20.1 1.3 %collective-permute-done.6 = bf16[2,8,3200]{2,1,0:T(8,128)(2,1)S(1)} collective-permute-done((bf16[2,8,3200]{2,1,0:T(8,128)(2,1)S(1)}, bf16[2,8,3200]{2,1,0:T(8,128)(2,1)S(1)}, u32[]{:S(2)}, u32[]{:S(2)}) %collective-permute-start.6) | collective-permute-done | bytes 102432 | tf_op jit(solution)/shard_map/ppermute | solution.py:50
  21.5 0.5 collective-permute-start.7
  22.0 0.0 collective-permute-done.1
  22.0 1.2 %collective-permute-start.2 = (f32[8,3072]{1,0:T(8,128)S(1)}, f32[8,3072]{1,0:T(8,128)S(1)}, u32[]{:S(2)}, u32[]{:S(2)}) collective-permute-start(f32[8,3072]{1,0:T(8,128)S(1)} %add.13), channel_id=1, source_target_pairs={{0,4},{1,5},{2,6},{3,7},{4,0},{5,1},{6,2},{7,3},{8,12},{9,13},{10,... | collective-permute-start | bytes 294920 | tf_op jit(solution)/shard_map/ppermute | solution.py:50
  23.2 3.6 %collective-permute-done.2 = f32[8,3072]{1,0:T(8,128)S(1)} collective-permute-done((f32[8,3072]{1,0:T(8,128)S(1)}, f32[8,3072]{1,0:T(8,128)S(1)}, u32[]{:S(2)}, u32[]{:S(2)}) %collective-permute-start.2) | collective-permute-done | bytes 98336 | tf_op jit(solution)/shard_map/ppermute | solution.py:50
  26.8 3.3 %collective-permute-start.3 = (f32[8,3072]{1,0:T(8,128)S(1)}, f32[8,3072]{1,0:T(8,128)S(1)}, u32[]{:S(2)}, u32[]{:S(2)}) collective-permute-start(f32[8,3072]{1,0:T(8,128)S(1)} %add.14), channel_id=1, source_target_pairs={{0,8},{1,9},{2,10},{3,11},{4,12},{5,13},{6,14},{7,15},{8,0},{9,1},... | collective-permute-start | bytes 294920 | tf_op jit(solution)/shard_map/ppermute | solution.py:50
  30.2 0.0 collective-permute-done.11
  30.2 0.1 collective-permute-start.12
  30.3 0.0 collective-permute-done.7
  30.3 0.1 pad_maximum_fusion
  30.4 0.6 %collective-permute-start.8 = (bf16[8,8,3200]{2,1,0:T(8,128)(2,1)S(1)}, bf16[8,8,3200]{2,1,0:T(8,128)(2,1)S(1)}, u32[]{:S(2)}, u32[]{:S(2)}) collective-permute-start(bf16[8,8,3200]{2,1,0:T(8,128)(2,1)S(1)} %pad_maximum_fusion), channel_id=1, source_target_pairs={{0,1},{1,0},{2,3},{3,2},{4,5},{5,4},{6,7},{7,6},{8,9},{9,8},{10,11... | collective-permute-start | bytes 1228808 | tf_op jit(solution)/shard_map/ppermute | solution.py:50
  31.0 2.8 %collective-permute-done.3 = f32[8,3072]{1,0:T(8,128)S(1)} collective-permute-done((f32[8,3072]{1,0:T(8,128)S(1)}, f32[8,3072]{1,0:T(8,128)S(1)}, u32[]{:S(2)}, u32[]{:S(2)}) %collective-permute-start.3) | collective-permute-done | bytes 98336 | tf_op jit(solution)/shard_map/ppermute | solution.py:50
  33.8 0.0 copy-done.1
  33.8 0.0 copy-start.4
  33.8 0.1 collective-permute-start.4
  33.9 0.0 collective-permute-done.12
  34.0 0.0 copy-start.3
  34.0 0.0 collective-permute-done.8
  34.0 0.0 copy-start.2
  34.0 1.2 %collective-permute-done.4.other = f32[8,3072]{1,0:T(8,128)S(1)} collective-permute-done((f32[8,3072]{1,0:T(8,128)S(1)}, f32[8,3072]{1,0:T(8,128)S(1)}, u32[]{:S(2)}, u32[]{:S(2)}) %collective-permute-start.4) | collective-permute-done | bytes 98336 | tf_op jit(solution)/shard_map/ppermute | solution.py:50
  35.2 0.0 copy-start.5
  35.2 0.7 %broadcast_in_dim.16.keep = f32[8,8,128]{2,1,0:T(8,128)} broadcast(f32[8]{0:T(128)S(1)} %subtract_convert_fusion), dimensions={0} | broadcast | bytes 32800 | tf_op jit(solution)/shard_map/broadcast_in_dim | solution.py:226
  35.9 0.0 copy-done.4
  35.9 0.0 copy-done.3
  35.9 0.0 copy-done.2
  35.9 0.0 copy-done.5
  35.9 18.1 %correlate.1 = f32[16,8,1024]{2,1,0:T(8,128)} custom-call(s32[12]{0:T(128)} %copy-done.1, bf16[8,8,6144]{2,1,0:T(8,128)(2,1)} %spectra.3, f32[8,8,128]{2,1,0:T(8,128)} %broadcast_in_dim.16.keep, f32[8,3072]{1,0:T(8,128)} %copy-done.4, f32[8,3072]{1,0:T(8,128)} %copy-done.5, bf16[16,8,3200]{2,1,0:T(8,128)(2,1)} %copy-done.2, bf16[16,8,3072]{2,1,0:T(8,128)(2,1)} %copy-done.3, ...), custom_call_target="tpu_custom_call" | custom-call | tf_op jit(solution)/shard_map/correlate/pallas_call | solution.py:253
  (19 shorter events, 0.3 us)
Async XLA Ops:
  2.0 1.1 %copy-start = (bf16[8,8,6144]{2,1,0:T(8,128)(2,1)S(1)}, bf16[8,8,6144]{2,1,0:T(8,128)(2,1)}, u32[]{:S(2)}) copy-start(bf16[8,8,6144]{2,1,0:T(8,128)(2,1)} %spectra.3) | copy-start | bytes 2359300
  3.2 30.7 %copy-start.1 = (s32[12]{0:T(128)}, s32[12]{0:T(128)S(1)}, u32[]{:S(2)}) copy-start(s32[12]{0:T(128)S(1)} %concatenate.33.info) | copy-start | bytes 148
  3.8 12.5 %collective-permute-start = (f32[8,3072]{1,0:T(8,128)S(1)}, f32[8,3072]{1,0:T(8,128)S(1)}, u32[]{:S(2)}, u32[]{:S(2)}) collective-permute-start(f32[8,3072]{1,0:T(8,128)S(1)} %get-tuple-element.10), channel_id=1, source_target_pairs={{0,1},{1,0},{2,3},{3,2},{4,5},{5,4},{6,7},{7,6},{8,9},{9,8},{10,11... | collective-permute-start | bytes 294920 | tf_op jit(solution)/shard_map/ppermute | solution.py:50
  4.4 11.3 %collective-permute-start.5 = (bf16[1,8,3200]{2,1,0:T(8,128)(2,1)S(1)}, bf16[1,8,3200]{2,1,0:T(8,128)(2,1)S(1)}, u32[]{:S(2)}, u32[]{:S(2)}) collective-permute-start(bf16[1,8,3200]{2,1,0:T(8,128)(2,1)S(1)} %bitcast.6), channel_id=1, source_target_pairs={{0,8},{1,9},{2,10},{3,11},{4,12},{5,13},{6,14},{7,15},{8,0},{9,1},... | collective-permute-start | bytes 153608 | tf_op jit(solution)/shard_map/ppermute | solution.py:50
  8.0 6.0 %collective-permute-start.9 = (bf16[1,8,3072]{2,1,0:T(8,128)(2,1)S(1)}, bf16[1,8,3072]{2,1,0:T(8,128)(2,1)S(1)}, u32[]{:S(2)}, u32[]{:S(2)}) collective-permute-start(bf16[1,8,3072]{2,1,0:T(8,128)(2,1)S(1)} %bitcast.10), channel_id=1, source_target_pairs={{0,8},{1,9},{2,10},{3,11},{4,12},{5,13},{6,14},{7,15},{8,0},{9,1},... | collective-permute-start | bytes 147464 | tf_op jit(solution)/shard_map/ppermute | solution.py:50
  14.1 5.3 %collective-permute-start.10 = (bf16[2,8,3072]{2,1,0:T(8,128)(2,1)S(1)}, bf16[2,8,3072]{2,1,0:T(8,128)(2,1)S(1)}, u32[]{:S(2)}, u32[]{:S(2)}) collective-permute-start(bf16[2,8,3072]{2,1,0:T(8,128)(2,1)S(1)} %pad_maximum_fusion.5), channel_id=1, source_target_pairs={{0,2},{1,3},{2,0},{3,1},{4,6},{5,7},{6,4},{7,5},{8,10},{9,11},{10,... | collective-permute-start | bytes 294920 | tf_op jit(solution)/shard_map/ppermute | solution.py:50
  15.7 5.7 %collective-permute-start.6 = (bf16[2,8,3200]{2,1,0:T(8,128)(2,1)S(1)}, bf16[2,8,3200]{2,1,0:T(8,128)(2,1)S(1)}, u32[]{:S(2)}, u32[]{:S(2)}) collective-permute-start(bf16[2,8,3200]{2,1,0:T(8,128)(2,1)S(1)} %pad_maximum_fusion.4), channel_id=1, source_target_pairs={{0,4},{1,5},{2,6},{3,7},{4,0},{5,1},{6,2},{7,3},{8,12},{9,13},{10,... | collective-permute-start | bytes 307208 | tf_op jit(solution)/shard_map/ppermute | solution.py:50
  16.3 5.7 %collective-permute-start.1 = (f32[8,3072]{1,0:T(8,128)S(1)}, f32[8,3072]{1,0:T(8,128)S(1)}, u32[]{:S(2)}, u32[]{:S(2)}) collective-permute-start(f32[8,3072]{1,0:T(8,128)S(1)} %add.12), channel_id=1, source_target_pairs={{0,2},{1,3},{2,0},{3,1},{4,6},{5,7},{6,4},{7,5},{8,10},{9,11},{10,... | collective-permute-start | bytes 294920 | tf_op jit(solution)/shard_map/ppermute | solution.py:50
  19.4 10.8 %collective-permute-start.11 = (bf16[4,8,3072]{2,1,0:T(8,128)(2,1)S(1)}, bf16[4,8,3072]{2,1,0:T(8,128)(2,1)S(1)}, u32[]{:S(2)}, u32[]{:S(2)}) collective-permute-start(bf16[4,8,3072]{2,1,0:T(8,128)(2,1)S(1)} %pad_maximum_fusion.3), channel_id=1, source_target_pairs={{0,4},{1,5},{2,6},{3,7},{4,0},{5,1},{6,2},{7,3},{8,12},{9,13},{10,... | collective-permute-start | bytes 589832 | tf_op jit(solution)/shard_map/ppermute | solution.py:50
  21.5 8.8 %collective-permute-start.7 = (bf16[4,8,3200]{2,1,0:T(8,128)(2,1)S(1)}, bf16[4,8,3200]{2,1,0:T(8,128)(2,1)S(1)}, u32[]{:S(2)}, u32[]{:S(2)}) collective-permute-start(bf16[4,8,3200]{2,1,0:T(8,128)(2,1)S(1)} %pad_maximum_fusion.2), channel_id=1, source_target_pairs={{0,2},{1,3},{2,0},{3,1},{4,6},{5,7},{6,4},{7,5},{8,10},{9,11},{10,... | collective-permute-start | bytes 614408 | tf_op jit(solution)/shard_map/ppermute | solution.py:50
  22.0 4.8 %collective-permute-start.2 = (f32[8,3072]{1,0:T(8,128)S(1)}, f32[8,3072]{1,0:T(8,128)S(1)}, u32[]{:S(2)}, u32[]{:S(2)}) collective-permute-start(f32[8,3072]{1,0:T(8,128)S(1)} %add.13), channel_id=1, source_target_pairs={{0,4},{1,5},{2,6},{3,7},{4,0},{5,1},{6,2},{7,3},{8,12},{9,13},{10,... | collective-permute-start | bytes 294920 | tf_op jit(solution)/shard_map/ppermute | solution.py:50
  26.8 7.0 %collective-permute-start.3 = (f32[8,3072]{1,0:T(8,128)S(1)}, f32[8,3072]{1,0:T(8,128)S(1)}, u32[]{:S(2)}, u32[]{:S(2)}) collective-permute-start(f32[8,3072]{1,0:T(8,128)S(1)} %add.14), channel_id=1, source_target_pairs={{0,8},{1,9},{2,10},{3,11},{4,12},{5,13},{6,14},{7,15},{8,0},{9,1},... | collective-permute-start | bytes 294920 | tf_op jit(solution)/shard_map/ppermute | solution.py:50
  30.2 3.7 %collective-permute-start.12 = (bf16[8,8,3072]{2,1,0:T(8,128)(2,1)S(1)}, bf16[8,8,3072]{2,1,0:T(8,128)(2,1)S(1)}, u32[]{:S(2)}, u32[]{:S(2)}) collective-permute-start(bf16[8,8,3072]{2,1,0:T(8,128)(2,1)S(1)} %pad_maximum_fusion.1), channel_id=1, source_target_pairs={{0,1},{1,0},{2,3},{3,2},{4,5},{5,4},{6,7},{7,6},{8,9},{9,8},{10,11... | collective-permute-start | bytes 1179656 | tf_op jit(solution)/shard_map/ppermute | solution.py:50
  30.4 3.6 %collective-permute-start.8 = (bf16[8,8,3200]{2,1,0:T(8,128)(2,1)S(1)}, bf16[8,8,3200]{2,1,0:T(8,128)(2,1)S(1)}, u32[]{:S(2)}, u32[]{:S(2)}) collective-permute-start(bf16[8,8,3200]{2,1,0:T(8,128)(2,1)S(1)} %pad_maximum_fusion), channel_id=1, source_target_pairs={{0,1},{1,0},{2,3},{3,2},{4,5},{5,4},{6,7},{7,6},{8,9},{9,8},{10,11... | collective-permute-start | bytes 1228808 | tf_op jit(solution)/shard_map/ppermute | solution.py:50
  33.8 2.1 %copy-start.4 = (f32[8,3072]{1,0:T(8,128)}, f32[8,3072]{1,0:T(8,128)S(1)}, u32[]{:S(2)}) copy-start(f32[8,3072]{1,0:T(8,128)S(1)} %add.15.own) | copy-start | bytes 294916
  33.8 1.4 %collective-permute-start.4 = (f32[8,3072]{1,0:T(8,128)S(1)}, f32[8,3072]{1,0:T(8,128)S(1)}, u32[]{:S(2)}, u32[]{:S(2)}) collective-permute-start(f32[8,3072]{1,0:T(8,128)S(1)} %add.15.own), channel_id=1, source_target_pairs={{0,1},{1,0},{2,3},{3,2},{4,5},{5,4},{6,7},{7,6},{8,9},{9,8},{10,11... | collective-permute-start | bytes 294920 | tf_op jit(solution)/shard_map/ppermute | solution.py:50
  34.0 1.9 %copy-start.3 = (bf16[16,8,3072]{2,1,0:T(8,128)(2,1)}, bf16[16,8,3072]{2,1,0:T(8,128)(2,1)S(1)}, u32[]{:S(2)}) copy-start(bf16[16,8,3072]{2,1,0:T(8,128)(2,1)S(1)} %constant_dynamic-update-slice_fusion.5.got_b) | copy-start | bytes 2359300
  34.0 1.9 %copy-start.2 = (bf16[16,8,3200]{2,1,0:T(8,128)(2,1)}, bf16[16,8,3200]{2,1,0:T(8,128)(2,1)S(1)}, u32[]{:S(2)}) copy-start(bf16[16,8,3200]{2,1,0:T(8,128)(2,1)S(1)} %constant_dynamic-update-slice_fusion.got_a) | copy-start | bytes 2457604
  35.2 0.7 %copy-start.5 = (f32[8,3072]{1,0:T(8,128)}, f32[8,3072]{1,0:T(8,128)S(1)}, u32[]{:S(2)}) copy-start(f32[8,3072]{1,0:T(8,128)S(1)} %collective-permute-done.4.other) | copy-start | bytes 294916

commit v2 on v0

v2 whole, which is shorter than its diff:
```python
import functools
import math

import jax
import jax.numpy as jnp
import ml_dtypes
import numpy as np
from jax import lax
from jax.experimental import pallas as pl
from jax.experimental.pallas import tpu as pltpu
from jax.sharding import PartitionSpec as P

NFFT = 12000
LAGW = 1024
SMOOTH = 64
LANES = 128
SPLIT = 4
LAGS = LAGW // SPLIT
VMEM = pl.BlockSpec(memory_space=pltpu.VMEM)
SMEM = pl.BlockSpec(memory_space=pltpu.SMEM)
f32 = jnp.float32
bf16 = jnp.bfloat16


def lag_tables(bins):
    k = np.arange(1, bins + 1, dtype=np.int64)
    angle = 2.0 * np.pi / NFFT * np.mod(k[:, None] * np.arange(LAGS)[None, :], NFFT)
    both = np.stack([np.cos(angle), -np.sin(angle)]).reshape(2, bins // LANES, LANES, LAGS)
    table = both.transpose(1, 0, 2, 3).reshape(2 * bins, LAGS).astype(ml_dtypes.bfloat16)
    turn = 2.0 * np.pi / NFFT * np.mod(k[None, :] * (LAGS * np.arange(SPLIT))[:, None], NFFT)
    return table, np.stack([np.cos(turn), np.sin(turn)]).astype(np.float32)


def orders(owners):
    bits = [1 << i for i in range(owners.bit_length() - 1)]
    far = bits[:0:-1]
    other = far[:-2] + far[-2:][::-1]
    return bits[1:], (far + [1], other + [1])


def masks(order):
    out = [0]
    for bit in order:
        out = out + [m ^ bit for m in out]
    return out


def swap(value, bit):
    owners = lax.axis_size("chan")
    return lax.ppermute(value, "chan", [(i, i ^ bit) for i in range(owners)])


def prepare(bins, source_pick, lag_start, bad_flag, spectra, *outs):
    core = lax.axis_index("chan") & 1
    pick, lag = source_pick[0], lag_start[0]
    half = bins // 2
    keep = (1 - bad_flag[pick]).astype(f32)
    row = lax.broadcasted_iota(jnp.int32, (spectra.shape[1], LANES), 0)
    high = lax.shift_right_arithmetic(lag, 5)
    low = lag - high * 32
    extra = jnp.where(row == 0, high.astype(f32), jnp.where(row == 1, low.astype(f32), keep))
    for h in range(2):
        own, other, rows = outs[3 * h : 3 * h + 3]
        for part in range(2):
            src = pl.ds(part * bins + h * half, half)
            total = spectra[0, :, src].astype(f32)
            for r in range(1, spectra.shape[0]):
                total = total + spectra[r, :, src].astype(f32)

            @pl.when(core == part)
            def _():
                own[...] = total

            @pl.when(core != part)
            def _():
                other[...] = total

            rows[0, :, pl.ds(part * half, half)] = spectra[pick, :, src]
        rows[0, :, pl.ds(bins, LANES)] = extra.astype(bf16)


def cos_sin(turns):
    whole = jnp.floor(turns * (1.0 / NFFT) + 0.5)
    rest = turns - whole * NFFT
    quarter = jnp.floor(rest * (4.0 / NFFT) + 0.5)
    phi = (rest - quarter * (NFFT / 4)) * (2.0 * math.pi / NFFT)
    sq = phi * phi
    s = phi * (1.0 + sq * (-1 / 6 + sq * (1 / 120 + sq * (-1 / 5040))))
    c = 1.0 + sq * (-0.5 + sq * (1 / 24 + sq * (-1 / 720 + sq * (1 / 40320))))
    swapped = jnp.abs(quarter) == 1.0
    cos_neg = (quarter == 1.0) | (jnp.abs(quarter) == 2.0)
    sin_neg = (quarter == -1.0) | (jnp.abs(quarter) == 2.0)
    cosine = jnp.where(swapped, s, c)
    sine = jnp.where(swapped, c, s)
    return jnp.where(cos_neg, -cosine, cosine), jnp.where(sin_neg, -sine, sine)


def correlate(h, bins, order_a, order, channels, bad_flag, spectra, own, other, got, table, turn, *rest):
    if h == 0:
        out, rec, src, ang, cross = rest
        before = None
    else:
        before, out, rec, src, ang, cross = rest
    me = lax.axis_index("chan").astype(jnp.int32)
    core = me & 1
    receivers, windows = spectra.shape[0], spectra.shape[1]
    sources = got.shape[0]
    half = bins // 2
    chunks = half // LANES
    span = sources * receivers
    norm = 1.0 / math.sqrt(windows * bins)
    block_i = lax.broadcasted_iota(jnp.int32, (LANES, LANES), 0) // SMOOTH
    block_j = lax.broadcasted_iota(jnp.int32, (LANES, LANES), 1) // SMOOTH
    same = jnp.where(block_i == block_j, 1.0, 0.0).astype(bf16)
    lane = lax.broadcasted_iota(jnp.int32, (1, LANES), 1)
    inv = 1.0 / channels
    places, seen = masks(order_a), masks(order)
    held = [seen.index(m) for m in places]
    keep = [(1 - bad_flag[r]).astype(f32) for r in range(receivers)]
    tail = got[:, :, pl.ds(bins, LANES)].astype(f32)
    lags = tail[:, 0, :] * 32.0 + tail[:, 1, :]

    def scales(power):
        count = power.shape[0]
        power = power.reshape(count * windows, LANES)
        high = power.astype(bf16)
        low = (power - high.astype(f32)).astype(bf16)
        level = jnp.dot(high, same, preferred_element_type=f32) + jnp.dot(
            low, same, preferred_element_type=f32
        )
        return lax.rsqrt(level * (1.0 / SMOOTH) + 1e-6).reshape(count, windows, LANES)

    def chunk(c, _):
        re_at = pl.ds(pl.multiple_of(c * LANES, LANES), LANES)
        im_at = pl.ds(pl.multiple_of(half + c * LANES, LANES), LANES)
        bin_at = pl.ds(pl.multiple_of(h * half + c * LANES, LANES), LANES)
        imag_at = pl.ds(pl.multiple_of(bins + h * half + c * LANES, LANES), LANES)
        m_own, m_other = own[:, re_at] * inv, other[:, re_at] * inv
        m_re = jnp.where(core == 0, m_own, m_other)
        m_im = jnp.where(core == 0, m_other, m_own)
        x_re = spectra[:, :, bin_at].astype(f32) - m_re[None]
        x_im = spectra[:, :, imag_at].astype(f32) - m_im[None]
        scale = scales(x_re * x_re + x_im * x_im)
        for r in range(receivers):
            factor = scale[r] * keep[r]
            rec[0, r] = (x_re[r] * factor).astype(bf16).astype(f32)
            rec[1, r] = (x_im[r] * factor).astype(bf16).astype(f32)
        k = (lane + (h * half + 1) + c * LANES).astype(f32)
        ang[0], ang[1] = cos_sin(lags * k)
        g_re = got[:, :, re_at].astype(f32) - m_re[None]
        g_im = got[:, :, im_at].astype(f32) - m_im[None]
        scale = scales(g_re * g_re + g_im * g_im)
        for i in range(sources):
            factor = scale[i] * jnp.broadcast_to(tail[i, 2:3, :], (windows, LANES))
            w_re = (g_re[i] * factor).astype(bf16).astype(f32)
            w_im = (g_im[i] * factor).astype(bf16).astype(f32)
            cosine = jnp.broadcast_to(ang[0, i : i + 1, :], (windows, LANES))
            sine = jnp.broadcast_to(ang[1, i : i + 1, :], (windows, LANES))
            src[0, i] = (w_re * cosine + w_im * sine).astype(bf16).astype(f32)
            src[1, i] = (w_im * cosine - w_re * sine).astype(bf16).astype(f32)
        a = [rec[0, :, w, :] for w in range(windows)]
        b = [rec[1, :, w, :] for w in range(windows)]
        turns = [(turn[0, q : q + 1, bin_at], turn[1, q : q + 1, bin_at]) for q in range(SPLIT)]
        for p in range(0, sources, 2):
            pair = []
            for i in (held[p], held[p + 1]):
                c_re = c_im = None
                for w in range(windows):
                    g = jnp.broadcast_to(src[0, i, w : w + 1, :], (receivers, LANES))
                    e = jnp.broadcast_to(src[1, i, w : w + 1, :], (receivers, LANES))
                    t_re = g * a[w] + e * b[w]
                    t_im = g * b[w] - e * a[w]
                    c_re = t_re if c_re is None else c_re + t_re
                    c_im = t_im if c_im is None else c_im + t_im
                pair.append((c_re * norm, c_im * norm))
            p_re = jnp.concatenate([pair[0][0], pair[1][0]], 0)
            p_im = jnp.concatenate([pair[0][1], pair[1][1]], 0)
            for q in range(SPLIT):
                ct, st = turns[q]
                done = (p_re, p_im) if q == 0 else (p_re * ct - p_im * st, p_re * st + p_im * ct)
                at = q * span + p * receivers
                for part in range(2):
                    cols = pl.ds(pl.multiple_of((2 * c + part) * LANES, LANES), LANES)
                    cross[at : at + 2 * receivers, cols] = done[part].astype(bf16)
        return 0

    lax.fori_loop(0, chunks, chunk, 0)
    product = jnp.dot(cross[...], table[...], preferred_element_type=f32)
    if h == 0:
        out[...] = product
        return
    product = product + before[...]
    for p in range(sources):
        source = jnp.bitwise_xor(me, places[p])
        for q in range(SPLIT):
            at = q * span + p * receivers
            out[source, :, q * LAGS : (q + 1) * LAGS] = product[at : at + receivers, :]


def shards(spectra, bad_flag, source_pick, lag_start):
    receivers, windows, width_both = spectra.shape
    bins = width_both // 2
    owners = lax.axis_size("chan")
    half = bins // 2
    flat = jax.ShapeDtypeStruct((windows, half), f32)
    rows = jax.ShapeDtypeStruct((1, windows, bins + LANES), bf16)
    ready = pl.pallas_call(
        functools.partial(prepare, bins),
        out_shape=(flat, flat, rows) * 2,
        in_specs=[SMEM, SMEM, SMEM, VMEM],
        out_specs=(VMEM,) * 6,
        compiler_params=pltpu.CompilerParams(vmem_limit_bytes=16 << 20),
        name="prepare",
    )(source_pick, lag_start, bad_flag, spectra)
    near, order = orders(owners)
    table, turn = lag_tables(bins)
    whole = SPLIT * owners * receivers
    result = ()
    for h in range(2):
        own, other, got = ready[3 * h : 3 * h + 3]
        total = own + swap(other, 1)
        for bit in near:
            total = total + swap(total, bit)
        rest = swap(total, 1)
        for bit in order[h]:
            got = jnp.concatenate([got, swap(got, bit)], 0)
        shape = (whole, LAGS) if h == 0 else (owners, receivers, LAGW)
        result = (pl.pallas_call(
            functools.partial(correlate, h, bins, order[0], order[h], receivers * owners),
            out_shape=jax.ShapeDtypeStruct(shape, f32),
            in_specs=[SMEM] + [VMEM] * (6 + h),
            out_specs=VMEM,
            scratch_shapes=[
                pltpu.VMEM((2, receivers, windows, LANES), f32),
                pltpu.VMEM((2, owners, windows, LANES), f32),
                pltpu.VMEM((2, owners, LANES), f32),
                pltpu.VMEM((whole, bins), bf16),
            ],
            compiler_params=pltpu.CompilerParams(vmem_limit_bytes=30 << 20),
            cost_estimate=pl.CostEstimate(flops=6 * 10**9, bytes_accessed=6 << 20, transcendentals=0),
            name="correlate",
        )(bad_flag, spectra, total, rest, got, jnp.asarray(table[h * bins : (h + 1) * bins]), jnp.asarray(turn), *result),)
    return result[0]


def solution(mesh):
    in_specs = (
        P(("groups", "chan"), None, None),
        P(("groups", "chan")),
        P(("groups", "chan")),
        P(("groups", "chan")),
    )
    out_specs = P(None, ("groups", "chan"), None)
    return jax.shard_map(shards, mesh=mesh, in_specs=in_specs, out_specs=out_specs, check_vma=False)
```

time: 1600 us -> 46.7 us (0.03)
  waiting for transfers between devices: 1470 us -> 8.14 us
  other arithmetic: 104 us -> 0.26 us
  starting transfers between devices: 0.64 us -> 18.5 us
  Pallas kernels: 0 us -> 16 us
    psum x17 -> x0, waiting for transfers between devices: 1470 us -> none  [the longest x16 1430 us: broadcast(): return lax.psum(kept, axis)]
    another operation x2 -> x0, other arithmetic: 55.8 us -> none
    ppermute x0 -> x18, starting transfers between devices: none -> 18.5 us  [swap(): return lax.ppermute(value, 'chan', [(i, i ^ bit) for i in range(owners)])]
    pallas_call x0 -> x3, Pallas kernels: none -> 16 us  [the longest x2 15.4 us: shards(): pl.pallas_call(functools.partial(correlate, h, bins, order[0], order[h],...]
  transfers between devices with their start and end apart: 17 -> 18, of which waited for: 17 -> 6; matrix products, arithmetic and copies ran while one was open for 4% -> 1% of each run, Pallas kernels for 0% -> 16%
where the time goes in v2:
time: 46.7 us; the launch traced here: 46.5 us
  starting transfers between devices  18.5 us (40%)
  Pallas kernels  16 us (34%)
  waiting for transfers between devices  8.14 us (17%)
  local copies, waits for them, and re-layouts  1.99 us (4%)
  between operations  1.55 us (3%)
    ppermute x18, starting transfers between devices, swap(): return lax.ppermute(value, 'chan', [(i, i ^ bit) for i in range(owners)])  18.5 us
    pallas_call x2, Pallas kernels, shards(): pl.pallas_call(functools.partial(correlate, h, bins, order[0], order[h],...  15.4 us
    ppermute x18, waiting for transfers between devices, swap(): return lax.ppermute(value, 'chan', [(i, i ^ bit) for i in range(owners)])  8.14 us
    unnamed x21, local copies, waits for them, and re-layouts  1.92 us
  transfers between devices with their start and end apart: 18, of which 6 were waited for; matrix products, arithmetic and copies ran while one was open for 1% of the time, Pallas kernels for 16%

profile of v2, /device:TPU:0, one launch (start us, length us, event | category | flops | bytes accessed | tf_op | source)
XLA Modules:
  0.0 46.5 jit_solution(8673111821095924401)
XLA Ops:
  1.3 0.0 copy-start
  1.3 1.1 %copy-done = bf16[8,8,6144]{2,1,0:T(8,128)(2,1)S(1)} copy-done((bf16[8,8,6144]{2,1,0:T(8,128)(2,1)S(1)}, bf16[8,8,6144]{2,1,0:T(8,128)(2,1)}, u32[]{:S(2)}) %copy-start) | copy-done | bytes 786456
  2.4 0.0 copy-start.2
  2.4 0.7 %copy-done.2 = s32[8]{0:T(128)S(1)} copy-done((s32[8]{0:T(128)S(1)}, s32[8]{0:T(128)}, u32[]{:S(2)}) %copy-start.2) | copy-done | bytes 56
  3.1 0.7 %prepare.1 = (f32[8,1536]{1,0:T(8,128)S(1)}, f32[8,1536]{1,0:T(8,128)S(1)}, bf16[1,8,3200]{2,1,0:T(8,128)(2,1)S(1)}, f32[8,1536]{1,0:T(8,128)S(1)}, f32[8,1536]{...) custom-call(s32[1]{0:T(128)S(6)} %copy.16.source_pick, s32[1]{0:T(128)S(6)} %copy.17.lag_start, s32[8]{0:T(128)S(1)} %copy-done.2, ...), custom_call_target="tpu_custom_call" | custom-call | tf_op jit(solution)/shard_map/prepare/pallas_call | solution.py:207
  3.8 4.1 %collective-permute-start.14 = (bf16[1,8,3200]{2,1,0:T(8,128)(2,1)S(1)}, bf16[1,8,3200]{2,1,0:T(8,128)(2,1)S(1)}, u32[]{:S(2)}, u32[]{:S(2)}) collective-permute-start(bf16[1,8,3200]{2,1,0:T(8,128)(2,1)S(1)} %get-tuple-element.16), channel_id=1, source_target_pairs={{0,8},{1,9},{2,10},{3,11},{4,12},{5,13},{6,14},{7,15},{8,0},{9,1},... | collective-permute-start | bytes 153608 | tf_op jit(solution)/shard_map/ppermute | solution.py:50
  7.9 0.0 collective-permute-start.9
  7.9 0.2 collective-permute-start.5
  8.0 0.4 collective-permute-start
  8.4 0.7 %collective-permute-done.9 = f32[8,1536]{1,0:T(8,128)S(1)} collective-permute-done((f32[8,1536]{1,0:T(8,128)S(1)}, f32[8,1536]{1,0:T(8,128)S(1)}, u32[]{:S(2)}, u32[]{:S(2)}) %collective-permute-start.9) | collective-permute-done | bytes 49184 | tf_op jit(solution)/shard_map/ppermute | solution.py:50
  9.1 1.6 %collective-permute-start.10 = (f32[8,1536]{1,0:T(8,128)S(1)}, f32[8,1536]{1,0:T(8,128)S(1)}, u32[]{:S(2)}, u32[]{:S(2)}) collective-permute-start(f32[8,1536]{1,0:T(8,128)S(1)} %add.28), channel_id=1, source_target_pairs={{0,2},{1,3},{2,0},{3,1},{4,6},{5,7},{6,4},{7,5},{8,10},{9,11},{10,... | collective-permute-start | bytes 147464 | tf_op jit(solution)/shard_map/ppermute | solution.py:50
  10.7 0.0 collective-permute-done
  10.7 0.6 %collective-permute-start.1 = (f32[8,1536]{1,0:T(8,128)S(1)}, f32[8,1536]{1,0:T(8,128)S(1)}, u32[]{:S(2)}, u32[]{:S(2)}) collective-permute-start(f32[8,1536]{1,0:T(8,128)S(1)} %add.24), channel_id=1, source_target_pairs={{0,2},{1,3},{2,0},{3,1},{4,6},{5,7},{6,4},{7,5},{8,10},{9,11},{10,... | collective-permute-start | bytes 147464 | tf_op jit(solution)/shard_map/ppermute | solution.py:50
  11.3 0.0 collective-permute-done.14
  11.3 1.8 %collective-permute-start.15 = (bf16[2,8,3200]{2,1,0:T(8,128)(2,1)S(1)}, bf16[2,8,3200]{2,1,0:T(8,128)(2,1)S(1)}, u32[]{:S(2)}, u32[]{:S(2)}) collective-permute-start(bf16[2,8,3200]{2,1,0:T(8,128)(2,1)S(1)} %pad_maximum_fusion.5), channel_id=1, source_target_pairs={{0,4},{1,5},{2,6},{3,7},{4,0},{5,1},{6,2},{7,3},{8,12},{9,13},{10,... | collective-permute-start | bytes 307208 | tf_op jit(solution)/shard_map/ppermute | solution.py:50
  13.1 0.0 collective-permute-done.5
  13.1 1.6 %collective-permute-start.6 = (bf16[2,8,3200]{2,1,0:T(8,128)(2,1)S(1)}, bf16[2,8,3200]{2,1,0:T(8,128)(2,1)S(1)}, u32[]{:S(2)}, u32[]{:S(2)}) collective-permute-start(bf16[2,8,3200]{2,1,0:T(8,128)(2,1)S(1)} %pad_maximum_fusion.4), channel_id=1, source_target_pairs={{0,2},{1,3},{2,0},{3,1},{4,6},{5,7},{6,4},{7,5},{8,10},{9,11},{10,... | collective-permute-start | bytes 307208 | tf_op jit(solution)/shard_map/ppermute | solution.py:50
  14.7 0.0 collective-permute-done.10
  14.8 1.6 %collective-permute-start.11 = (f32[8,1536]{1,0:T(8,128)S(1)}, f32[8,1536]{1,0:T(8,128)S(1)}, u32[]{:S(2)}, u32[]{:S(2)}) collective-permute-start(f32[8,1536]{1,0:T(8,128)S(1)} %add.29), channel_id=1, source_target_pairs={{0,4},{1,5},{2,6},{3,7},{4,0},{5,1},{6,2},{7,3},{8,12},{9,13},{10,... | collective-permute-start | bytes 147464 | tf_op jit(solution)/shard_map/ppermute | solution.py:50
  16.3 0.0 collective-permute-done.1
  16.3 0.6 %collective-permute-start.2 = (f32[8,1536]{1,0:T(8,128)S(1)}, f32[8,1536]{1,0:T(8,128)S(1)}, u32[]{:S(2)}, u32[]{:S(2)}) collective-permute-start(f32[8,1536]{1,0:T(8,128)S(1)} %add.25), channel_id=1, source_target_pairs={{0,4},{1,5},{2,6},{3,7},{4,0},{5,1},{6,2},{7,3},{8,12},{9,13},{10,... | collective-permute-start | bytes 147464 | tf_op jit(solution)/shard_map/ppermute | solution.py:50
  16.9 2.2 %collective-permute-done.11 = f32[8,1536]{1,0:T(8,128)S(1)} collective-permute-done((f32[8,1536]{1,0:T(8,128)S(1)}, f32[8,1536]{1,0:T(8,128)S(1)}, u32[]{:S(2)}, u32[]{:S(2)}) %collective-permute-start.11) | collective-permute-done | bytes 49184 | tf_op jit(solution)/shard_map/ppermute | solution.py:50
  19.1 3.2 %collective-permute-start.12 = (f32[8,1536]{1,0:T(8,128)S(1)}, f32[8,1536]{1,0:T(8,128)S(1)}, u32[]{:S(2)}, u32[]{:S(2)}) collective-permute-start(f32[8,1536]{1,0:T(8,128)S(1)} %add.30), channel_id=1, source_target_pairs={{0,8},{1,9},{2,10},{3,11},{4,12},{5,13},{6,14},{7,15},{8,0},{9,1},... | collective-permute-start | bytes 147464 | tf_op jit(solution)/shard_map/ppermute | solution.py:50
  22.4 0.0 collective-permute-done.2
  22.4 0.8 %collective-permute-start.3 = (f32[8,1536]{1,0:T(8,128)S(1)}, f32[8,1536]{1,0:T(8,128)S(1)}, u32[]{:S(2)}, u32[]{:S(2)}) collective-permute-start(f32[8,1536]{1,0:T(8,128)S(1)} %add.26), channel_id=1, source_target_pairs={{0,8},{1,9},{2,10},{3,11},{4,12},{5,13},{6,14},{7,15},{8,0},{9,1},... | collective-permute-start | bytes 147464 | tf_op jit(solution)/shard_map/ppermute | solution.py:50
  23.2 0.0 collective-permute-done.15
  23.2 0.3 collective-permute-start.16
  23.6 0.0 collective-permute-done.6
  23.6 1.5 %collective-permute-start.7 = (bf16[4,8,3200]{2,1,0:T(8,128)(2,1)S(1)}, bf16[4,8,3200]{2,1,0:T(8,128)(2,1)S(1)}, u32[]{:S(2)}, u32[]{:S(2)}) collective-permute-start(bf16[4,8,3200]{2,1,0:T(8,128)(2,1)S(1)} %pad_maximum_fusion.2), channel_id=1, source_target_pairs={{0,4},{1,5},{2,6},{3,7},{4,0},{5,1},{6,2},{7,3},{8,12},{9,13},{10,... | collective-permute-start | bytes 614408 | tf_op jit(solution)/shard_map/ppermute | solution.py:50
  25.2 0.0 collective-permute-done.12
  25.2 0.1 collective-permute-start.13
  25.3 2.7 %collective-permute-done.3 = f32[8,1536]{1,0:T(8,128)S(1)} collective-permute-done((f32[8,1536]{1,0:T(8,128)S(1)}, f32[8,1536]{1,0:T(8,128)S(1)}, u32[]{:S(2)}, u32[]{:S(2)}) %collective-permute-start.3) | collective-permute-done | bytes 49184 | tf_op jit(solution)/shard_map/ppermute | solution.py:50
  28.0 0.0 copy-start.1
  28.0 0.0 copy-start.3
  28.0 0.0 copy-start.5
  28.0 0.0 copy-start.6
  28.0 0.1 collective-permute-start.4
  28.1 1.0 %collective-permute-done.16 = bf16[4,8,3200]{2,1,0:T(8,128)(2,1)S(1)} collective-permute-done((bf16[4,8,3200]{2,1,0:T(8,128)(2,1)S(1)}, bf16[4,8,3200]{2,1,0:T(8,128)(2,1)S(1)}, u32[]{:S(2)}, u32[]{:S(2)}) %collective-permute-start.16) | collective-permute-done | bytes 204832 | tf_op jit(solution)/shard_map/ppermute | solution.py:50
  29.1 0.1 pad_maximum_fusion.1
  29.1 0.1 collective-permute-start.17
  29.2 0.6 %collective-permute-done.7 = bf16[4,8,3200]{2,1,0:T(8,128)(2,1)S(1)} collective-permute-done((bf16[4,8,3200]{2,1,0:T(8,128)(2,1)S(1)}, bf16[4,8,3200]{2,1,0:T(8,128)(2,1)S(1)}, u32[]{:S(2)}, u32[]{:S(2)}) %collective-permute-start.7) | collective-permute-done | bytes 204832 | tf_op jit(solution)/shard_map/ppermute | solution.py:50
  29.8 0.1 pad_maximum_fusion
  29.9 0.1 collective-permute-start.8
  30.0 1.0 %collective-permute-done.17 = bf16[8,8,3200]{2,1,0:T(8,128)(2,1)S(1)} collective-permute-done((bf16[8,8,3200]{2,1,0:T(8,128)(2,1)S(1)}, bf16[8,8,3200]{2,1,0:T(8,128)(2,1)S(1)}, u32[]{:S(2)}, u32[]{:S(2)}) %collective-permute-start.17) | collective-permute-done | bytes 409632 | tf_op jit(solution)/shard_map/ppermute | solution.py:50
  31.0 0.0 copy-start.4
  31.0 0.0 collective-permute-done.13.other
  31.0 0.0 copy-done.1
  31.0 0.0 copy-done.3
  31.0 0.0 copy-done.5
  31.0 0.0 copy-done.6
  31.0 7.3 %correlate.2.rest_0_ = f32[512,256]{1,0:T(8,128)S(1)} custom-call(s32[8]{0:T(128)S(1)} %copy-done.3, bf16[8,8,6144]{2,1,0:T(8,128)(2,1)S(1)} %copy-done.1, f32[8,1536]{1,0:T(8,128)S(1)} %add.31.own, f32[8,1536]{1,0:T(8,128)S(1)} %collective-permute-done.13.other, bf16[16,8,3200]{2,1,0:T(8,128)(2,1)S(1)} %constant_dynamic-update-slice_fusion.5.got, ...), custom_call_target="tpu_custom_call" | custom-call | flops 6000000000 | bytes 6291456 | tf_op jit(solution)/shard_map/correlate/pallas_call | solution.py:228
  38.4 0.0 collective-permute-done.8
  38.4 0.0 collective-permute-done.4.other
  38.4 0.0 copy-done.4
  38.5 8.0 %correlate.3 = f32[16,8,1024]{2,1,0:T(8,128)} custom-call(s32[8]{0:T(128)S(1)} %copy-done.3, bf16[8,8,6144]{2,1,0:T(8,128)(2,1)S(1)} %copy-done.1, f32[8,1536]{1,0:T(8,128)S(1)} %add.27.own, f32[8,1536]{1,0:T(8,128)S(1)} %collective-permute-done.4.other, bf16[16,8,3200]{2,1,0:T(8,128)(2,1)S(1)} %constant_dynamic-update-slice_fusion.got, ...), custom_call_target="tpu_custom_call" | custom-call | flops 6000000000 | bytes 6291456 | tf_op jit(solution)/shard_map/correlate/pallas_call | solution.py:228
  (21 shorter events, 0.3 us)
Async XLA Ops:
  1.3 1.1 %copy-start = (bf16[8,8,6144]{2,1,0:T(8,128)(2,1)S(1)}, bf16[8,8,6144]{2,1,0:T(8,128)(2,1)}, u32[]{:S(2)}) copy-start(bf16[8,8,6144]{2,1,0:T(8,128)(2,1)} %spectra.5) | copy-start | bytes 2359300
  2.4 0.7 %copy-start.2 = (s32[8]{0:T(128)S(1)}, s32[8]{0:T(128)}, u32[]{:S(2)}) copy-start(s32[8]{0:T(128)} %bad_flag.5) | copy-start | bytes 100
  3.8 7.5 %collective-permute-start.14 = (bf16[1,8,3200]{2,1,0:T(8,128)(2,1)S(1)}, bf16[1,8,3200]{2,1,0:T(8,128)(2,1)S(1)}, u32[]{:S(2)}, u32[]{:S(2)}) collective-permute-start(bf16[1,8,3200]{2,1,0:T(8,128)(2,1)S(1)} %get-tuple-element.16), channel_id=1, source_target_pairs={{0,8},{1,9},{2,10},{3,11},{4,12},{5,13},{6,14},{7,15},{8,0},{9,1},... | collective-permute-start | bytes 153608 | tf_op jit(solution)/shard_map/ppermute | solution.py:50
  7.9 1.2 %collective-permute-start.9 = (f32[8,1536]{1,0:T(8,128)S(1)}, f32[8,1536]{1,0:T(8,128)S(1)}, u32[]{:S(2)}, u32[]{:S(2)}) collective-permute-start(f32[8,1536]{1,0:T(8,128)S(1)} %get-tuple-element.15), channel_id=1, source_target_pairs={{0,1},{1,0},{2,3},{3,2},{4,5},{5,4},{6,7},{7,6},{8,9},{9,8},{10,11... | collective-permute-start | bytes 147464 | tf_op jit(solution)/shard_map/ppermute | solution.py:50
  7.9 5.2 %collective-permute-start.5 = (bf16[1,8,3200]{2,1,0:T(8,128)(2,1)S(1)}, bf16[1,8,3200]{2,1,0:T(8,128)(2,1)S(1)}, u32[]{:S(2)}, u32[]{:S(2)}) collective-permute-start(bf16[1,8,3200]{2,1,0:T(8,128)(2,1)S(1)} %get-tuple-element.13), channel_id=1, source_target_pairs={{0,8},{1,9},{2,10},{3,11},{4,12},{5,13},{6,14},{7,15},{8,0},{9,1},... | collective-permute-start | bytes 153608 | tf_op jit(solution)/shard_map/ppermute | solution.py:50
  8.0 2.7 %collective-permute-start = (f32[8,1536]{1,0:T(8,128)S(1)}, f32[8,1536]{1,0:T(8,128)S(1)}, u32[]{:S(2)}, u32[]{:S(2)}) collective-permute-start(f32[8,1536]{1,0:T(8,128)S(1)} %get-tuple-element.12), channel_id=1, source_target_pairs={{0,1},{1,0},{2,3},{3,2},{4,5},{5,4},{6,7},{7,6},{8,9},{9,8},{10,11... | collective-permute-start | bytes 147464 | tf_op jit(solution)/shard_map/ppermute | solution.py:50
  9.1 5.6 %collective-permute-start.10 = (f32[8,1536]{1,0:T(8,128)S(1)}, f32[8,1536]{1,0:T(8,128)S(1)}, u32[]{:S(2)}, u32[]{:S(2)}) collective-permute-start(f32[8,1536]{1,0:T(8,128)S(1)} %add.28), channel_id=1, source_target_pairs={{0,2},{1,3},{2,0},{3,1},{4,6},{5,7},{6,4},{7,5},{8,10},{9,11},{10,... | collective-permute-start | bytes 147464 | tf_op jit(solution)/shard_map/ppermute | solution.py:50
  10.7 5.6 %collective-permute-start.1 = (f32[8,1536]{1,0:T(8,128)S(1)}, f32[8,1536]{1,0:T(8,128)S(1)}, u32[]{:S(2)}, u32[]{:S(2)}) collective-permute-start(f32[8,1536]{1,0:T(8,128)S(1)} %add.24), channel_id=1, source_target_pairs={{0,2},{1,3},{2,0},{3,1},{4,6},{5,7},{6,4},{7,5},{8,10},{9,11},{10,... | collective-permute-start | bytes 147464 | tf_op jit(solution)/shard_map/ppermute | solution.py:50
  11.3 11.9 %collective-permute-start.15 = (bf16[2,8,3200]{2,1,0:T(8,128)(2,1)S(1)}, bf16[2,8,3200]{2,1,0:T(8,128)(2,1)S(1)}, u32[]{:S(2)}, u32[]{:S(2)}) collective-permute-start(bf16[2,8,3200]{2,1,0:T(8,128)(2,1)S(1)} %pad_maximum_fusion.5), channel_id=1, source_target_pairs={{0,4},{1,5},{2,6},{3,7},{4,0},{5,1},{6,2},{7,3},{8,12},{9,13},{10,... | collective-permute-start | bytes 307208 | tf_op jit(solution)/shard_map/ppermute | solution.py:50
  13.1 10.5 %collective-permute-start.6 = (bf16[2,8,3200]{2,1,0:T(8,128)(2,1)S(1)}, bf16[2,8,3200]{2,1,0:T(8,128)(2,1)S(1)}, u32[]{:S(2)}, u32[]{:S(2)}) collective-permute-start(bf16[2,8,3200]{2,1,0:T(8,128)(2,1)S(1)} %pad_maximum_fusion.4), channel_id=1, source_target_pairs={{0,2},{1,3},{2,0},{3,1},{4,6},{5,7},{6,4},{7,5},{8,10},{9,11},{10,... | collective-permute-start | bytes 307208 | tf_op jit(solution)/shard_map/ppermute | solution.py:50
  14.8 4.4 %collective-permute-start.11 = (f32[8,1536]{1,0:T(8,128)S(1)}, f32[8,1536]{1,0:T(8,128)S(1)}, u32[]{:S(2)}, u32[]{:S(2)}) collective-permute-start(f32[8,1536]{1,0:T(8,128)S(1)} %add.29), channel_id=1, source_target_pairs={{0,4},{1,5},{2,6},{3,7},{4,0},{5,1},{6,2},{7,3},{8,12},{9,13},{10,... | collective-permute-start | bytes 147464 | tf_op jit(solution)/shard_map/ppermute | solution.py:50
  16.3 6.0 %collective-permute-start.2 = (f32[8,1536]{1,0:T(8,128)S(1)}, f32[8,1536]{1,0:T(8,128)S(1)}, u32[]{:S(2)}, u32[]{:S(2)}) collective-permute-start(f32[8,1536]{1,0:T(8,128)S(1)} %add.25), channel_id=1, source_target_pairs={{0,4},{1,5},{2,6},{3,7},{4,0},{5,1},{6,2},{7,3},{8,12},{9,13},{10,... | collective-permute-start | bytes 147464 | tf_op jit(solution)/shard_map/ppermute | solution.py:50
  19.1 6.0 %collective-permute-start.12 = (f32[8,1536]{1,0:T(8,128)S(1)}, f32[8,1536]{1,0:T(8,128)S(1)}, u32[]{:S(2)}, u32[]{:S(2)}) collective-permute-start(f32[8,1536]{1,0:T(8,128)S(1)} %add.30), channel_id=1, source_target_pairs={{0,8},{1,9},{2,10},{3,11},{4,12},{5,13},{6,14},{7,15},{8,0},{9,1},... | collective-permute-start | bytes 147464 | tf_op jit(solution)/shard_map/ppermute | solution.py:50
  22.4 5.6 %collective-permute-start.3 = (f32[8,1536]{1,0:T(8,128)S(1)}, f32[8,1536]{1,0:T(8,128)S(1)}, u32[]{:S(2)}, u32[]{:S(2)}) collective-permute-start(f32[8,1536]{1,0:T(8,128)S(1)} %add.26), channel_id=1, source_target_pairs={{0,8},{1,9},{2,10},{3,11},{4,12},{5,13},{6,14},{7,15},{8,0},{9,1},... | collective-permute-start | bytes 147464 | tf_op jit(solution)/shard_map/ppermute | solution.py:50
  23.2 5.8 %collective-permute-start.16 = (bf16[4,8,3200]{2,1,0:T(8,128)(2,1)S(1)}, bf16[4,8,3200]{2,1,0:T(8,128)(2,1)S(1)}, u32[]{:S(2)}, u32[]{:S(2)}) collective-permute-start(bf16[4,8,3200]{2,1,0:T(8,128)(2,1)S(1)} %pad_maximum_fusion.3), channel_id=1, source_target_pairs={{0,2},{1,3},{2,0},{3,1},{4,6},{5,7},{6,4},{7,5},{8,10},{9,11},{10,... | collective-permute-start | bytes 614408 | tf_op jit(solution)/shard_map/ppermute | solution.py:50
  23.6 6.2 %collective-permute-start.7 = (bf16[4,8,3200]{2,1,0:T(8,128)(2,1)S(1)}, bf16[4,8,3200]{2,1,0:T(8,128)(2,1)S(1)}, u32[]{:S(2)}, u32[]{:S(2)}) collective-permute-start(bf16[4,8,3200]{2,1,0:T(8,128)(2,1)S(1)} %pad_maximum_fusion.2), channel_id=1, source_target_pairs={{0,4},{1,5},{2,6},{3,7},{4,0},{5,1},{6,2},{7,3},{8,12},{9,13},{10,... | collective-permute-start | bytes 614408 | tf_op jit(solution)/shard_map/ppermute | solution.py:50
  25.2 5.8 %collective-permute-start.13 = (f32[8,1536]{1,0:T(8,128)S(1)}, f32[8,1536]{1,0:T(8,128)S(1)}, u32[]{:S(2)}, u32[]{:S(2)}) collective-permute-start(f32[8,1536]{1,0:T(8,128)S(1)} %add.31.own), channel_id=1, source_target_pairs={{0,1},{1,0},{2,3},{3,2},{4,5},{5,4},{6,7},{7,6},{8,9},{9,8},{10,11... | collective-permute-start | bytes 147464 | tf_op jit(solution)/shard_map/ppermute | solution.py:50
  28.0 3.0 %copy-start.1 = (bf16[8,8,6144]{2,1,0:T(8,128)(2,1)S(1)}, bf16[8,8,6144]{2,1,0:T(8,128)(2,1)}, u32[]{:S(2)}) copy-start(bf16[8,8,6144]{2,1,0:T(8,128)(2,1)} %spectra.5) | copy-start | bytes 2359300
  28.0 3.1 %copy-start.3 = (s32[8]{0:T(128)S(1)}, s32[8]{0:T(128)}, u32[]{:S(2)}) copy-start(s32[8]{0:T(128)} %bad_flag.5) | copy-start | bytes 100
  28.0 3.1 %copy-start.5 = (bf16[3072,256]{1,0:T(8,128)(2,1)S(1)}, bf16[3072,256]{1,0:T(8,128)(2,1)}, u32[]{:S(2)}) copy-start(bf16[3072,256]{1,0:T(8,128)(2,1)} %constant.6.clone.table) | copy-start | bytes 4718596
  28.0 3.0 %copy-start.6 = (f32[2,4,3072]{2,1,0:T(4,128)S(1)}, f32[2,4,3072]{2,1,0:T(4,128)}, u32[]{:S(2)}) copy-start(f32[2,4,3072]{2,1,0:T(4,128)} %constant.7.clone.turn) | copy-start | bytes 294916
  28.0 10.4 %collective-permute-start.4 = (f32[8,1536]{1,0:T(8,128)S(1)}, f32[8,1536]{1,0:T(8,128)S(1)}, u32[]{:S(2)}, u32[]{:S(2)}) collective-permute-start(f32[8,1536]{1,0:T(8,128)S(1)} %add.27.own), channel_id=1, source_target_pairs={{0,1},{1,0},{2,3},{3,2},{4,5},{5,4},{6,7},{7,6},{8,9},{9,8},{10,11... | collective-permute-start | bytes 147464 | tf_op jit(solution)/shard_map/ppermute | solution.py:50
  29.1 1.8 %collective-permute-start.17 = (bf16[8,8,3200]{2,1,0:T(8,128)(2,1)S(1)}, bf16[8,8,3200]{2,1,0:T(8,128)(2,1)S(1)}, u32[]{:S(2)}, u32[]{:S(2)}) collective-permute-start(bf16[8,8,3200]{2,1,0:T(8,128)(2,1)S(1)} %pad_maximum_fusion.1), channel_id=1, source_target_pairs={{0,1},{1,0},{2,3},{3,2},{4,5},{5,4},{6,7},{7,6},{8,9},{9,8},{10,11... | collective-permute-start | bytes 1228808 | tf_op jit(solution)/shard_map/ppermute | solution.py:50
  29.9 8.5 %collective-permute-start.8 = (bf16[8,8,3200]{2,1,0:T(8,128)(2,1)S(1)}, bf16[8,8,3200]{2,1,0:T(8,128)(2,1)S(1)}, u32[]{:S(2)}, u32[]{:S(2)}) collective-permute-start(bf16[8,8,3200]{2,1,0:T(8,128)(2,1)S(1)} %pad_maximum_fusion), channel_id=1, source_target_pairs={{0,1},{1,0},{2,3},{3,2},{4,5},{5,4},{6,7},{7,6},{8,9},{9,8},{10,11... | collective-permute-start | bytes 1228808 | tf_op jit(solution)/shard_map/ppermute | solution.py:50
  31.0 7.5 %copy-start.4 = (bf16[3072,256]{1,0:T(8,128)(2,1)S(1)}, bf16[3072,256]{1,0:T(8,128)(2,1)}, u32[]{:S(2)}) copy-start(bf16[3072,256]{1,0:T(8,128)(2,1)} %constant.8.clone.table) | copy-start | bytes 4718596

commit v3 on v2

v3 whole, which is shorter than its diff:
```python
import functools
import math

import jax
import jax.numpy as jnp
import ml_dtypes
import numpy as np
from jax import lax
from jax.experimental import pallas as pl
from jax.experimental.pallas import tpu as pltpu
from jax.sharding import PartitionSpec as P

NFFT = 12000
LAGW = 1024
SMOOTH = 64
LANES = 128
UNROLL = 3
VMEM = pl.BlockSpec(memory_space=pltpu.VMEM)
SMEM = pl.BlockSpec(memory_space=pltpu.SMEM)
HBM = pl.BlockSpec(memory_space=pltpu.HBM)
f32 = jnp.float32
bf16 = jnp.bfloat16


def lag_table(bins):
    k = np.arange(1, bins + 1, dtype=np.int64)
    angle = 2.0 * np.pi / NFFT * np.mod(k[:, None] * np.arange(LAGW)[None, :], NFFT)
    both = np.stack([np.cos(angle), -np.sin(angle)]).reshape(2, bins // LANES, LANES, LAGW)
    return both.transpose(1, 0, 2, 3).reshape(2 * bins, LAGW).astype(ml_dtypes.bfloat16)


def orders(owners):
    bits = [1 << i for i in range(owners.bit_length() - 1)]
    far = bits[:0:-1]
    other = far[-1:] + far[:-1]
    return (bits[1:], bits[1:]), (far + [1], other + [1])


def masks(order):
    out = [0]
    for bit in order:
        out = out + [m ^ bit for m in out]
    return out


def swap(value, bit):
    owners = lax.axis_size("chan")
    return lax.ppermute(value, "chan", [(i, i ^ bit) for i in range(owners)])


def prepare(bins, source_pick, lag_start, bad_flag, spectra, *rest):
    outs, (held, flags, sems, flag_sem) = rest[:6], rest[6:]
    core = lax.axis_index("chan") & 1
    pick, lag = source_pick[0], lag_start[0]
    half = bins // 2
    copies = []
    for h in range(2):
        for part in range(2):
            src = pl.ds(part * bins + h * half, half)
            slot = 2 * h + part
            copies.append(pltpu.make_async_copy(spectra.at[:, :, src], held.at[slot], sems.at[slot]))
    flag_copy = pltpu.make_async_copy(bad_flag, flags, flag_sem)
    flag_copy.start()
    for copy in copies:
        copy.start()
    row = lax.broadcasted_iota(jnp.int32, (spectra.shape[1], LANES), 0)
    high = lax.shift_right_arithmetic(lag, 5)
    low = lag - high * 32
    flag_copy.wait()
    keep = (1 - flags[pick]).astype(f32)
    extra = jnp.where(row == 0, high.astype(f32), jnp.where(row == 1, low.astype(f32), keep))
    for h in range(2):
        own, other, rows = outs[3 * h : 3 * h + 3]
        rows[0, :, pl.ds(bins, LANES)] = extra.astype(bf16)
        for part in range(2):
            slot = 2 * h + part
            copies[slot].wait()
            total = held[slot, 0].astype(f32)
            for r in range(1, held.shape[1]):
                total = total + held[slot, r].astype(f32)

            @pl.when(core == part)
            def _():
                own[...] = total

            @pl.when(core != part)
            def _():
                other[...] = total

            rows[0, :, pl.ds(part * half, half)] = held[slot, pick]


def cos_sin(turns):
    whole = jnp.floor(turns * (1.0 / NFFT) + 0.5)
    rest = turns - whole * NFFT
    quarter = jnp.floor(rest * (4.0 / NFFT) + 0.5)
    phi = (rest - quarter * (NFFT / 4)) * (2.0 * math.pi / NFFT)
    sq = phi * phi
    s = phi * (1.0 + sq * (-1 / 6 + sq * (1 / 120 + sq * (-1 / 5040))))
    c = 1.0 + sq * (-0.5 + sq * (1 / 24 + sq * (-1 / 720 + sq * (1 / 40320))))
    swapped = jnp.abs(quarter) == 1.0
    cos_neg = (quarter == 1.0) | (jnp.abs(quarter) == 2.0)
    sin_neg = (quarter == -1.0) | (jnp.abs(quarter) == 2.0)
    cosine = jnp.where(swapped, s, c)
    sine = jnp.where(swapped, c, s)
    return jnp.where(cos_neg, -cosine, cosine), jnp.where(sin_neg, -sine, sine)


def correlate(h, bins, order, first_order, channels, bad_flag, spectra, own, other, got, table, *rest):
    before, (out, rec, src, ang, cross) = rest[:h], rest[h:]
    me = lax.axis_index("chan").astype(jnp.int32)
    core = me & 1
    receivers, windows = spectra.shape[0], spectra.shape[1]
    sources = got.shape[0]
    half = bins // 2
    chunks = half // LANES
    norm = 1.0 / math.sqrt(windows * bins)
    block_i = lax.broadcasted_iota(jnp.int32, (LANES, LANES), 0) // SMOOTH
    block_j = lax.broadcasted_iota(jnp.int32, (LANES, LANES), 1) // SMOOTH
    same = jnp.where(block_i == block_j, 1.0 / SMOOTH, 0.0).astype(bf16)
    lane = lax.broadcasted_iota(jnp.int32, (1, LANES), 1)
    inv = 1.0 / channels
    places, seen = masks(first_order), masks(order)
    held = [seen.index(m) for m in places]
    keep = [(1 - bad_flag[r]).astype(f32) for r in range(receivers)]
    tail = got[:, :, pl.ds(bins, LANES)].astype(f32)
    lags = tail[:, 0, :] * 32.0 + tail[:, 1, :]

    def scales(power):
        count = power.shape[0]
        power = power.reshape(count * windows, LANES)
        high = power.astype(bf16)
        low = (power - high.astype(f32)).astype(bf16)
        level = jnp.dot(high, same, preferred_element_type=f32) + jnp.dot(
            low, same, preferred_element_type=f32
        )
        return lax.rsqrt(level + 1e-6).reshape(count, windows, LANES)

    def rounded(value):
        return value.astype(bf16).astype(f32)

    def chunk(c, _):
        re_at = pl.ds(pl.multiple_of(c * LANES, LANES), LANES)
        im_at = pl.ds(pl.multiple_of(half + c * LANES, LANES), LANES)
        bin_at = pl.ds(pl.multiple_of(h * half + c * LANES, LANES), LANES)
        imag_at = pl.ds(pl.multiple_of(bins + h * half + c * LANES, LANES), LANES)
        m_own, m_other = own[:, re_at] * inv, other[:, re_at] * inv
        m_re = jnp.where(core == 0, m_own, m_other)
        m_im = jnp.where(core == 0, m_other, m_own)
        x_re = spectra[:, :, bin_at].astype(f32) - m_re[None]
        x_im = spectra[:, :, imag_at].astype(f32) - m_im[None]
        scale = scales(x_re * x_re + x_im * x_im)
        for r in range(receivers):
            factor = scale[r] * keep[r]
            rec[0, r] = rounded(x_re[r] * factor)
            rec[1, r] = rounded(x_im[r] * factor)
        k = (lane + (h * half + 1) + c * LANES).astype(f32)
        ang[0], ang[1] = cos_sin(lags * k)
        g_re = got[:, :, re_at].astype(f32) - m_re[None]
        g_im = got[:, :, im_at].astype(f32) - m_im[None]
        scale = scales(g_re * g_re + g_im * g_im)
        for i in range(sources):
            factor = scale[i] * jnp.broadcast_to(tail[i, 2:3, :], (windows, LANES))
            w_re = rounded(g_re[i] * factor)
            w_im = rounded(g_im[i] * factor)
            cosine = ang[0, pl.ds(i, windows, stride=0), :]
            sine = ang[1, pl.ds(i, windows, stride=0), :]
            src[0, i] = rounded(w_re * cosine + w_im * sine)
            src[1, i] = rounded(w_im * cosine - w_re * sine)
        a = [rec[0, :, w, :] for w in range(windows)]
        b = [rec[1, :, w, :] for w in range(windows)]
        for p in range(0, sources, 2):
            pair = []
            for i in (held[p], held[p + 1]):
                c_re = c_im = None
                for w in range(windows):
                    g = src[0, i, pl.ds(w, receivers, stride=0), :]
                    e = src[1, i, pl.ds(w, receivers, stride=0), :]
                    t_re = g * a[w] + e * b[w]
                    t_im = g * b[w] - e * a[w]
                    c_re = t_re if c_re is None else c_re + t_re
                    c_im = t_im if c_im is None else c_im + t_im
                pair.append((c_re * norm, c_im * norm))
            for part in range(2):
                cols = pl.ds(pl.multiple_of((2 * c + part) * LANES, LANES), LANES)
                both = jnp.concatenate([pair[0][part], pair[1][part]], 0)
                cross[p * receivers : (p + 2) * receivers, cols] = both.astype(bf16)
        return 0

    lax.fori_loop(0, chunks, chunk, 0, unroll=UNROLL)
    product = jnp.dot(cross[...], table[...], preferred_element_type=f32)
    if h == 0:
        out[...] = product
        return
    product = product + before[0][...]
    for p in range(sources):
        source = jnp.bitwise_xor(me, places[p])
        out[source] = product[p * receivers : (p + 1) * receivers, :]


def shards(spectra, bad_flag, source_pick, lag_start):
    receivers, windows, width_both = spectra.shape
    bins = width_both // 2
    owners = lax.axis_size("chan")
    half = bins // 2
    flat = jax.ShapeDtypeStruct((windows, half), f32)
    rows = jax.ShapeDtypeStruct((1, windows, bins + LANES), bf16)
    ready = pl.pallas_call(
        functools.partial(prepare, bins),
        out_shape=(flat, flat, rows) * 2,
        in_specs=[SMEM, SMEM, HBM, HBM],
        out_specs=(VMEM,) * 6,
        scratch_shapes=[
            pltpu.VMEM((4, receivers, windows, half), bf16),
            pltpu.SMEM((receivers,), jnp.int32),
            pltpu.SemaphoreType.DMA((4,)),
            pltpu.SemaphoreType.DMA(()),
        ],
        compiler_params=pltpu.CompilerParams(vmem_limit_bytes=16 << 20),
        name="prepare",
    )(source_pick, lag_start, bad_flag, spectra)
    total_order, row_order = orders(owners)
    table = lag_table(bins)
    totals, gots = [], []
    for h in range(2):
        own, other, got = ready[3 * h : 3 * h + 3]
        total = own + swap(other, 1)
        for bit in total_order[h]:
            total = total + swap(total, bit)
        totals.append((total, swap(total, 1)))
        for bit in row_order[h]:
            got = jnp.concatenate([got, swap(got, bit)], 0)
        gots.append(got)
    result = ()
    for h in range(2):
        shape = (owners * receivers, LAGW) if h == 0 else (owners, receivers, LAGW)
        result = (pl.pallas_call(
            functools.partial(correlate, h, bins, row_order[h], row_order[0], receivers * owners),
            out_shape=jax.ShapeDtypeStruct(shape, f32),
            in_specs=[SMEM] + [VMEM] * (5 + h),
            out_specs=VMEM,
            scratch_shapes=[
                pltpu.VMEM((2, receivers, windows, LANES), f32),
                pltpu.VMEM((2, owners, windows, LANES), f32),
                pltpu.VMEM((2, owners, LANES), f32),
                pltpu.VMEM((owners * receivers, bins), bf16),
            ],
            compiler_params=pltpu.CompilerParams(vmem_limit_bytes=24 << 20),
            cost_estimate=pl.CostEstimate(flops=5 * 10**9, bytes_accessed=10 << 20, transcendentals=0),
            name="correlate",
        )(bad_flag, spectra, *totals[h], gots[h], jnp.asarray(table[h * bins : (h + 1) * bins]), *result),)
    return result[0]


def solution(mesh):
    in_specs = (
        P(("groups", "chan"), None, None),
        P(("groups", "chan")),
        P(("groups", "chan")),
        P(("groups", "chan")),
    )
    out_specs = P(None, ("groups", "chan"), None)
    return jax.shard_map(shards, mesh=mesh, in_specs=in_specs, out_specs=out_specs, check_vma=False)
```

time: 46.7 us -> 42.5 us (0.910)
  Pallas kernels: 16 us -> 12.2 us
  waiting for transfers between devices: 8.14 us -> 6.39 us
  starting transfers between devices: 18.5 us -> 19.9 us
    pallas_call x2, Pallas kernels: 15.4 us -> 11.5 us  [shards(): pl.pallas_call(functools.partial(correlate, h, bins, row_order[h], row_or...]
    ppermute x18, waiting for transfers between devices: 8.14 us -> 6.39 us  [swap(): return lax.ppermute(value, 'chan', [(i, i ^ bit) for i in range(owners)])]
    ppermute x18, starting transfers between devices: 18.5 us -> 19.9 us  [swap(): return lax.ppermute(value, 'chan', [(i, i ^ bit) for i in range(owners)])]
  transfers between devices with their start and end apart: 18 -> 18, of which waited for: 6 -> 5; matrix products, arithmetic and copies ran while one was open for 1% -> 1% of each run, Pallas kernels for 16% -> 13%
where the time goes in v3:
time: 42.5 us; the launch traced here: 42.4 us
  starting transfers between devices  19.9 us (47%)
  Pallas kernels  12.2 us (29%)
  waiting for transfers between devices  6.39 us (15%)
  local copies, waits for them, and re-layouts  1.98 us (5%)
  between operations  1.56 us (4%)
    ppermute x18, starting transfers between devices, swap(): return lax.ppermute(value, 'chan', [(i, i ^ bit) for i in range(owners)])  19.9 us
    pallas_call x2, Pallas kernels, shards(): pl.pallas_call(functools.partial(correlate, h, bins, row_order[h], row_or...  11.5 us
    ppermute x18, waiting for transfers between devices, swap(): return lax.ppermute(value, 'chan', [(i, i ^ bit) for i in range(owners)])  6.39 us
    unnamed x21, local copies, waits for them, and re-layouts  1.9 us
  transfers between devices with their start and end apart: 18, of which 5 were waited for; matrix products, arithmetic and copies ran while one was open for 1% of the time, Pallas kernels for 13%

profile of v3, /device:TPU:0, one launch (start us, length us, event | category | flops | bytes accessed | tf_op | source)
XLA Modules:
  0.0 42.4 jit_solution(3152163234310433793)
XLA Ops:
  0.0 0.0 copy-start.3
  1.3 0.0 copy-start
  1.3 1.1 %copy-done = bf16[8,8,6144]{2,1,0:T(8,128)(2,1)S(1)} copy-done((bf16[8,8,6144]{2,1,0:T(8,128)(2,1)S(1)}, bf16[8,8,6144]{2,1,0:T(8,128)(2,1)}, u32[]{:S(2)}) %copy-start) | copy-done | bytes 786456
  2.4 0.0 copy-start.2
  2.4 0.7 %copy-done.2 = s32[8]{0:T(128)S(1)} copy-done((s32[8]{0:T(128)S(1)}, s32[8]{0:T(128)}, u32[]{:S(2)}) %copy-start.2) | copy-done | bytes 56
  3.1 0.0 copy-start.1
  3.1 0.0 copy-start.4
  3.1 0.7 %prepare.1 = (f32[8,1536]{1,0:T(8,128)S(1)}, f32[8,1536]{1,0:T(8,128)S(1)}, bf16[1,8,3200]{2,1,0:T(8,128)(2,1)S(1)}, f32[8,1536]{1,0:T(8,128)S(1)}, f32[8,1536]{...) custom-call(s32[1]{0:T(128)S(6)} %copy.15.source_pick, s32[1]{0:T(128)S(6)} %copy.16.lag_start, s32[8]{0:T(128)S(1)} %copy-done.2, ...), custom_call_target="tpu_custom_call" | custom-call | tf_op jit(solution)/shard_map/prepare/pallas_call | solution.py:208
  3.8 4.1 %collective-permute-start.14 = (bf16[1,8,3200]{2,1,0:T(8,128)(2,1)S(1)}, bf16[1,8,3200]{2,1,0:T(8,128)(2,1)S(1)}, u32[]{:S(2)}, u32[]{:S(2)}) collective-permute-start(bf16[1,8,3200]{2,1,0:T(8,128)(2,1)S(1)} %get-tuple-element.16), channel_id=1, source_target_pairs={{0,8},{1,9},{2,10},{3,11},{4,12},{5,13},{6,14},{7,15},{8,0},{9,1},... | collective-permute-start | bytes 153608 | tf_op jit(solution)/shard_map/ppermute | solution.py:48
  7.9 0.0 collective-permute-start.9
  7.9 1.5 %collective-permute-start.5 = (bf16[1,8,3200]{2,1,0:T(8,128)(2,1)S(1)}, bf16[1,8,3200]{2,1,0:T(8,128)(2,1)S(1)}, u32[]{:S(2)}, u32[]{:S(2)}) collective-permute-start(bf16[1,8,3200]{2,1,0:T(8,128)(2,1)S(1)} %get-tuple-element.13), channel_id=1, source_target_pairs={{0,2},{1,3},{2,0},{3,1},{4,6},{5,7},{6,4},{7,5},{8,10},{9,11},{10,... | collective-permute-start | bytes 153608 | tf_op jit(solution)/shard_map/ppermute | solution.py:48
  9.5 0.2 collective-permute-start
  9.7 0.0 collective-permute-done.9
  9.7 1.0 %collective-permute-start.10 = (f32[8,1536]{1,0:T(8,128)S(1)}, f32[8,1536]{1,0:T(8,128)S(1)}, u32[]{:S(2)}, u32[]{:S(2)}) collective-permute-start(f32[8,1536]{1,0:T(8,128)S(1)} %add.28), channel_id=1, source_target_pairs={{0,2},{1,3},{2,0},{3,1},{4,6},{5,7},{6,4},{7,5},{8,10},{9,11},{10,... | collective-permute-start | bytes 147464 | tf_op jit(solution)/shard_map/ppermute | solution.py:48
  10.8 0.0 collective-permute-done
  10.8 1.1 %collective-permute-start.1 = (f32[8,1536]{1,0:T(8,128)S(1)}, f32[8,1536]{1,0:T(8,128)S(1)}, u32[]{:S(2)}, u32[]{:S(2)}) collective-permute-start(f32[8,1536]{1,0:T(8,128)S(1)} %add.24), channel_id=1, source_target_pairs={{0,2},{1,3},{2,0},{3,1},{4,6},{5,7},{6,4},{7,5},{8,10},{9,11},{10,... | collective-permute-start | bytes 147464 | tf_op jit(solution)/shard_map/ppermute | solution.py:48
  11.9 0.0 collective-permute-done.14
  11.9 1.6 %collective-permute-start.15 = (bf16[2,8,3200]{2,1,0:T(8,128)(2,1)S(1)}, bf16[2,8,3200]{2,1,0:T(8,128)(2,1)S(1)}, u32[]{:S(2)}, u32[]{:S(2)}) collective-permute-start(bf16[2,8,3200]{2,1,0:T(8,128)(2,1)S(1)} %pad_maximum_fusion.5), channel_id=1, source_target_pairs={{0,4},{1,5},{2,6},{3,7},{4,0},{5,1},{6,2},{7,3},{8,12},{9,13},{10,... | collective-permute-start | bytes 307208 | tf_op jit(solution)/shard_map/ppermute | solution.py:48
  13.6 0.0 collective-permute-done.5
  13.6 1.5 %collective-permute-start.6 = (bf16[2,8,3200]{2,1,0:T(8,128)(2,1)S(1)}, bf16[2,8,3200]{2,1,0:T(8,128)(2,1)S(1)}, u32[]{:S(2)}, u32[]{:S(2)}) collective-permute-start(bf16[2,8,3200]{2,1,0:T(8,128)(2,1)S(1)} %pad_maximum_fusion.4), channel_id=1, source_target_pairs={{0,8},{1,9},{2,10},{3,11},{4,12},{5,13},{6,14},{7,15},{8,0},{9,1},... | collective-permute-start | bytes 307208 | tf_op jit(solution)/shard_map/ppermute | solution.py:48
  15.1 0.0 collective-permute-done.10
  15.2 0.7 %collective-permute-start.11 = (f32[8,1536]{1,0:T(8,128)S(1)}, f32[8,1536]{1,0:T(8,128)S(1)}, u32[]{:S(2)}, u32[]{:S(2)}) collective-permute-start(f32[8,1536]{1,0:T(8,128)S(1)} %add.29), channel_id=1, source_target_pairs={{0,4},{1,5},{2,6},{3,7},{4,0},{5,1},{6,2},{7,3},{8,12},{9,13},{10,... | collective-permute-start | bytes 147464 | tf_op jit(solution)/shard_map/ppermute | solution.py:48
  15.8 0.0 collective-permute-done.1
  15.9 1.5 %collective-permute-start.2 = (f32[8,1536]{1,0:T(8,128)S(1)}, f32[8,1536]{1,0:T(8,128)S(1)}, u32[]{:S(2)}, u32[]{:S(2)}) collective-permute-start(f32[8,1536]{1,0:T(8,128)S(1)} %add.25), channel_id=1, source_target_pairs={{0,4},{1,5},{2,6},{3,7},{4,0},{5,1},{6,2},{7,3},{8,12},{9,13},{10,... | collective-permute-start | bytes 147464 | tf_op jit(solution)/shard_map/ppermute | solution.py:48
  17.3 2.5 %collective-permute-done.11 = f32[8,1536]{1,0:T(8,128)S(1)} collective-permute-done((f32[8,1536]{1,0:T(8,128)S(1)}, f32[8,1536]{1,0:T(8,128)S(1)}, u32[]{:S(2)}, u32[]{:S(2)}) %collective-permute-start.11) | collective-permute-done | bytes 49184 | tf_op jit(solution)/shard_map/ppermute | solution.py:48
  19.8 1.7 %collective-permute-start.12 = (f32[8,1536]{1,0:T(8,128)S(1)}, f32[8,1536]{1,0:T(8,128)S(1)}, u32[]{:S(2)}, u32[]{:S(2)}) collective-permute-start(f32[8,1536]{1,0:T(8,128)S(1)} %add.30), channel_id=1, source_target_pairs={{0,8},{1,9},{2,10},{3,11},{4,12},{5,13},{6,14},{7,15},{8,0},{9,1},... | collective-permute-start | bytes 147464 | tf_op jit(solution)/shard_map/ppermute | solution.py:48
  21.6 0.0 collective-permute-done.2
  21.6 1.3 %collective-permute-start.3 = (f32[8,1536]{1,0:T(8,128)S(1)}, f32[8,1536]{1,0:T(8,128)S(1)}, u32[]{:S(2)}, u32[]{:S(2)}) collective-permute-start(f32[8,1536]{1,0:T(8,128)S(1)} %add.26), channel_id=1, source_target_pairs={{0,8},{1,9},{2,10},{3,11},{4,12},{5,13},{6,14},{7,15},{8,0},{9,1},... | collective-permute-start | bytes 147464 | tf_op jit(solution)/shard_map/ppermute | solution.py:48
  22.9 0.0 collective-permute-done.15
  23.0 1.6 %collective-permute-start.16 = (bf16[4,8,3200]{2,1,0:T(8,128)(2,1)S(1)}, bf16[4,8,3200]{2,1,0:T(8,128)(2,1)S(1)}, u32[]{:S(2)}, u32[]{:S(2)}) collective-permute-start(bf16[4,8,3200]{2,1,0:T(8,128)(2,1)S(1)} %pad_maximum_fusion.3), channel_id=1, source_target_pairs={{0,2},{1,3},{2,0},{3,1},{4,6},{5,7},{6,4},{7,5},{8,10},{9,11},{10,... | collective-permute-start | bytes 614408 | tf_op jit(solution)/shard_map/ppermute | solution.py:48
  24.5 0.0 collective-permute-done.6
  24.6 1.7 %collective-permute-start.7 = (bf16[4,8,3200]{2,1,0:T(8,128)(2,1)S(1)}, bf16[4,8,3200]{2,1,0:T(8,128)(2,1)S(1)}, u32[]{:S(2)}, u32[]{:S(2)}) collective-permute-start(bf16[4,8,3200]{2,1,0:T(8,128)(2,1)S(1)} %pad_maximum_fusion.2), channel_id=1, source_target_pairs={{0,4},{1,5},{2,6},{3,7},{4,0},{5,1},{6,2},{7,3},{8,12},{9,13},{10,... | collective-permute-start | bytes 614408 | tf_op jit(solution)/shard_map/ppermute | solution.py:48
  26.3 0.0 collective-permute-done.12
  26.3 0.1 collective-permute-start.13
  26.4 0.9 %collective-permute-done.3 = f32[8,1536]{1,0:T(8,128)S(1)} collective-permute-done((f32[8,1536]{1,0:T(8,128)S(1)}, f32[8,1536]{1,0:T(8,128)S(1)}, u32[]{:S(2)}, u32[]{:S(2)}) %collective-permute-start.3) | collective-permute-done | bytes 49184 | tf_op jit(solution)/shard_map/ppermute | solution.py:48
  27.3 0.1 collective-permute-start.4
  27.3 1.4 %collective-permute-done.16 = bf16[4,8,3200]{2,1,0:T(8,128)(2,1)S(1)} collective-permute-done((bf16[4,8,3200]{2,1,0:T(8,128)(2,1)S(1)}, bf16[4,8,3200]{2,1,0:T(8,128)(2,1)S(1)}, u32[]{:S(2)}, u32[]{:S(2)}) %collective-permute-start.16) | collective-permute-done | bytes 204832 | tf_op jit(solution)/shard_map/ppermute | solution.py:48
  28.8 0.1 pad_maximum_fusion.1
  28.8 0.1 collective-permute-start.17
  28.9 1.5 %collective-permute-done.7 = bf16[4,8,3200]{2,1,0:T(8,128)(2,1)S(1)} collective-permute-done((bf16[4,8,3200]{2,1,0:T(8,128)(2,1)S(1)}, bf16[4,8,3200]{2,1,0:T(8,128)(2,1)S(1)}, u32[]{:S(2)}, u32[]{:S(2)}) %collective-permute-start.7) | collective-permute-done | bytes 204832 | tf_op jit(solution)/shard_map/ppermute | solution.py:48
  30.4 0.1 pad_maximum_fusion
  30.5 0.1 collective-permute-start.8
  30.6 0.1 collective-permute-done.17
  30.6 0.0 slice-start
  30.7 0.0 slice-start.1
  30.7 0.0 collective-permute-done.13.other
  30.7 0.0 copy-done.3
  30.7 0.0 copy-done.1
  30.7 0.0 copy-done.4
  30.7 5.4 %correlate.2.rest_0_ = f32[128,1024]{1,0:T(8,128)S(1)} custom-call(s32[8]{0:T(128)S(1)} %copy-done.3, bf16[8,8,6144]{2,1,0:T(8,128)(2,1)S(1)} %copy-done.1, f32[8,1536]{1,0:T(8,128)S(1)} %add.31.own, f32[8,1536]{1,0:T(8,128)S(1)} %collective-permute-done.13.other, bf16[16,8,3200]{2,1,0:T(8,128)(2,1)S(1)} %constant_dynamic-update-slice_fusion.5.got, ...), custom_call_target="tpu_custom_call" | custom-call | flops 5000000000 | bytes 10485760 | tf_op jit(solution)/shard_map/correlate/pallas_call | solution.py:237
  36.1 0.0 collective-permute-done.8
  36.2 0.0 collective-permute-done.4.other
  36.2 0.0 slice-done
  36.2 0.0 slice-done.1
  36.2 6.2 %correlate.3 = f32[16,8,1024]{2,1,0:T(8,128)} custom-call(s32[8]{0:T(128)S(1)} %copy-done.3, bf16[8,8,6144]{2,1,0:T(8,128)(2,1)S(1)} %copy-done.1, f32[8,1536]{1,0:T(8,128)S(1)} %add.27.own, f32[8,1536]{1,0:T(8,128)S(1)} %collective-permute-done.4.other, bf16[16,8,3200]{2,1,0:T(8,128)(2,1)S(1)} %constant_dynamic-update-slice_fusion.got, ...), custom_call_target="tpu_custom_call" | custom-call | flops 5000000000 | bytes 10485760 | tf_op jit(solution)/shard_map/correlate/pallas_call | solution.py:237
  (22 shorter events, 0.3 us)
Async XLA Ops:
  0.0 30.7 %copy-start.3 = (s32[8]{0:T(128)S(1)}, s32[8]{0:T(128)}, u32[]{:S(2)}) copy-start(s32[8]{0:T(128)} %bad_flag.5) | copy-start | bytes 100
  1.3 1.1 %copy-start = (bf16[8,8,6144]{2,1,0:T(8,128)(2,1)S(1)}, bf16[8,8,6144]{2,1,0:T(8,128)(2,1)}, u32[]{:S(2)}) copy-start(bf16[8,8,6144]{2,1,0:T(8,128)(2,1)} %spectra.5) | copy-start | bytes 2359300
  2.4 0.7 %copy-start.2 = (s32[8]{0:T(128)S(1)}, s32[8]{0:T(128)}, u32[]{:S(2)}) copy-start(s32[8]{0:T(128)} %bad_flag.5) | copy-start | bytes 100
  3.1 27.6 %copy-start.1 = (bf16[8,8,6144]{2,1,0:T(8,128)(2,1)S(1)}, bf16[8,8,6144]{2,1,0:T(8,128)(2,1)}, u32[]{:S(2)}) copy-start(bf16[8,8,6144]{2,1,0:T(8,128)(2,1)} %spectra.5) | copy-start | bytes 2359300
  3.1 27.6 %copy-start.4 = (bf16[3072,1024]{1,0:T(8,128)(2,1)S(1)}, bf16[3072,1024]{1,0:T(8,128)(2,1)}, u32[]{:S(2)}) copy-start(bf16[3072,1024]{1,0:T(8,128)(2,1)} %constant.4.clone.table) | copy-start | bytes 18874372
  3.8 8.1 %collective-permute-start.14 = (bf16[1,8,3200]{2,1,0:T(8,128)(2,1)S(1)}, bf16[1,8,3200]{2,1,0:T(8,128)(2,1)S(1)}, u32[]{:S(2)}, u32[]{:S(2)}) collective-permute-start(bf16[1,8,3200]{2,1,0:T(8,128)(2,1)S(1)} %get-tuple-element.16), channel_id=1, source_target_pairs={{0,8},{1,9},{2,10},{3,11},{4,12},{5,13},{6,14},{7,15},{8,0},{9,1},... | collective-permute-start | bytes 153608 | tf_op jit(solution)/shard_map/ppermute | solution.py:48
  7.9 1.8 %collective-permute-start.9 = (f32[8,1536]{1,0:T(8,128)S(1)}, f32[8,1536]{1,0:T(8,128)S(1)}, u32[]{:S(2)}, u32[]{:S(2)}) collective-permute-start(f32[8,1536]{1,0:T(8,128)S(1)} %get-tuple-element.15), channel_id=1, source_target_pairs={{0,1},{1,0},{2,3},{3,2},{4,5},{5,4},{6,7},{7,6},{8,9},{9,8},{10,11... | collective-permute-start | bytes 147464 | tf_op jit(solution)/shard_map/ppermute | solution.py:48
  7.9 5.6 %collective-permute-start.5 = (bf16[1,8,3200]{2,1,0:T(8,128)(2,1)S(1)}, bf16[1,8,3200]{2,1,0:T(8,128)(2,1)S(1)}, u32[]{:S(2)}, u32[]{:S(2)}) collective-permute-start(bf16[1,8,3200]{2,1,0:T(8,128)(2,1)S(1)} %get-tuple-element.13), channel_id=1, source_target_pairs={{0,2},{1,3},{2,0},{3,1},{4,6},{5,7},{6,4},{7,5},{8,10},{9,11},{10,... | collective-permute-start | bytes 153608 | tf_op jit(solution)/shard_map/ppermute | solution.py:48
  9.5 1.3 %collective-permute-start = (f32[8,1536]{1,0:T(8,128)S(1)}, f32[8,1536]{1,0:T(8,128)S(1)}, u32[]{:S(2)}, u32[]{:S(2)}) collective-permute-start(f32[8,1536]{1,0:T(8,128)S(1)} %get-tuple-element.12), channel_id=1, source_target_pairs={{0,1},{1,0},{2,3},{3,2},{4,5},{5,4},{6,7},{7,6},{8,9},{9,8},{10,11... | collective-permute-start | bytes 147464 | tf_op jit(solution)/shard_map/ppermute | solution.py:48
  9.7 5.4 %collective-permute-start.10 = (f32[8,1536]{1,0:T(8,128)S(1)}, f32[8,1536]{1,0:T(8,128)S(1)}, u32[]{:S(2)}, u32[]{:S(2)}) collective-permute-start(f32[8,1536]{1,0:T(8,128)S(1)} %add.28), channel_id=1, source_target_pairs={{0,2},{1,3},{2,0},{3,1},{4,6},{5,7},{6,4},{7,5},{8,10},{9,11},{10,... | collective-permute-start | bytes 147464 | tf_op jit(solution)/shard_map/ppermute | solution.py:48
  10.8 5.1 %collective-permute-start.1 = (f32[8,1536]{1,0:T(8,128)S(1)}, f32[8,1536]{1,0:T(8,128)S(1)}, u32[]{:S(2)}, u32[]{:S(2)}) collective-permute-start(f32[8,1536]{1,0:T(8,128)S(1)} %add.24), channel_id=1, source_target_pairs={{0,2},{1,3},{2,0},{3,1},{4,6},{5,7},{6,4},{7,5},{8,10},{9,11},{10,... | collective-permute-start | bytes 147464 | tf_op jit(solution)/shard_map/ppermute | solution.py:48
  11.9 11.0 %collective-permute-start.15 = (bf16[2,8,3200]{2,1,0:T(8,128)(2,1)S(1)}, bf16[2,8,3200]{2,1,0:T(8,128)(2,1)S(1)}, u32[]{:S(2)}, u32[]{:S(2)}) collective-permute-start(bf16[2,8,3200]{2,1,0:T(8,128)(2,1)S(1)} %pad_maximum_fusion.5), channel_id=1, source_target_pairs={{0,4},{1,5},{2,6},{3,7},{4,0},{5,1},{6,2},{7,3},{8,12},{9,13},{10,... | collective-permute-start | bytes 307208 | tf_op jit(solution)/shard_map/ppermute | solution.py:48
  13.6 11.0 %collective-permute-start.6 = (bf16[2,8,3200]{2,1,0:T(8,128)(2,1)S(1)}, bf16[2,8,3200]{2,1,0:T(8,128)(2,1)S(1)}, u32[]{:S(2)}, u32[]{:S(2)}) collective-permute-start(bf16[2,8,3200]{2,1,0:T(8,128)(2,1)S(1)} %pad_maximum_fusion.4), channel_id=1, source_target_pairs={{0,8},{1,9},{2,10},{3,11},{4,12},{5,13},{6,14},{7,15},{8,0},{9,1},... | collective-permute-start | bytes 307208 | tf_op jit(solution)/shard_map/ppermute | solution.py:48
  15.2 4.7 %collective-permute-start.11 = (f32[8,1536]{1,0:T(8,128)S(1)}, f32[8,1536]{1,0:T(8,128)S(1)}, u32[]{:S(2)}, u32[]{:S(2)}) collective-permute-start(f32[8,1536]{1,0:T(8,128)S(1)} %add.29), channel_id=1, source_target_pairs={{0,4},{1,5},{2,6},{3,7},{4,0},{5,1},{6,2},{7,3},{8,12},{9,13},{10,... | collective-permute-start | bytes 147464 | tf_op jit(solution)/shard_map/ppermute | solution.py:48
  15.9 5.7 %collective-permute-start.2 = (f32[8,1536]{1,0:T(8,128)S(1)}, f32[8,1536]{1,0:T(8,128)S(1)}, u32[]{:S(2)}, u32[]{:S(2)}) collective-permute-start(f32[8,1536]{1,0:T(8,128)S(1)} %add.25), channel_id=1, source_target_pairs={{0,4},{1,5},{2,6},{3,7},{4,0},{5,1},{6,2},{7,3},{8,12},{9,13},{10,... | collective-permute-start | bytes 147464 | tf_op jit(solution)/shard_map/ppermute | solution.py:48
  19.8 6.4 %collective-permute-start.12 = (f32[8,1536]{1,0:T(8,128)S(1)}, f32[8,1536]{1,0:T(8,128)S(1)}, u32[]{:S(2)}, u32[]{:S(2)}) collective-permute-start(f32[8,1536]{1,0:T(8,128)S(1)} %add.30), channel_id=1, source_target_pairs={{0,8},{1,9},{2,10},{3,11},{4,12},{5,13},{6,14},{7,15},{8,0},{9,1},... | collective-permute-start | bytes 147464 | tf_op jit(solution)/shard_map/ppermute | solution.py:48
  21.6 5.7 %collective-permute-start.3 = (f32[8,1536]{1,0:T(8,128)S(1)}, f32[8,1536]{1,0:T(8,128)S(1)}, u32[]{:S(2)}, u32[]{:S(2)}) collective-permute-start(f32[8,1536]{1,0:T(8,128)S(1)} %add.26), channel_id=1, source_target_pairs={{0,8},{1,9},{2,10},{3,11},{4,12},{5,13},{6,14},{7,15},{8,0},{9,1},... | collective-permute-start | bytes 147464 | tf_op jit(solution)/shard_map/ppermute | solution.py:48
  23.0 5.8 %collective-permute-start.16 = (bf16[4,8,3200]{2,1,0:T(8,128)(2,1)S(1)}, bf16[4,8,3200]{2,1,0:T(8,128)(2,1)S(1)}, u32[]{:S(2)}, u32[]{:S(2)}) collective-permute-start(bf16[4,8,3200]{2,1,0:T(8,128)(2,1)S(1)} %pad_maximum_fusion.3), channel_id=1, source_target_pairs={{0,2},{1,3},{2,0},{3,1},{4,6},{5,7},{6,4},{7,5},{8,10},{9,11},{10,... | collective-permute-start | bytes 614408 | tf_op jit(solution)/shard_map/ppermute | solution.py:48
  24.6 5.8 %collective-permute-start.7 = (bf16[4,8,3200]{2,1,0:T(8,128)(2,1)S(1)}, bf16[4,8,3200]{2,1,0:T(8,128)(2,1)S(1)}, u32[]{:S(2)}, u32[]{:S(2)}) collective-permute-start(bf16[4,8,3200]{2,1,0:T(8,128)(2,1)S(1)} %pad_maximum_fusion.2), channel_id=1, source_target_pairs={{0,4},{1,5},{2,6},{3,7},{4,0},{5,1},{6,2},{7,3},{8,12},{9,13},{10,... | collective-permute-start | bytes 614408 | tf_op jit(solution)/shard_map/ppermute | solution.py:48
  26.3 4.4 %collective-permute-start.13 = (f32[8,1536]{1,0:T(8,128)S(1)}, f32[8,1536]{1,0:T(8,128)S(1)}, u32[]{:S(2)}, u32[]{:S(2)}) collective-permute-start(f32[8,1536]{1,0:T(8,128)S(1)} %add.31.own), channel_id=1, source_target_pairs={{0,1},{1,0},{2,3},{3,2},{4,5},{5,4},{6,7},{7,6},{8,9},{9,8},{10,11... | collective-permute-start | bytes 147464 | tf_op jit(solution)/shard_map/ppermute | solution.py:48
  27.3 8.9 %collective-permute-start.4 = (f32[8,1536]{1,0:T(8,128)S(1)}, f32[8,1536]{1,0:T(8,128)S(1)}, u32[]{:S(2)}, u32[]{:S(2)}) collective-permute-start(f32[8,1536]{1,0:T(8,128)S(1)} %add.27.own), channel_id=1, source_target_pairs={{0,1},{1,0},{2,3},{3,2},{4,5},{5,4},{6,7},{7,6},{8,9},{9,8},{10,11... | collective-permute-start | bytes 147464 | tf_op jit(solution)/shard_map/ppermute | solution.py:48
  28.8 1.8 %collective-permute-start.17 = (bf16[8,8,3200]{2,1,0:T(8,128)(2,1)S(1)}, bf16[8,8,3200]{2,1,0:T(8,128)(2,1)S(1)}, u32[]{:S(2)}, u32[]{:S(2)}) collective-permute-start(bf16[8,8,3200]{2,1,0:T(8,128)(2,1)S(1)} %pad_maximum_fusion.1), channel_id=1, source_target_pairs={{0,1},{1,0},{2,3},{3,2},{4,5},{5,4},{6,7},{7,6},{8,9},{9,8},{10,11... | collective-permute-start | bytes 1228808 | tf_op jit(solution)/shard_map/ppermute | solution.py:48
  30.5 5.7 %collective-permute-start.8 = (bf16[8,8,3200]{2,1,0:T(8,128)(2,1)S(1)}, bf16[8,8,3200]{2,1,0:T(8,128)(2,1)S(1)}, u32[]{:S(2)}, u32[]{:S(2)}) collective-permute-start(bf16[8,8,3200]{2,1,0:T(8,128)(2,1)S(1)} %pad_maximum_fusion), channel_id=1, source_target_pairs={{0,1},{1,0},{2,3},{3,2},{4,5},{5,4},{6,7},{7,6},{8,9},{9,8},{10,11... | collective-permute-start | bytes 1228808 | tf_op jit(solution)/shard_map/ppermute | solution.py:48
  30.6 5.5 %slice-start = ((s8[6291456]{0:T(1024)(128)(4,1)}), s8[4194304]{0:T(1024)(128)(4,1)S(1)}, s32[]{:S(2)}) async-start(s8[6291456]{0:T(1024)(128)(4,1)} %bitcast), calls=%async_computation | async-start | bytes 8388608
  30.7 5.5 %slice-start.1 = ((s8[6291456]{0:T(1024)(128)(4,1)}), s8[2097152]{0:T(1024)(128)(4,1)S(1)}, s32[]{:S(2)}) async-start(s8[6291456]{0:T(1024)(128)(4,1)} %bitcast), calls=%async_computation.1 | async-start | bytes 4194304

commit v4 on v3

--- a/solution.py
+++ b/solution.py
@@ -31,9 +31,9 @@
 
 def orders(owners):
     bits = [1 << i for i in range(owners.bit_length() - 1)]
-    far = bits[:0:-1]
-    other = far[-1:] + far[:-1]
-    return (bits[1:], bits[1:]), (far + [1], other + [1])
+    near, far = bits[1:], bits[:0:-1]
+    totals = near[1::-1] + near[2:], near[-1:] + near[:-1]
+    return totals, (far + [1], far[-1:] + far[:-1] + [1])
 
 
 def masks(order):
@@ -48,36 +48,43 @@
     return lax.ppermute(value, "chan", [(i, i ^ bit) for i in range(owners)])
 
 
-def prepare(bins, source_pick, lag_start, bad_flag, spectra, *rest):
-    outs, (held, flags, sems, flag_sem) = rest[:6], rest[6:]
-    core = lax.axis_index("chan") & 1
+def pick_rows(bins, source_pick, lag_start, bad_flag, spectra, first, second, flags, sems):
+    half = bins // 2
     pick, lag = source_pick[0], lag_start[0]
-    half = bins // 2
-    copies = []
-    for h in range(2):
+    copies = [pltpu.make_async_copy(bad_flag, flags, sems.at[4])]
+    for h, rows in enumerate((first, second)):
         for part in range(2):
-            src = pl.ds(part * bins + h * half, half)
-            slot = 2 * h + part
-            copies.append(pltpu.make_async_copy(spectra.at[:, :, src], held.at[slot], sems.at[slot]))
-    flag_copy = pltpu.make_async_copy(bad_flag, flags, flag_sem)
-    flag_copy.start()
+            copies.append(
+                pltpu.make_async_copy(
+                    spectra.at[pick, :, pl.ds(part * bins + h * half, half)],
+                    rows.at[0, :, pl.ds(part * half, half)],
+                    sems.at[2 * h + part],
+                )
+            )
     for copy in copies:
         copy.start()
     row = lax.broadcasted_iota(jnp.int32, (spectra.shape[1], LANES), 0)
     high = lax.shift_right_arithmetic(lag, 5)
     low = lag - high * 32
-    flag_copy.wait()
+    copies[0].wait()
     keep = (1 - flags[pick]).astype(f32)
     extra = jnp.where(row == 0, high.astype(f32), jnp.where(row == 1, low.astype(f32), keep))
+    for rows in (first, second):
+        rows[0, :, pl.ds(bins, LANES)] = extra.astype(bf16)
+    for copy in copies[1:]:
+        copy.wait()
+
+
+def add_channels(bins, spectra, *outs):
+    core = lax.axis_index("chan") & 1
+    half = bins // 2
     for h in range(2):
-        own, other, rows = outs[3 * h : 3 * h + 3]
-        rows[0, :, pl.ds(bins, LANES)] = extra.astype(bf16)
+        own, other = outs[2 * h : 2 * h + 2]
         for part in range(2):
-            slot = 2 * h + part
-            copies[slot].wait()
-            total = held[slot, 0].astype(f32)
-            for r in range(1, held.shape[1]):
-                total = total + held[slot, r].astype(f32)
+            src = pl.ds(part * bins + h * half, half)
+            total = spectra[0, :, src].astype(f32)
+            for r in range(1, spectra.shape[0]):
+                total = total + spectra[r, :, src].astype(f32)
 
             @pl.when(core == part)
             def _():
@@ -86,8 +93,6 @@
             @pl.when(core != part)
             def _():
                 other[...] = total
-
-            rows[0, :, pl.ds(part * half, half)] = held[slot, pick]
 
 
 def cos_sin(turns):
@@ -125,6 +130,7 @@
     keep = [(1 - bad_flag[r]).astype(f32) for r in range(receivers)]
     tail = got[:, :, pl.ds(bins, LANES)].astype(f32)
     lags = tail[:, 0, :] * 32.0 + tail[:, 1, :]
+    kept = tail[:, 2, :]
 
     def scales(power):
         count = power.shape[0]
@@ -155,14 +161,14 @@
             rec[0, r] = rounded(x_re[r] * factor)
             rec[1, r] = rounded(x_im[r] * factor)
         k = (lane + (h * half + 1) + c * LANES).astype(f32)
-        ang[0], ang[1] = cos_sin(lags * k)
+        cosine, sine = cos_sin(lags * k)
+        ang[0], ang[1] = cosine * kept, sine * kept
         g_re = got[:, :, re_at].astype(f32) - m_re[None]
         g_im = got[:, :, im_at].astype(f32) - m_im[None]
         scale = scales(g_re * g_re + g_im * g_im)
         for i in range(sources):
-            factor = scale[i] * jnp.broadcast_to(tail[i, 2:3, :], (windows, LANES))
-            w_re = rounded(g_re[i] * factor)
-            w_im = rounded(g_im[i] * factor)
+            w_re = rounded(g_re[i] * scale[i])
+            w_im = rounded(g_im[i] * scale[i])
             cosine = ang[0, pl.ds(i, windows, stride=0), :]
             sine = ang[1, pl.ds(i, windows, stride=0), :]
             src[0, i] = rounded(w_re * cosine + w_im * sine)
@@ -205,25 +211,34 @@
     half = bins // 2
     flat = jax.ShapeDtypeStruct((windows, half), f32)
     rows = jax.ShapeDtypeStruct((1, windows, bins + LANES), bf16)
-    ready = pl.pallas_call(
-        functools.partial(prepare, bins),
-        out_shape=(flat, flat, rows) * 2,
+    first, second = pl.pallas_call(
+        functools.partial(pick_rows, bins),
+        out_shape=(rows, rows),
         in_specs=[SMEM, SMEM, HBM, HBM],
-        out_specs=(VMEM,) * 6,
-        scratch_shapes=[
-            pltpu.VMEM((4, receivers, windows, half), bf16),
-            pltpu.SMEM((receivers,), jnp.int32),
-            pltpu.SemaphoreType.DMA((4,)),
-            pltpu.SemaphoreType.DMA(()),
-        ],
-        compiler_params=pltpu.CompilerParams(vmem_limit_bytes=16 << 20),
-        name="prepare",
-    )(source_pick, lag_start, bad_flag, spectra)
+        out_specs=(VMEM, VMEM),
+        scratch_shapes=[pltpu.SMEM((receivers,), jnp.int32), pltpu.SemaphoreType.DMA((5,))],
+        compiler_params=pltpu.CompilerParams(vmem_limit_bytes=8 << 20),
+        name="pick_rows",
+    )(
+        source_pick,
+        lag_start,
+        pltpu.with_memory_space_constraint(bad_flag, pltpu.HBM),
+        pltpu.with_memory_space_constraint(spectra, pltpu.HBM),
+    )
+    sums = pl.pallas_call(
+        functools.partial(add_channels, bins),
+        out_shape=(flat,) * 4,
+        in_specs=[VMEM],
+        out_specs=(VMEM,) * 4,
+        compiler_params=pltpu.CompilerParams(vmem_limit_bytes=8 << 20),
+        name="add_channels",
+    )(spectra)
     total_order, row_order = orders(owners)
     table = lag_table(bins)
     totals, gots = [], []
     for h in range(2):
-        own, other, got = ready[3 * h : 3 * h + 3]
+        own, other = sums[2 * h : 2 * h + 2]
+        got = (first, second)[h]
         total = own + swap(other, 1)
         for bit in total_order[h]:
             total = total + swap(total, bit)

time: 42.5 us -> 41.4 us (0.974)
  starting transfers between devices: 19.9 us -> 16.9 us
  waiting for transfers between devices: 6.39 us -> 8.68 us
  local copies, waits for them, and re-layouts: 1.98 us -> 1.33 us
    ppermute x18, starting transfers between devices: 19.9 us -> 16.9 us  [swap(): return lax.ppermute(value, 'chan', [(i, i ^ bit) for i in range(owners)])]
    ppermute x18, waiting for transfers between devices: 6.39 us -> 8.68 us  [swap(): return lax.ppermute(value, 'chan', [(i, i ^ bit) for i in range(owners)])]
    unnamed x21 -> x19, local copies, waits for them, and re-layouts: 1.9 us -> 1.26 us
    pallas_call x1 -> x2, Pallas kernels: 0.72 us -> 0.95 us  [the longest x1 0.84 us: shards(): pl.pallas_call(functools.partial(pick_rows, bins), out_shape=(rows, rows)...]
  transfers between devices with their start and end apart: 18 -> 18, of which waited for: 5 -> 7; matrix products, arithmetic and copies ran while one was open for 1% -> 1% of each run, Pallas kernels for 13% -> 13%
where the time goes in v4:
time: 41.4 us; the launch traced here: 41.2 us
  starting transfers between devices  16.9 us (41%)
  Pallas kernels  12.3 us (30%)
  waiting for transfers between devices  8.68 us (21%)
  between operations  1.61 us (4%)
  local copies, waits for them, and re-layouts  1.33 us (3%)
    ppermute x18, starting transfers between devices, swap(): return lax.ppermute(value, 'chan', [(i, i ^ bit) for i in range(owners)])  16.9 us
    pallas_call x2, Pallas kernels, shards(): pl.pallas_call(functools.partial(correlate, h, bins, row_order[h], row_or...  11.4 us
    ppermute x18, waiting for transfers between devices, swap(): return lax.ppermute(value, 'chan', [(i, i ^ bit) for i in range(owners)])  8.68 us
    unnamed x19, local copies, waits for them, and re-layouts  1.26 us
    pallas_call x1, Pallas kernels, shards(): pl.pallas_call(functools.partial(pick_rows, bins), out_shape=(rows, rows)...  0.84 us
  transfers between devices with their start and end apart: 18, of which 7 were waited for; matrix products, arithmetic and copies ran while one was open for 1% of the time, Pallas kernels for 13%

profile of v4, /device:TPU:0, one launch (start us, length us, event | category | flops | bytes accessed | tf_op | source)
XLA Modules:
  0.0 41.2 jit_solution(2459264408288195038)
XLA Ops:
  0.0 0.0 copy-start.1
  0.0 0.0 copy-start.2
  1.4 0.8 %pick_rows.1 = (bf16[1,8,3200]{2,1,0:T(8,128)(2,1)S(1)}, bf16[1,8,3200]{2,1,0:T(8,128)(2,1)S(1)}) custom-call(s32[1]{0:T(128)S(6)} %copy.15.source_pick, s32[1]{0:T(128)S(6)} %copy.16.lag_start, s32[8]{0:T(128)} %bad_flag.5, bf16[8,8,6144]{2,1,0:T(8,128)(2,1)} %spectra.7), custom_call_target="tpu_custom_call" | custom-call | tf_op jit(solution)/shard_map/pick_rows/pallas_call | solution.py:214
  2.2 4.1 %collective-permute-start.14 = (bf16[1,8,3200]{2,1,0:T(8,128)(2,1)S(1)}, bf16[1,8,3200]{2,1,0:T(8,128)(2,1)S(1)}, u32[]{:S(2)}, u32[]{:S(2)}) collective-permute-start(bf16[1,8,3200]{2,1,0:T(8,128)(2,1)S(1)} %get-tuple-element.16), channel_id=1, source_target_pairs={{0,8},{1,9},{2,10},{3,11},{4,12},{5,13},{6,14},{7,15},{8,0},{9,1},... | collective-permute-start | bytes 153608 | tf_op jit(solution)/shard_map/ppermute | solution.py:48
  6.3 0.0 copy-start
  6.3 1.1 %copy-done = bf16[8,8,6144]{2,1,0:T(8,128)(2,1)S(1)} copy-done((bf16[8,8,6144]{2,1,0:T(8,128)(2,1)S(1)}, bf16[8,8,6144]{2,1,0:T(8,128)(2,1)}, u32[]{:S(2)}) %copy-start) | copy-done | bytes 786456
  7.5 0.0 copy-start.3
  7.5 0.1 add_channels.1
  7.6 0.1 collective-permute-start.9
  7.7 1.6 %collective-permute-start.5 = (bf16[1,8,3200]{2,1,0:T(8,128)(2,1)S(1)}, bf16[1,8,3200]{2,1,0:T(8,128)(2,1)S(1)}, u32[]{:S(2)}, u32[]{:S(2)}) collective-permute-start(bf16[1,8,3200]{2,1,0:T(8,128)(2,1)S(1)} %get-tuple-element.13), channel_id=1, source_target_pairs={{0,2},{1,3},{2,0},{3,1},{4,6},{5,7},{6,4},{7,5},{8,10},{9,11},{10,... | collective-permute-start | bytes 153608 | tf_op jit(solution)/shard_map/ppermute | solution.py:48
  9.2 0.2 collective-permute-start
  9.4 0.0 collective-permute-done.9
  9.4 1.6 %collective-permute-start.10 = (f32[8,1536]{1,0:T(8,128)S(1)}, f32[8,1536]{1,0:T(8,128)S(1)}, u32[]{:S(2)}, u32[]{:S(2)}) collective-permute-start(f32[8,1536]{1,0:T(8,128)S(1)} %add.28), channel_id=1, source_target_pairs={{0,4},{1,5},{2,6},{3,7},{4,0},{5,1},{6,2},{7,3},{8,12},{9,13},{10,... | collective-permute-start | bytes 147464 | tf_op jit(solution)/shard_map/ppermute | solution.py:48
  11.1 0.0 collective-permute-done
  11.1 0.4 collective-permute-start.1
  11.5 0.0 collective-permute-done.14
  11.5 1.0 %collective-permute-start.15 = (bf16[2,8,3200]{2,1,0:T(8,128)(2,1)S(1)}, bf16[2,8,3200]{2,1,0:T(8,128)(2,1)S(1)}, u32[]{:S(2)}, u32[]{:S(2)}) collective-permute-start(bf16[2,8,3200]{2,1,0:T(8,128)(2,1)S(1)} %pad_maximum_fusion.5), channel_id=1, source_target_pairs={{0,4},{1,5},{2,6},{3,7},{4,0},{5,1},{6,2},{7,3},{8,12},{9,13},{10,... | collective-permute-start | bytes 307208 | tf_op jit(solution)/shard_map/ppermute | solution.py:48
  12.5 0.0 collective-permute-done.5
  12.6 2.7 %collective-permute-start.6 = (bf16[2,8,3200]{2,1,0:T(8,128)(2,1)S(1)}, bf16[2,8,3200]{2,1,0:T(8,128)(2,1)S(1)}, u32[]{:S(2)}, u32[]{:S(2)}) collective-permute-start(bf16[2,8,3200]{2,1,0:T(8,128)(2,1)S(1)} %pad_maximum_fusion.4), channel_id=1, source_target_pairs={{0,8},{1,9},{2,10},{3,11},{4,12},{5,13},{6,14},{7,15},{8,0},{9,1},... | collective-permute-start | bytes 307208 | tf_op jit(solution)/shard_map/ppermute | solution.py:48
  15.2 0.0 collective-permute-done.10
  15.3 0.6 %collective-permute-start.11 = (f32[8,1536]{1,0:T(8,128)S(1)}, f32[8,1536]{1,0:T(8,128)S(1)}, u32[]{:S(2)}, u32[]{:S(2)}) collective-permute-start(f32[8,1536]{1,0:T(8,128)S(1)} %add.29), channel_id=1, source_target_pairs={{0,2},{1,3},{2,0},{3,1},{4,6},{5,7},{6,4},{7,5},{8,10},{9,11},{10,... | collective-permute-start | bytes 147464 | tf_op jit(solution)/shard_map/ppermute | solution.py:48
  15.8 1.6 %collective-permute-done.1 = f32[8,1536]{1,0:T(8,128)S(1)} collective-permute-done((f32[8,1536]{1,0:T(8,128)S(1)}, f32[8,1536]{1,0:T(8,128)S(1)}, u32[]{:S(2)}, u32[]{:S(2)}) %collective-permute-start.1) | collective-permute-done | bytes 49184 | tf_op jit(solution)/shard_map/ppermute | solution.py:48
  17.4 0.8 %collective-permute-start.2 = (f32[8,1536]{1,0:T(8,128)S(1)}, f32[8,1536]{1,0:T(8,128)S(1)}, u32[]{:S(2)}, u32[]{:S(2)}) collective-permute-start(f32[8,1536]{1,0:T(8,128)S(1)} %add.25), channel_id=1, source_target_pairs={{0,2},{1,3},{2,0},{3,1},{4,6},{5,7},{6,4},{7,5},{8,10},{9,11},{10,... | collective-permute-start | bytes 147464 | tf_op jit(solution)/shard_map/ppermute | solution.py:48
  18.2 1.2 %collective-permute-done.11 = f32[8,1536]{1,0:T(8,128)S(1)} collective-permute-done((f32[8,1536]{1,0:T(8,128)S(1)}, f32[8,1536]{1,0:T(8,128)S(1)}, u32[]{:S(2)}, u32[]{:S(2)}) %collective-permute-start.11) | collective-permute-done | bytes 49184 | tf_op jit(solution)/shard_map/ppermute | solution.py:48
  19.4 0.6 %collective-permute-start.12 = (f32[8,1536]{1,0:T(8,128)S(1)}, f32[8,1536]{1,0:T(8,128)S(1)}, u32[]{:S(2)}, u32[]{:S(2)}) collective-permute-start(f32[8,1536]{1,0:T(8,128)S(1)} %add.30), channel_id=1, source_target_pairs={{0,8},{1,9},{2,10},{3,11},{4,12},{5,13},{6,14},{7,15},{8,0},{9,1},... | collective-permute-start | bytes 147464 | tf_op jit(solution)/shard_map/ppermute | solution.py:48
  20.1 1.5 %collective-permute-done.2 = f32[8,1536]{1,0:T(8,128)S(1)} collective-permute-done((f32[8,1536]{1,0:T(8,128)S(1)}, f32[8,1536]{1,0:T(8,128)S(1)}, u32[]{:S(2)}, u32[]{:S(2)}) %collective-permute-start.2) | collective-permute-done | bytes 49184 | tf_op jit(solution)/shard_map/ppermute | solution.py:48
  21.6 0.3 collective-permute-start.3
  21.9 0.0 collective-permute-done.15
  21.9 0.9 %collective-permute-start.16 = (bf16[4,8,3200]{2,1,0:T(8,128)(2,1)S(1)}, bf16[4,8,3200]{2,1,0:T(8,128)(2,1)S(1)}, u32[]{:S(2)}, u32[]{:S(2)}) collective-permute-start(bf16[4,8,3200]{2,1,0:T(8,128)(2,1)S(1)} %pad_maximum_fusion.3), channel_id=1, source_target_pairs={{0,2},{1,3},{2,0},{3,1},{4,6},{5,7},{6,4},{7,5},{8,10},{9,11},{10,... | collective-permute-start | bytes 614408 | tf_op jit(solution)/shard_map/ppermute | solution.py:48
  22.8 0.0 collective-permute-done.6
  22.8 1.8 %collective-permute-start.7 = (bf16[4,8,3200]{2,1,0:T(8,128)(2,1)S(1)}, bf16[4,8,3200]{2,1,0:T(8,128)(2,1)S(1)}, u32[]{:S(2)}, u32[]{:S(2)}) collective-permute-start(bf16[4,8,3200]{2,1,0:T(8,128)(2,1)S(1)} %pad_maximum_fusion.2), channel_id=1, source_target_pairs={{0,4},{1,5},{2,6},{3,7},{4,0},{5,1},{6,2},{7,3},{8,12},{9,13},{10,... | collective-permute-start | bytes 614408 | tf_op jit(solution)/shard_map/ppermute | solution.py:48
  24.6 0.0 collective-permute-done.12
  24.7 0.1 collective-permute-start.13
  24.7 1.3 %collective-permute-done.3 = f32[8,1536]{1,0:T(8,128)S(1)} collective-permute-done((f32[8,1536]{1,0:T(8,128)S(1)}, f32[8,1536]{1,0:T(8,128)S(1)}, u32[]{:S(2)}, u32[]{:S(2)}) %collective-permute-start.3) | collective-permute-done | bytes 49184 | tf_op jit(solution)/shard_map/ppermute | solution.py:48
  26.0 0.1 collective-permute-start.4
  26.1 1.6 %collective-permute-done.16 = bf16[4,8,3200]{2,1,0:T(8,128)(2,1)S(1)} collective-permute-done((bf16[4,8,3200]{2,1,0:T(8,128)(2,1)S(1)}, bf16[4,8,3200]{2,1,0:T(8,128)(2,1)S(1)}, u32[]{:S(2)}, u32[]{:S(2)}) %collective-permute-start.16) | collective-permute-done | bytes 204832 | tf_op jit(solution)/shard_map/ppermute | solution.py:48
  27.7 0.1 pad_maximum_fusion.1
  27.8 0.1 collective-permute-start.17
  27.9 0.8 %collective-permute-done.7 = bf16[4,8,3200]{2,1,0:T(8,128)(2,1)S(1)} collective-permute-done((bf16[4,8,3200]{2,1,0:T(8,128)(2,1)S(1)}, bf16[4,8,3200]{2,1,0:T(8,128)(2,1)S(1)}, u32[]{:S(2)}, u32[]{:S(2)}) %collective-permute-start.7) | collective-permute-done | bytes 204832 | tf_op jit(solution)/shard_map/ppermute | solution.py:48
  28.6 0.1 pad_maximum_fusion
  28.7 0.1 collective-permute-start.8
  28.8 0.8 %collective-permute-done.17 = bf16[8,8,3200]{2,1,0:T(8,128)(2,1)S(1)} collective-permute-done((bf16[8,8,3200]{2,1,0:T(8,128)(2,1)S(1)}, bf16[8,8,3200]{2,1,0:T(8,128)(2,1)S(1)}, u32[]{:S(2)}, u32[]{:S(2)}) %collective-permute-start.17) | collective-permute-done | bytes 409632 | tf_op jit(solution)/shard_map/ppermute | solution.py:48
  29.6 0.0 slice-start
  29.6 0.0 slice-start.1
  29.6 0.0 collective-permute-done.13.other
  29.7 0.0 copy-done.1
  29.7 0.0 copy-done.2
  29.7 0.0 copy-done.3
  29.7 5.3 %correlate.2.rest_0_ = f32[128,1024]{1,0:T(8,128)S(1)} custom-call(s32[8]{0:T(128)S(1)} %copy-done.2, bf16[8,8,6144]{2,1,0:T(8,128)(2,1)S(1)} %copy-done.1, f32[8,1536]{1,0:T(8,128)S(1)} %add.31.own, f32[8,1536]{1,0:T(8,128)S(1)} %collective-permute-done.13.other, bf16[16,8,3200]{2,1,0:T(8,128)(2,1)S(1)} %constant_dynamic-update-slice_fusion.5.got, ...), custom_call_target="tpu_custom_call" | custom-call | flops 5000000000 | bytes 10485760 | tf_op jit(solution)/shard_map/correlate/pallas_call | solution.py:252
  35.0 0.0 collective-permute-done.8
  35.0 0.0 collective-permute-done.4.other
  35.0 0.0 slice-done
  35.1 0.0 slice-done.1
  35.1 6.1 %correlate.3 = f32[16,8,1024]{2,1,0:T(8,128)} custom-call(s32[8]{0:T(128)S(1)} %copy-done.2, bf16[8,8,6144]{2,1,0:T(8,128)(2,1)S(1)} %copy-done.1, f32[8,1536]{1,0:T(8,128)S(1)} %add.27.own, f32[8,1536]{1,0:T(8,128)S(1)} %collective-permute-done.4.other, bf16[16,8,3200]{2,1,0:T(8,128)(2,1)S(1)} %constant_dynamic-update-slice_fusion.got, ...), custom_call_target="tpu_custom_call" | custom-call | flops 5000000000 | bytes 10485760 | tf_op jit(solution)/shard_map/correlate/pallas_call | solution.py:252
  (22 shorter events, 0.3 us)
Async XLA Ops:
  0.0 29.7 %copy-start.1 = (bf16[8,8,6144]{2,1,0:T(8,128)(2,1)S(1)}, bf16[8,8,6144]{2,1,0:T(8,128)(2,1)}, u32[]{:S(2)}) copy-start(bf16[8,8,6144]{2,1,0:T(8,128)(2,1)} %spectra.7) | copy-start | bytes 2359300
  0.0 29.7 %copy-start.2 = (s32[8]{0:T(128)S(1)}, s32[8]{0:T(128)}, u32[]{:S(2)}) copy-start(s32[8]{0:T(128)} %bad_flag.5) | copy-start | bytes 100
  2.2 9.3 %collective-permute-start.14 = (bf16[1,8,3200]{2,1,0:T(8,128)(2,1)S(1)}, bf16[1,8,3200]{2,1,0:T(8,128)(2,1)S(1)}, u32[]{:S(2)}, u32[]{:S(2)}) collective-permute-start(bf16[1,8,3200]{2,1,0:T(8,128)(2,1)S(1)} %get-tuple-element.16), channel_id=1, source_target_pairs={{0,8},{1,9},{2,10},{3,11},{4,12},{5,13},{6,14},{7,15},{8,0},{9,1},... | collective-permute-start | bytes 153608 | tf_op jit(solution)/shard_map/ppermute | solution.py:48
  6.3 1.1 %copy-start = (bf16[8,8,6144]{2,1,0:T(8,128)(2,1)S(1)}, bf16[8,8,6144]{2,1,0:T(8,128)(2,1)}, u32[]{:S(2)}) copy-start(bf16[8,8,6144]{2,1,0:T(8,128)(2,1)} %spectra.7) | copy-start | bytes 2359300
  7.5 22.2 %copy-start.3 = (bf16[3072,1024]{1,0:T(8,128)(2,1)S(1)}, bf16[3072,1024]{1,0:T(8,128)(2,1)}, u32[]{:S(2)}) copy-start(bf16[3072,1024]{1,0:T(8,128)(2,1)} %constant.4.clone.table) | copy-start | bytes 18874372
  7.6 1.8 %collective-permute-start.9 = (f32[8,1536]{1,0:T(8,128)S(1)}, f32[8,1536]{1,0:T(8,128)S(1)}, u32[]{:S(2)}, u32[]{:S(2)}) collective-permute-start(f32[8,1536]{1,0:T(8,128)S(1)} %get-tuple-element.15), channel_id=1, source_target_pairs={{0,1},{1,0},{2,3},{3,2},{4,5},{5,4},{6,7},{7,6},{8,9},{9,8},{10,11... | collective-permute-start | bytes 147464 | tf_op jit(solution)/shard_map/ppermute | solution.py:48
  7.7 4.9 %collective-permute-start.5 = (bf16[1,8,3200]{2,1,0:T(8,128)(2,1)S(1)}, bf16[1,8,3200]{2,1,0:T(8,128)(2,1)S(1)}, u32[]{:S(2)}, u32[]{:S(2)}) collective-permute-start(bf16[1,8,3200]{2,1,0:T(8,128)(2,1)S(1)} %get-tuple-element.13), channel_id=1, source_target_pairs={{0,2},{1,3},{2,0},{3,1},{4,6},{5,7},{6,4},{7,5},{8,10},{9,11},{10,... | collective-permute-start | bytes 153608 | tf_op jit(solution)/shard_map/ppermute | solution.py:48
  9.2 1.8 %collective-permute-start = (f32[8,1536]{1,0:T(8,128)S(1)}, f32[8,1536]{1,0:T(8,128)S(1)}, u32[]{:S(2)}, u32[]{:S(2)}) collective-permute-start(f32[8,1536]{1,0:T(8,128)S(1)} %get-tuple-element.12), channel_id=1, source_target_pairs={{0,1},{1,0},{2,3},{3,2},{4,5},{5,4},{6,7},{7,6},{8,9},{9,8},{10,11... | collective-permute-start | bytes 147464 | tf_op jit(solution)/shard_map/ppermute | solution.py:48
  9.4 5.8 %collective-permute-start.10 = (f32[8,1536]{1,0:T(8,128)S(1)}, f32[8,1536]{1,0:T(8,128)S(1)}, u32[]{:S(2)}, u32[]{:S(2)}) collective-permute-start(f32[8,1536]{1,0:T(8,128)S(1)} %add.28), channel_id=1, source_target_pairs={{0,4},{1,5},{2,6},{3,7},{4,0},{5,1},{6,2},{7,3},{8,12},{9,13},{10,... | collective-permute-start | bytes 147464 | tf_op jit(solution)/shard_map/ppermute | solution.py:48
  11.1 6.3 %collective-permute-start.1 = (f32[8,1536]{1,0:T(8,128)S(1)}, f32[8,1536]{1,0:T(8,128)S(1)}, u32[]{:S(2)}, u32[]{:S(2)}) collective-permute-start(f32[8,1536]{1,0:T(8,128)S(1)} %add.24), channel_id=1, source_target_pairs={{0,8},{1,9},{2,10},{3,11},{4,12},{5,13},{6,14},{7,15},{8,0},{9,1},... | collective-permute-start | bytes 147464 | tf_op jit(solution)/shard_map/ppermute | solution.py:48
  11.5 10.3 %collective-permute-start.15 = (bf16[2,8,3200]{2,1,0:T(8,128)(2,1)S(1)}, bf16[2,8,3200]{2,1,0:T(8,128)(2,1)S(1)}, u32[]{:S(2)}, u32[]{:S(2)}) collective-permute-start(bf16[2,8,3200]{2,1,0:T(8,128)(2,1)S(1)} %pad_maximum_fusion.5), channel_id=1, source_target_pairs={{0,4},{1,5},{2,6},{3,7},{4,0},{5,1},{6,2},{7,3},{8,12},{9,13},{10,... | collective-permute-start | bytes 307208 | tf_op jit(solution)/shard_map/ppermute | solution.py:48
  12.6 10.2 %collective-permute-start.6 = (bf16[2,8,3200]{2,1,0:T(8,128)(2,1)S(1)}, bf16[2,8,3200]{2,1,0:T(8,128)(2,1)S(1)}, u32[]{:S(2)}, u32[]{:S(2)}) collective-permute-start(bf16[2,8,3200]{2,1,0:T(8,128)(2,1)S(1)} %pad_maximum_fusion.4), channel_id=1, source_target_pairs={{0,8},{1,9},{2,10},{3,11},{4,12},{5,13},{6,14},{7,15},{8,0},{9,1},... | collective-permute-start | bytes 307208 | tf_op jit(solution)/shard_map/ppermute | solution.py:48
  15.3 4.2 %collective-permute-start.11 = (f32[8,1536]{1,0:T(8,128)S(1)}, f32[8,1536]{1,0:T(8,128)S(1)}, u32[]{:S(2)}, u32[]{:S(2)}) collective-permute-start(f32[8,1536]{1,0:T(8,128)S(1)} %add.29), channel_id=1, source_target_pairs={{0,2},{1,3},{2,0},{3,1},{4,6},{5,7},{6,4},{7,5},{8,10},{9,11},{10,... | collective-permute-start | bytes 147464 | tf_op jit(solution)/shard_map/ppermute | solution.py:48
  17.4 4.2 %collective-permute-start.2 = (f32[8,1536]{1,0:T(8,128)S(1)}, f32[8,1536]{1,0:T(8,128)S(1)}, u32[]{:S(2)}, u32[]{:S(2)}) collective-permute-start(f32[8,1536]{1,0:T(8,128)S(1)} %add.25), channel_id=1, source_target_pairs={{0,2},{1,3},{2,0},{3,1},{4,6},{5,7},{6,4},{7,5},{8,10},{9,11},{10,... | collective-permute-start | bytes 147464 | tf_op jit(solution)/shard_map/ppermute | solution.py:48
  19.4 5.2 %collective-permute-start.12 = (f32[8,1536]{1,0:T(8,128)S(1)}, f32[8,1536]{1,0:T(8,128)S(1)}, u32[]{:S(2)}, u32[]{:S(2)}) collective-permute-start(f32[8,1536]{1,0:T(8,128)S(1)} %add.30), channel_id=1, source_target_pairs={{0,8},{1,9},{2,10},{3,11},{4,12},{5,13},{6,14},{7,15},{8,0},{9,1},... | collective-permute-start | bytes 147464 | tf_op jit(solution)/shard_map/ppermute | solution.py:48
  21.6 4.5 %collective-permute-start.3 = (f32[8,1536]{1,0:T(8,128)S(1)}, f32[8,1536]{1,0:T(8,128)S(1)}, u32[]{:S(2)}, u32[]{:S(2)}) collective-permute-start(f32[8,1536]{1,0:T(8,128)S(1)} %add.26), channel_id=1, source_target_pairs={{0,4},{1,5},{2,6},{3,7},{4,0},{5,1},{6,2},{7,3},{8,12},{9,13},{10,... | collective-permute-start | bytes 147464 | tf_op jit(solution)/shard_map/ppermute | solution.py:48
  21.9 5.8 %collective-permute-start.16 = (bf16[4,8,3200]{2,1,0:T(8,128)(2,1)S(1)}, bf16[4,8,3200]{2,1,0:T(8,128)(2,1)S(1)}, u32[]{:S(2)}, u32[]{:S(2)}) collective-permute-start(bf16[4,8,3200]{2,1,0:T(8,128)(2,1)S(1)} %pad_maximum_fusion.3), channel_id=1, source_target_pairs={{0,2},{1,3},{2,0},{3,1},{4,6},{5,7},{6,4},{7,5},{8,10},{9,11},{10,... | collective-permute-start | bytes 614408 | tf_op jit(solution)/shard_map/ppermute | solution.py:48
  22.8 5.8 %collective-permute-start.7 = (bf16[4,8,3200]{2,1,0:T(8,128)(2,1)S(1)}, bf16[4,8,3200]{2,1,0:T(8,128)(2,1)S(1)}, u32[]{:S(2)}, u32[]{:S(2)}) collective-permute-start(bf16[4,8,3200]{2,1,0:T(8,128)(2,1)S(1)} %pad_maximum_fusion.2), channel_id=1, source_target_pairs={{0,4},{1,5},{2,6},{3,7},{4,0},{5,1},{6,2},{7,3},{8,12},{9,13},{10,... | collective-permute-start | bytes 614408 | tf_op jit(solution)/shard_map/ppermute | solution.py:48
  24.7 5.0 %collective-permute-start.13 = (f32[8,1536]{1,0:T(8,128)S(1)}, f32[8,1536]{1,0:T(8,128)S(1)}, u32[]{:S(2)}, u32[]{:S(2)}) collective-permute-start(f32[8,1536]{1,0:T(8,128)S(1)} %add.31.own), channel_id=1, source_target_pairs={{0,1},{1,0},{2,3},{3,2},{4,5},{5,4},{6,7},{7,6},{8,9},{9,8},{10,11... | collective-permute-start | bytes 147464 | tf_op jit(solution)/shard_map/ppermute | solution.py:48
  26.0 9.0 %collective-permute-start.4 = (f32[8,1536]{1,0:T(8,128)S(1)}, f32[8,1536]{1,0:T(8,128)S(1)}, u32[]{:S(2)}, u32[]{:S(2)}) collective-permute-start(f32[8,1536]{1,0:T(8,128)S(1)} %add.27.own), channel_id=1, source_target_pairs={{0,1},{1,0},{2,3},{3,2},{4,5},{5,4},{6,7},{7,6},{8,9},{9,8},{10,11... | collective-permute-start | bytes 147464 | tf_op jit(solution)/shard_map/ppermute | solution.py:48
  27.8 1.8 %collective-permute-start.17 = (bf16[8,8,3200]{2,1,0:T(8,128)(2,1)S(1)}, bf16[8,8,3200]{2,1,0:T(8,128)(2,1)S(1)}, u32[]{:S(2)}, u32[]{:S(2)}) collective-permute-start(bf16[8,8,3200]{2,1,0:T(8,128)(2,1)S(1)} %pad_maximum_fusion.1), channel_id=1, source_target_pairs={{0,1},{1,0},{2,3},{3,2},{4,5},{5,4},{6,7},{7,6},{8,9},{9,8},{10,11... | collective-permute-start | bytes 1228808 | tf_op jit(solution)/shard_map/ppermute | solution.py:48
  28.7 6.3 %collective-permute-start.8 = (bf16[8,8,3200]{2,1,0:T(8,128)(2,1)S(1)}, bf16[8,8,3200]{2,1,0:T(8,128)(2,1)S(1)}, u32[]{:S(2)}, u32[]{:S(2)}) collective-permute-start(bf16[8,8,3200]{2,1,0:T(8,128)(2,1)S(1)} %pad_maximum_fusion), channel_id=1, source_target_pairs={{0,1},{1,0},{2,3},{3,2},{4,5},{5,4},{6,7},{7,6},{8,9},{9,8},{10,11... | collective-permute-start | bytes 1228808 | tf_op jit(solution)/shard_map/ppermute | solution.py:48
  29.6 5.5 %slice-start = ((s8[6291456]{0:T(1024)(128)(4,1)}), s8[4194304]{0:T(1024)(128)(4,1)S(1)}, s32[]{:S(2)}) async-start(s8[6291456]{0:T(1024)(128)(4,1)} %bitcast), calls=%async_computation | async-start | bytes 8388608
  29.6 5.4 %slice-start.1 = ((s8[6291456]{0:T(1024)(128)(4,1)}), s8[2097152]{0:T(1024)(128)(4,1)S(1)}, s32[]{:S(2)}) async-start(s8[6291456]{0:T(1024)(128)(4,1)} %bitcast), calls=%async_computation.1 | async-start | bytes 4194304

commit v5 on v4

--- a/solution.py
+++ b/solution.py
@@ -15,6 +15,8 @@
 SMOOTH = 64
 LANES = 128
 UNROLL = 3
+PIECES = 4
+BEGIN = 3 * 10**9
 VMEM = pl.BlockSpec(memory_space=pltpu.VMEM)
 SMEM = pl.BlockSpec(memory_space=pltpu.SMEM)
 HBM = pl.BlockSpec(memory_space=pltpu.HBM)
@@ -48,7 +50,7 @@
     return lax.ppermute(value, "chan", [(i, i ^ bit) for i in range(owners)])
 
 
-def pick_rows(bins, source_pick, lag_start, bad_flag, spectra, first, second, flags, sems):
+def pick_rows(bins, source_pick, lag_start, bad_flag, spectra, first, second, keeps, flags, sems):
     half = bins // 2
     pick, lag = source_pick[0], lag_start[0]
     copies = [pltpu.make_async_copy(bad_flag, flags, sems.at[4])]
@@ -71,6 +73,8 @@
     extra = jnp.where(row == 0, high.astype(f32), jnp.where(row == 1, low.astype(f32), keep))
     for rows in (first, second):
         rows[0, :, pl.ds(bins, LANES)] = extra.astype(bf16)
+    for r in range(keeps.shape[0]):
+        keeps[r] = jnp.full(keeps.shape[1:], (1 - flags[r]).astype(f32))
     for copy in copies[1:]:
         copy.wait()
 
@@ -78,6 +82,7 @@
 def add_channels(bins, spectra, *outs):
     core = lax.axis_index("chan") & 1
     half = bins // 2
+    outs[4][...] = spectra[...]
     for h in range(2):
         own, other = outs[2 * h : 2 * h + 2]
         for part in range(2):
@@ -111,8 +116,76 @@
     return jnp.where(cos_neg, -cosine, cosine), jnp.where(sin_neg, -sine, sine)
 
 
-def correlate(h, bins, order, first_order, channels, bad_flag, spectra, own, other, got, table, *rest):
-    before, (out, rec, src, ang, cross) = rest[:h], rest[h:]
+def rounded(value):
+    return value.astype(bf16).astype(f32)
+
+
+def whitening(h, bins, channels, core, own, other, windows):
+    half = bins // 2
+    block_i = lax.broadcasted_iota(jnp.int32, (LANES, LANES), 0) // SMOOTH
+    block_j = lax.broadcasted_iota(jnp.int32, (LANES, LANES), 1) // SMOOTH
+    same = jnp.where(block_i == block_j, 1.0 / SMOOTH, 0.0).astype(bf16)
+    lane = lax.broadcasted_iota(jnp.int32, (1, LANES), 1)
+    inv = 1.0 / channels
+
+    def means(c):
+        at = pl.ds(pl.multiple_of(c * LANES, LANES), LANES)
+        m_own, m_other = own[:, at] * inv, other[:, at] * inv
+        return jnp.where(core == 0, m_own, m_other), jnp.where(core == 0, m_other, m_own)
+
+    def scales(power):
+        count = power.shape[0]
+        power = power.reshape(count * windows, LANES)
+        high = power.astype(bf16)
+        low = (power - high.astype(f32)).astype(bf16)
+        level = jnp.dot(high, same, preferred_element_type=f32) + jnp.dot(
+            low, same, preferred_element_type=f32
+        )
+        return lax.rsqrt(level + 1e-6).reshape(count, windows, LANES)
+
+    def numbers(c):
+        return (lane + (h * half + 1) + c * LANES).astype(f32)
+
+    return means, scales, numbers
+
+
+def cross_rows(c, half, mean, scales, number, got, first, lags, kept, ang, src, receivers, a, b, pairs, norm, store):
+    windows = got.shape[1]
+    count = got.shape[0] - first
+    re_at = pl.ds(pl.multiple_of(c * LANES, LANES), LANES)
+    im_at = pl.ds(pl.multiple_of(half + c * LANES, LANES), LANES)
+    cosine, sine = cos_sin(lags * number)
+    ang[0], ang[1] = cosine * kept, sine * kept
+    g_re = got[first:, :, re_at].astype(f32) - mean[0][None]
+    g_im = got[first:, :, im_at].astype(f32) - mean[1][None]
+    scale = scales(g_re * g_re + g_im * g_im)
+    for i in range(count):
+        w_re = rounded(g_re[i] * scale[i])
+        w_im = rounded(g_im[i] * scale[i])
+        cosine = ang[0, pl.ds(i, windows, stride=0), :]
+        sine = ang[1, pl.ds(i, windows, stride=0), :]
+        src[0, i] = rounded(w_re * cosine + w_im * sine)
+        src[1, i] = rounded(w_im * cosine - w_re * sine)
+    for row, members in pairs:
+        pair = []
+        for i in members:
+            c_re = c_im = None
+            for w in range(windows):
+                g = src[0, i - first, pl.ds(w, receivers, stride=0), :]
+                e = src[1, i - first, pl.ds(w, receivers, stride=0), :]
+                t_re = g * a[w] + e * b[w]
+                t_im = g * b[w] - e * a[w]
+                c_re = t_re if c_re is None else c_re + t_re
+                c_im = t_im if c_im is None else c_im + t_im
+            pair.append((c_re * norm, c_im * norm))
+        for part in range(2):
+            cols = pl.ds(pl.multiple_of((2 * c + part) * LANES, LANES), LANES)
+            both = jnp.concatenate([pair[0][part], pair[1][part]], 0)
+            store[row : row + 2 * receivers, cols] = both.astype(bf16)
+
+
+def correlate(h, bins, order, first_order, channels, keep, spectra, own, other, got, table, *rest):
+    before, (out, rec, src, ang, cross, *leaving) = rest[:h], rest[h:]
     me = lax.axis_index("chan").astype(jnp.int32)
     core = me & 1
     receivers, windows = spectra.shape[0], spectra.shape[1]
@@ -127,7 +200,6 @@
     inv = 1.0 / channels
     places, seen = masks(first_order), masks(order)
     held = [seen.index(m) for m in places]
-    keep = [(1 - bad_flag[r]).astype(f32) for r in range(receivers)]
     tail = got[:, :, pl.ds(bins, LANES)].astype(f32)
     lags = tail[:, 0, :] * 32.0 + tail[:, 1, :]
     kept = tail[:, 2, :]
@@ -141,9 +213,6 @@
             low, same, preferred_element_type=f32
         )
         return lax.rsqrt(level + 1e-6).reshape(count, windows, LANES)
-
-    def rounded(value):
-        return value.astype(bf16).astype(f32)
 
     def chunk(c, _):
         re_at = pl.ds(pl.multiple_of(c * LANES, LANES), LANES)
@@ -194,14 +263,99 @@
         return 0
 
     lax.fori_loop(0, chunks, chunk, 0, unroll=UNROLL)
-    product = jnp.dot(cross[...], table[...], preferred_element_type=f32)
     if h == 0:
-        out[...] = product
+        out[...] = jnp.dot(cross[...], table[...], preferred_element_type=f32)
         return
-    product = product + before[0][...]
-    for p in range(sources):
-        source = jnp.bitwise_xor(me, places[p])
-        out[source] = product[p * receivers : (p + 1) * receivers, :]
+    final, sems = leaving
+    copies = []
+    for piece in range(PIECES):
+        cols = slice(piece * LAGW // PIECES, (piece + 1) * LAGW // PIECES)
+        product = before[0][:, cols] + jnp.dot(
+            cross[...], table[:, cols], preferred_element_type=f32
+        )
+        for p in range(sources):
+            source = jnp.bitwise_xor(me, places[p])
+            final[source, :, cols] = product[p * receivers : (p + 1) * receivers, :]
+        copies.append(
+            pltpu.make_async_copy(final.at[:, :, cols], out.at[:, :, cols], sems.at[piece])
+        )
+        copies[-1].start()
+    for copy in copies:
+        copy.wait()
+
+
+def begin(h, bins, pairs, channels, keep, spectra, own, other, got, white, store, src, ang):
+    core = lax.axis_index("chan") & 1
+    receivers, windows = spectra.shape[0], spectra.shape[1]
+    half = bins // 2
+    norm = 1.0 / math.sqrt(windows * bins)
+    means, scales, numbers = whitening(h, bins, channels, core, own, other, windows)
+    tail = got[:, :, pl.ds(bins, LANES)].astype(f32)
+    lags, kept = tail[:, 0, :] * 32.0 + tail[:, 1, :], tail[:, 2, :]
+
+    def chunk(c, _):
+        bin_at = pl.ds(pl.multiple_of(h * half + c * LANES, LANES), LANES)
+        imag_at = pl.ds(pl.multiple_of(bins + h * half + c * LANES, LANES), LANES)
+        mean = means(c)
+        x_re = spectra[:, :, bin_at].astype(f32) - mean[0][None]
+        x_im = spectra[:, :, imag_at].astype(f32) - mean[1][None]
+        scale = scales(x_re * x_re + x_im * x_im)
+        for r in range(receivers):
+            factor = scale[r] * keep[r]
+            white[c, 0, r] = rounded(x_re[r] * factor)
+            white[c, 1, r] = rounded(x_im[r] * factor)
+        a = [white[c, 0, :, w, :] for w in range(windows)]
+        b = [white[c, 1, :, w, :] for w in range(windows)]
+        cross_rows(
+            c, half, mean, scales, numbers(c), got, 0, lags, kept, ang, src, receivers, a, b, pairs, norm, store
+        )
+        return 0
+
+    lax.fori_loop(0, half // LANES, chunk, 0, unroll=UNROLL)
+
+
+def finish(h, bins, first, early, pairs, places, channels, own, other, got, white, store, table, *rest):
+    before, (out, src, ang, cross, *leaving) = rest[:h], rest[h:]
+    me = lax.axis_index("chan").astype(jnp.int32)
+    core = me & 1
+    receivers, windows = white.shape[2], white.shape[3]
+    half = bins // 2
+    norm = 1.0 / math.sqrt(windows * bins)
+    means, scales, numbers = whitening(h, bins, channels, core, own, other, windows)
+    tail = got[first:, :, pl.ds(bins, LANES)].astype(f32)
+    lags, kept = tail[:, 0, :] * 32.0 + tail[:, 1, :], tail[:, 2, :]
+    for source, dest in early:
+        cross[dest : dest + 2 * receivers, :] = store[source : source + 2 * receivers, :]
+
+    def chunk(c, _):
+        a = [white[c, 0, :, w, :] for w in range(windows)]
+        b = [white[c, 1, :, w, :] for w in range(windows)]
+        cross_rows(
+            c, half, means(c), scales, numbers(c), got, first, lags, kept, ang, src, receivers, a, b, pairs, norm,
+            cross,
+        )
+        return 0
+
+    lax.fori_loop(0, half // LANES, chunk, 0, unroll=UNROLL)
+    if h == 0:
+        out[...] = jnp.dot(cross[...], table[...], preferred_element_type=f32)
+        return
+    final, sems = leaving
+    copies = []
+    for piece in range(PIECES):
+        cols = slice(piece * LAGW // PIECES, (piece + 1) * LAGW // PIECES)
+        product = before[0][:, cols] + jnp.dot(
+            cross[...], table[:, cols], preferred_element_type=f32
+        )
+        for p, place in enumerate(places):
+            source = jnp.bitwise_xor(me, place)
+            final[source, :, cols] = product[p * receivers : (p + 1) * receivers, :]
+        copies.append(
+            pltpu.make_async_copy(final.at[:, :, cols], out.at[:, :, cols], sems.at[piece])
+        )
+        copies[-1].start()
+    for copy in copies:
+        copy.wait()
 
 
 def shards(spectra, bad_flag, source_pick, lag_start):
@@ -211,11 +365,11 @@
     half = bins // 2
     flat = jax.ShapeDtypeStruct((windows, half), f32)
     rows = jax.ShapeDtypeStruct((1, windows, bins + LANES), bf16)
-    first, second = pl.pallas_call(
+    first, second, keep = pl.pallas_call(
         functools.partial(pick_rows, bins),
-        out_shape=(rows, rows),
+        out_shape=(rows, rows, jax.ShapeDtypeStruct((receivers, windows, LANES), f32)),
         in_specs=[SMEM, SMEM, HBM, HBM],
-        out_specs=(VMEM, VMEM),
+        out_specs=(VMEM,) * 3,
         scratch_shapes=[pltpu.SMEM((receivers,), jnp.int32), pltpu.SemaphoreType.DMA((5,))],
         compiler_params=pltpu.CompilerParams(vmem_limit_bytes=8 << 20),
         name="pick_rows",
@@ -227,15 +381,20 @@
     )
     sums = pl.pallas_call(
         functools.partial(add_channels, bins),
-        out_shape=(flat,) * 4,
+        out_shape=(flat,) * 4 + (jax.ShapeDtypeStruct(spectra.shape, bf16),),
         in_specs=[VMEM],
-        out_specs=(VMEM,) * 4,
+        out_specs=(VMEM,) * 5,
         compiler_params=pltpu.CompilerParams(vmem_limit_bytes=8 << 20),
         name="add_channels",
     )(spectra)
+    held_spectra = sums[4]
     total_order, row_order = orders(owners)
     table = lag_table(bins)
-    totals, gots = [], []
+    channels = receivers * owners
+    chunks = half // LANES
+    first_count = owners // 4
+    places = masks(row_order[0])
+    totals, gots, begun = [], [], []
     for h in range(2):
         own, other = sums[2 * h : 2 * h + 2]
         got = (first, second)[h]
@@ -243,28 +402,73 @@
         for bit in total_order[h]:
             total = total + swap(total, bit)
         totals.append((total, swap(total, 1)))
+        held = [masks(row_order[h]).index(m) for m in places]
+        pairs = [(p * receivers, (held[p], held[p + 1])) for p in range(0, owners, 2)]
+        early = [pair for pair in pairs if max(pair[1]) < first_count]
+        late = [pair for pair in pairs if max(pair[1]) >= first_count]
+        moved = [(2 * receivers * i, row) for i, (row, _) in enumerate(early)]
         for bit in row_order[h]:
+            if h == 0 and got.shape[0] == first_count:
+                begun.append(
+                    (moved, late)
+                    + tuple(
+                        pl.pallas_call(
+                            functools.partial(
+                                begin, h, bins, [(2 * receivers * i, m) for i, (_, m) in enumerate(early)], channels
+                            ),
+                            out_shape=(
+                                jax.ShapeDtypeStruct((chunks, 2, receivers, windows, LANES), f32),
+                                jax.ShapeDtypeStruct((first_count * receivers, bins), bf16),
+                            ),
+                            in_specs=[VMEM] * 5,
+                            out_specs=(VMEM, VMEM),
+                            scratch_shapes=[
+                                pltpu.VMEM((2, first_count, windows, LANES), f32),
+                                pltpu.VMEM((2, first_count, LANES), f32),
+                            ],
+                            compiler_params=pltpu.CompilerParams(vmem_limit_bytes=16 << 20),
+                            cost_estimate=pl.CostEstimate(flops=BEGIN, bytes_accessed=4 << 20, transcendentals=0),
+                            name="begin",
+                        )(keep, held_spectra, *totals[h], got)
+                    )
+                )
             got = jnp.concatenate([got, swap(got, bit)], 0)
         gots.append(got)
-    result = ()
-    for h in range(2):
-        shape = (owners * receivers, LAGW) if h == 0 else (owners, receivers, LAGW)
-        result = (pl.pallas_call(
-            functools.partial(correlate, h, bins, row_order[h], row_order[0], receivers * owners),
-            out_shape=jax.ShapeDtypeStruct(shape, f32),
-            in_specs=[SMEM] + [VMEM] * (5 + h),
-            out_specs=VMEM,
-            scratch_shapes=[
-                pltpu.VMEM((2, receivers, windows, LANES), f32),
-                pltpu.VMEM((2, owners, windows, LANES), f32),
-                pltpu.VMEM((2, owners, LANES), f32),
-                pltpu.VMEM((owners * receivers, bins), bf16),
-            ],
-            compiler_params=pltpu.CompilerParams(vmem_limit_bytes=24 << 20),
-            cost_estimate=pl.CostEstimate(flops=5 * 10**9, bytes_accessed=10 << 20, transcendentals=0),
-            name="correlate",
-        )(bad_flag, spectra, *totals[h], gots[h], jnp.asarray(table[h * bins : (h + 1) * bins]), *result),)
-    return result[0]
+    late_count = owners - first_count
+    whole = (owners * receivers, LAGW)
+    moved, late, white, store = begun[0]
+    part = pl.pallas_call(
+        functools.partial(finish, 0, bins, first_count, moved, late, places, channels),
+        out_shape=jax.ShapeDtypeStruct(whole, f32),
+        in_specs=[VMEM] * 6,
+        out_specs=VMEM,
+        scratch_shapes=[
+            pltpu.VMEM((2, late_count, windows, LANES), f32),
+            pltpu.VMEM((2, late_count, LANES), f32),
+            pltpu.VMEM((owners * receivers, bins), bf16),
+        ],
+        compiler_params=pltpu.CompilerParams(vmem_limit_bytes=16 << 20),
+        cost_estimate=pl.CostEstimate(flops=4 * 10**9, bytes_accessed=10 << 20, transcendentals=0),
+        name="finish",
+    )(*totals[0], gots[0], white, store, jnp.asarray(table[:bins]))
+    shape = (owners, receivers, LAGW)
+    return pl.pallas_call(
+        functools.partial(correlate, 1, bins, row_order[1], row_order[0], channels),
+        out_shape=jax.ShapeDtypeStruct(shape, f32),
+        in_specs=[VMEM] * 7,
+        out_specs=HBM,
+        scratch_shapes=[
+            pltpu.VMEM((2, receivers, windows, LANES), f32),
+            pltpu.VMEM((2, owners, windows, LANES), f32),
+            pltpu.VMEM((2, owners, LANES), f32),
+            pltpu.VMEM((owners * receivers, bins), bf16),
+            pltpu.VMEM(shape, f32),
+            pltpu.SemaphoreType.DMA((PIECES,)),
+        ],
+        compiler_params=pltpu.CompilerParams(vmem_limit_bytes=24 << 20),
+        cost_estimate=pl.CostEstimate(flops=5 * 10**9, bytes_accessed=10 << 20, transcendentals=0),
+        name="correlate",
+    )(keep, held_spectra, *totals[1], gots[1], jnp.asarray(table[bins:]), part)
 
 
 def solution(mesh):

time: 41.4 us -> 40.7 us (0.983)
  waiting for transfers between devices: 8.68 us -> 7.44 us
  starting transfers between devices: 16.9 us -> 17.8 us
    ppermute x18, waiting for transfers between devices: 8.68 us -> 7.44 us  [swap(): return lax.ppermute(value, 'chan', [(i, i ^ bit) for i in range(owners)])]
    ppermute x18, starting transfers between devices: 16.9 us -> 17.8 us  [swap(): return lax.ppermute(value, 'chan', [(i, i ^ bit) for i in range(owners)])]
    pallas_call x3 -> x4, Pallas kernels: 12.2 us -> 11.9 us  [the longest x1 5.46 us: shards(): pl.pallas_call(functools.partial(correlate, 1, bins, row_order[1], row_or...]
    unnamed x19 -> x17, local copies, waits for them, and re-layouts: 1.26 us -> 1.25 us
  transfers between devices with their start and end apart: 18 -> 18, of which waited for: 7 -> 7; matrix products, arithmetic and copies ran while one was open for 1% -> 1% of each run, Pallas kernels for 13% -> 16%
where the time goes in v5:
time: 40.7 us; the launch traced here: 40.4 us
  starting transfers between devices  17.8 us (44%)
  Pallas kernels  12 us (29%)
  waiting for transfers between devices  7.44 us (18%)
  between operations  1.53 us (4%)
  local copies, waits for them, and re-layouts  1.34 us (3%)
    ppermute x18, starting transfers between devices, swap(): return lax.ppermute(value, 'chan', [(i, i ^ bit) for i in range(owners)])  17.8 us
    ppermute x18, waiting for transfers between devices, swap(): return lax.ppermute(value, 'chan', [(i, i ^ bit) for i in range(owners)])  7.44 us
    pallas_call x1, Pallas kernels, shards(): pl.pallas_call(functools.partial(correlate, 1, bins, row_order[1], row_or...  5.46 us
    pallas_call x1, Pallas kernels, shards(): pl.pallas_call(functools.partial(finish, 0, bins, first_count, moved, lat...  3.79 us
    pallas_call x1, Pallas kernels, shards(): pl.pallas_call(functools.partial(begin, h, bins, [(2 * receivers * i, m)...  1.81 us
    unnamed x17, local copies, waits for them, and re-layouts  1.25 us
    pallas_call x1, Pallas kernels, shards(): pl.pallas_call(functools.partial(pick_rows, bins), out_shape=(rows, rows,...  0.84 us
  transfers between devices with their start and end apart: 18, of which 7 were waited for; matrix products, arithmetic and copies ran while one was open for 1% of the time, Pallas kernels for 16%

profile of v5, /device:TPU:0, one launch (start us, length us, event | category | flops | bytes accessed | tf_op | source)
XLA Modules:
  0.0 40.4 jit_solution(12277476251669959433)
XLA Ops:
  0.0 0.0 copy-start
  0.0 1.1 %copy-done = bf16[8,8,6144]{2,1,0:T(8,128)(2,1)S(1)} copy-done((bf16[8,8,6144]{2,1,0:T(8,128)(2,1)S(1)}, bf16[8,8,6144]{2,1,0:T(8,128)(2,1)}, u32[]{:S(2)}) %copy-start) | copy-done | bytes 786456
  1.1 0.1 add_channels.1
  1.3 0.5 %collective-permute-start.9 = (f32[8,1536]{1,0:T(8,128)S(1)}, f32[8,1536]{1,0:T(8,128)S(1)}, u32[]{:S(2)}, u32[]{:S(2)}) collective-permute-start(f32[8,1536]{1,0:T(8,128)S(1)} %get-tuple-element.21), channel_id=1, source_target_pairs={{0,1},{1,0},{2,3},{3,2},{4,5},{5,4},{6,7},{7,6},{8,9},{9,8},{10,11... | collective-permute-start | bytes 147464 | tf_op jit(solution)/shard_map/ppermute | solution.py:50
  3.1 0.8 %pick_rows.1 = (bf16[1,8,3200]{2,1,0:T(8,128)(2,1)S(1)}, bf16[1,8,3200]{2,1,0:T(8,128)(2,1)S(1)}, f32[8,8,128]{2,1,0:T(8,128)S(1)}) custom-call(s32[1]{0:T(128)S(6)} %copy.17.source_pick, s32[1]{0:T(128)S(6)} %copy.18.lag_start, s32[8]{0:T(128)} %bad_flag.1, bf16[8,8,6144]{2,1,0:T(8,128)(2,1)} %spectra.3), custom_call_target="tpu_custom_call" | custom-call | tf_op jit(solution)/shard_map/pick_rows/pallas_call | solution.py:368
  3.9 3.7 %collective-permute-start.14 = (bf16[1,8,3200]{2,1,0:T(8,128)(2,1)S(1)}, bf16[1,8,3200]{2,1,0:T(8,128)(2,1)S(1)}, u32[]{:S(2)}, u32[]{:S(2)}) collective-permute-start(bf16[1,8,3200]{2,1,0:T(8,128)(2,1)S(1)} %get-tuple-element.22), channel_id=1, source_target_pairs={{0,8},{1,9},{2,10},{3,11},{4,12},{5,13},{6,14},{7,15},{8,0},{9,1},... | collective-permute-start | bytes 153608 | tf_op jit(solution)/shard_map/ppermute | solution.py:50
  7.6 1.5 %collective-permute-start.5 = (bf16[1,8,3200]{2,1,0:T(8,128)(2,1)S(1)}, bf16[1,8,3200]{2,1,0:T(8,128)(2,1)S(1)}, u32[]{:S(2)}, u32[]{:S(2)}) collective-permute-start(bf16[1,8,3200]{2,1,0:T(8,128)(2,1)S(1)} %get-tuple-element.19), channel_id=1, source_target_pairs={{0,2},{1,3},{2,0},{3,1},{4,6},{5,7},{6,4},{7,5},{8,10},{9,11},{10,... | collective-permute-start | bytes 153608 | tf_op jit(solution)/shard_map/ppermute | solution.py:50
  9.1 0.0 collective-permute-start
  9.2 0.0 collective-permute-done.9
  9.2 1.6 %collective-permute-start.10 = (f32[8,1536]{1,0:T(8,128)S(1)}, f32[8,1536]{1,0:T(8,128)S(1)}, u32[]{:S(2)}, u32[]{:S(2)}) collective-permute-start(f32[8,1536]{1,0:T(8,128)S(1)} %add.28), channel_id=1, source_target_pairs={{0,4},{1,5},{2,6},{3,7},{4,0},{5,1},{6,2},{7,3},{8,12},{9,13},{10,... | collective-permute-start | bytes 147464 | tf_op jit(solution)/shard_map/ppermute | solution.py:50
  10.8 0.0 collective-permute-done
  10.8 0.4 collective-permute-start.1
  11.2 0.0 collective-permute-done.14
  11.3 1.2 %collective-permute-start.15 = (bf16[2,8,3200]{2,1,0:T(8,128)(2,1)S(1)}, bf16[2,8,3200]{2,1,0:T(8,128)(2,1)S(1)}, u32[]{:S(2)}, u32[]{:S(2)}) collective-permute-start(bf16[2,8,3200]{2,1,0:T(8,128)(2,1)S(1)} %pad_maximum_fusion.4), channel_id=1, source_target_pairs={{0,4},{1,5},{2,6},{3,7},{4,0},{5,1},{6,2},{7,3},{8,12},{9,13},{10,... | collective-permute-start | bytes 307208 | tf_op jit(solution)/shard_map/ppermute | solution.py:50
  12.4 0.0 collective-permute-done.5
  12.5 3.1 %collective-permute-start.6 = (bf16[2,8,3200]{2,1,0:T(8,128)(2,1)S(1)}, bf16[2,8,3200]{2,1,0:T(8,128)(2,1)S(1)}, u32[]{:S(2)}, u32[]{:S(2)}) collective-permute-start(bf16[2,8,3200]{2,1,0:T(8,128)(2,1)S(1)} %pad_maximum_fusion.3), channel_id=1, source_target_pairs={{0,8},{1,9},{2,10},{3,11},{4,12},{5,13},{6,14},{7,15},{8,0},{9,1},... | collective-permute-start | bytes 307208 | tf_op jit(solution)/shard_map/ppermute | solution.py:50
  15.6 0.0 collective-permute-done.10
  15.6 1.6 %collective-permute-start.11 = (f32[8,1536]{1,0:T(8,128)S(1)}, f32[8,1536]{1,0:T(8,128)S(1)}, u32[]{:S(2)}, u32[]{:S(2)}) collective-permute-start(f32[8,1536]{1,0:T(8,128)S(1)} %add.29), channel_id=1, source_target_pairs={{0,2},{1,3},{2,0},{3,1},{4,6},{5,7},{6,4},{7,5},{8,10},{9,11},{10,... | collective-permute-start | bytes 147464 | tf_op jit(solution)/shard_map/ppermute | solution.py:50
  17.2 0.0 collective-permute-done.1
  17.2 0.5 %collective-permute-start.2 = (f32[8,1536]{1,0:T(8,128)S(1)}, f32[8,1536]{1,0:T(8,128)S(1)}, u32[]{:S(2)}, u32[]{:S(2)}) collective-permute-start(f32[8,1536]{1,0:T(8,128)S(1)} %add.25), channel_id=1, source_target_pairs={{0,2},{1,3},{2,0},{3,1},{4,6},{5,7},{6,4},{7,5},{8,10},{9,11},{10,... | collective-permute-start | bytes 147464 | tf_op jit(solution)/shard_map/ppermute | solution.py:50
  17.8 2.3 %collective-permute-done.11 = f32[8,1536]{1,0:T(8,128)S(1)} collective-permute-done((f32[8,1536]{1,0:T(8,128)S(1)}, f32[8,1536]{1,0:T(8,128)S(1)}, u32[]{:S(2)}, u32[]{:S(2)}) %collective-permute-start.11) | collective-permute-done | bytes 49184 | tf_op jit(solution)/shard_map/ppermute | solution.py:50
  20.0 0.2 collective-permute-start.12
  20.2 1.1 %collective-permute-done.2 = f32[8,1536]{1,0:T(8,128)S(1)} collective-permute-done((f32[8,1536]{1,0:T(8,128)S(1)}, f32[8,1536]{1,0:T(8,128)S(1)}, u32[]{:S(2)}, u32[]{:S(2)}) %collective-permute-start.2) | collective-permute-done | bytes 49184 | tf_op jit(solution)/shard_map/ppermute | solution.py:50
  21.4 0.4 collective-permute-start.3
  21.7 0.0 collective-permute-done.15
  21.8 0.9 %collective-permute-start.16 = (bf16[4,8,3200]{2,1,0:T(8,128)(2,1)S(1)}, bf16[4,8,3200]{2,1,0:T(8,128)(2,1)S(1)}, u32[]{:S(2)}, u32[]{:S(2)}) collective-permute-start(bf16[4,8,3200]{2,1,0:T(8,128)(2,1)S(1)} %get-tuple-element.25.got), channel_id=1, source_target_pairs={{0,2},{1,3},{2,0},{3,1},{4,6},{5,7},{6,4},{7,5},{8,10},{9,11},{10,... | collective-permute-start | bytes 614408 | tf_op jit(solution)/shard_map/ppermute | solution.py:50
  22.7 0.0 collective-permute-done.6
  22.7 1.4 %collective-permute-start.7 = (bf16[4,8,3200]{2,1,0:T(8,128)(2,1)S(1)}, bf16[4,8,3200]{2,1,0:T(8,128)(2,1)S(1)}, u32[]{:S(2)}, u32[]{:S(2)}) collective-permute-start(bf16[4,8,3200]{2,1,0:T(8,128)(2,1)S(1)} %pad_maximum_fusion.2), channel_id=1, source_target_pairs={{0,4},{1,5},{2,6},{3,7},{4,0},{5,1},{6,2},{7,3},{8,12},{9,13},{10,... | collective-permute-start | bytes 614408 | tf_op jit(solution)/shard_map/ppermute | solution.py:50
  24.1 1.3 %collective-permute-done.12 = f32[8,1536]{1,0:T(8,128)S(1)} collective-permute-done((f32[8,1536]{1,0:T(8,128)S(1)}, f32[8,1536]{1,0:T(8,128)S(1)}, u32[]{:S(2)}, u32[]{:S(2)}) %collective-permute-start.12) | collective-permute-done | bytes 49184 | tf_op jit(solution)/shard_map/ppermute | solution.py:50
  25.5 0.1 collective-permute-start.13
  25.5 0.0 slice-start.2
  25.6 0.9 %collective-permute-done.3 = f32[8,1536]{1,0:T(8,128)S(1)} collective-permute-done((f32[8,1536]{1,0:T(8,128)S(1)}, f32[8,1536]{1,0:T(8,128)S(1)}, u32[]{:S(2)}, u32[]{:S(2)}) %collective-permute-start.3) | collective-permute-done | bytes 49184 | tf_op jit(solution)/shard_map/ppermute | solution.py:50
  26.4 0.1 collective-permute-start.4
  26.5 0.2 collective-permute-done.13.other
  26.7 0.0 slice-start.3
  26.7 1.8 %begin.1 = (f32[12,2,8,8,128]{4,3,2,1,0:T(8,128)S(1)}, bf16[32,3072]{1,0:T(8,128)(2,1)S(1)}) custom-call(f32[8,8,128]{2,1,0:T(8,128)S(1)} %get-tuple-element.15.keep, bf16[8,8,6144]{2,1,0:T(8,128)(2,1)S(1)} %get-tuple-element.16.spectra, f32[8,1536]{1,0:T(8,128)S(1)} %add.31.own, f32[8,1536]{1,0:T(8,128)S(1)} %collective-permute-done.13.other, ...), custom_call_target="tpu_custom_call" | custom-call | flops 3000000000 | bytes 4194304 | tf_op jit(solution)/shard_map/begin/pallas_call | solution.py:415
  28.6 0.0 collective-permute-done.16
  28.6 0.1 pad_maximum_fusion.1
  28.6 0.3 collective-permute-start.17
  29.0 0.0 collective-permute-done.7
  29.0 0.1 pad_maximum_fusion
  29.0 0.3 collective-permute-start.8
  29.4 1.1 %collective-permute-done.17 = bf16[8,8,3200]{2,1,0:T(8,128)(2,1)S(1)} collective-permute-done((bf16[8,8,3200]{2,1,0:T(8,128)(2,1)S(1)}, bf16[8,8,3200]{2,1,0:T(8,128)(2,1)S(1)}, u32[]{:S(2)}, u32[]{:S(2)}) %collective-permute-start.17) | collective-permute-done | bytes 409632 | tf_op jit(solution)/shard_map/ppermute | solution.py:50
  30.5 0.5 %collective-permute-done.8 = bf16[8,8,3200]{2,1,0:T(8,128)(2,1)S(1)} collective-permute-done((bf16[8,8,3200]{2,1,0:T(8,128)(2,1)S(1)}, bf16[8,8,3200]{2,1,0:T(8,128)(2,1)S(1)}, u32[]{:S(2)}, u32[]{:S(2)}) %collective-permute-start.8) | collective-permute-done | bytes 409632 | tf_op jit(solution)/shard_map/ppermute | solution.py:50
  31.0 0.0 slice-start
  31.1 0.0 slice-done.2
  31.1 0.0 slice-done.3
  31.1 0.0 slice-start.1
  31.1 3.8 %finish.1.rest_0_ = f32[128,1024]{1,0:T(8,128)S(1)} custom-call(f32[8,1536]{1,0:T(8,128)S(1)} %add.31.own, f32[8,1536]{1,0:T(8,128)S(1)} %collective-permute-done.13.other, bf16[16,8,3200]{2,1,0:T(8,128)(2,1)S(1)} %constant_dynamic-update-slice_fusion.8.got, f32[12,2,8,8,128]{4,3,2,1,0:T(8,128)S(1)} %get-tuple-element.23.white, ...), custom_call_target="tpu_custom_call" | custom-call | flops 4000000000 | bytes 10485760 | tf_op jit(solution)/shard_map/finish/pallas_call | solution.py:440
  34.9 0.0 collective-permute-done.4.other
  34.9 0.0 slice-done
  34.9 0.0 slice-done.1
  35.0 5.5 %correlate.1 = f32[16,8,1024]{2,1,0:T(8,128)} custom-call(f32[8,8,128]{2,1,0:T(8,128)S(1)} %get-tuple-element.15.keep, bf16[8,8,6144]{2,1,0:T(8,128)(2,1)S(1)} %get-tuple-element.16.spectra, f32[8,1536]{1,0:T(8,128)S(1)} %add.27.own, f32[8,1536]{1,0:T(8,128)S(1)} %collective-permute-done.4.other, ...), custom_call_target="tpu_custom_call" | custom-call | flops 5000000000 | bytes 10485760 | tf_op jit(solution)/shard_map/correlate/pallas_call | solution.py:455
  (23 shorter events, 0.3 us)
Async XLA Ops:
  0.0 1.1 %copy-start = (bf16[8,8,6144]{2,1,0:T(8,128)(2,1)S(1)}, bf16[8,8,6144]{2,1,0:T(8,128)(2,1)}, u32[]{:S(2)}) copy-start(bf16[8,8,6144]{2,1,0:T(8,128)(2,1)} %spectra.3) | copy-start | bytes 2359300
  1.3 7.9 %collective-permute-start.9 = (f32[8,1536]{1,0:T(8,128)S(1)}, f32[8,1536]{1,0:T(8,128)S(1)}, u32[]{:S(2)}, u32[]{:S(2)}) collective-permute-start(f32[8,1536]{1,0:T(8,128)S(1)} %get-tuple-element.21), channel_id=1, source_target_pairs={{0,1},{1,0},{2,3},{3,2},{4,5},{5,4},{6,7},{7,6},{8,9},{9,8},{10,11... | collective-permute-start | bytes 147464 | tf_op jit(solution)/shard_map/ppermute | solution.py:50
  3.9 7.3 %collective-permute-start.14 = (bf16[1,8,3200]{2,1,0:T(8,128)(2,1)S(1)}, bf16[1,8,3200]{2,1,0:T(8,128)(2,1)S(1)}, u32[]{:S(2)}, u32[]{:S(2)}) collective-permute-start(bf16[1,8,3200]{2,1,0:T(8,128)(2,1)S(1)} %get-tuple-element.22), channel_id=1, source_target_pairs={{0,8},{1,9},{2,10},{3,11},{4,12},{5,13},{6,14},{7,15},{8,0},{9,1},... | collective-permute-start | bytes 153608 | tf_op jit(solution)/shard_map/ppermute | solution.py:50
  7.6 4.8 %collective-permute-start.5 = (bf16[1,8,3200]{2,1,0:T(8,128)(2,1)S(1)}, bf16[1,8,3200]{2,1,0:T(8,128)(2,1)S(1)}, u32[]{:S(2)}, u32[]{:S(2)}) collective-permute-start(bf16[1,8,3200]{2,1,0:T(8,128)(2,1)S(1)} %get-tuple-element.19), channel_id=1, source_target_pairs={{0,2},{1,3},{2,0},{3,1},{4,6},{5,7},{6,4},{7,5},{8,10},{9,11},{10,... | collective-permute-start | bytes 153608 | tf_op jit(solution)/shard_map/ppermute | solution.py:50
  9.1 1.7 %collective-permute-start = (f32[8,1536]{1,0:T(8,128)S(1)}, f32[8,1536]{1,0:T(8,128)S(1)}, u32[]{:S(2)}, u32[]{:S(2)}) collective-permute-start(f32[8,1536]{1,0:T(8,128)S(1)} %get-tuple-element.18), channel_id=1, source_target_pairs={{0,1},{1,0},{2,3},{3,2},{4,5},{5,4},{6,7},{7,6},{8,9},{9,8},{10,11... | collective-permute-start | bytes 147464 | tf_op jit(solution)/shard_map/ppermute | solution.py:50
  9.2 6.4 %collective-permute-start.10 = (f32[8,1536]{1,0:T(8,128)S(1)}, f32[8,1536]{1,0:T(8,128)S(1)}, u32[]{:S(2)}, u32[]{:S(2)}) collective-permute-start(f32[8,1536]{1,0:T(8,128)S(1)} %add.28), channel_id=1, source_target_pairs={{0,4},{1,5},{2,6},{3,7},{4,0},{5,1},{6,2},{7,3},{8,12},{9,13},{10,... | collective-permute-start | bytes 147464 | tf_op jit(solution)/shard_map/ppermute | solution.py:50
  10.8 6.4 %collective-permute-start.1 = (f32[8,1536]{1,0:T(8,128)S(1)}, f32[8,1536]{1,0:T(8,128)S(1)}, u32[]{:S(2)}, u32[]{:S(2)}) collective-permute-start(f32[8,1536]{1,0:T(8,128)S(1)} %add.24), channel_id=1, source_target_pairs={{0,8},{1,9},{2,10},{3,11},{4,12},{5,13},{6,14},{7,15},{8,0},{9,1},... | collective-permute-start | bytes 147464 | tf_op jit(solution)/shard_map/ppermute | solution.py:50
  11.3 10.5 %collective-permute-start.15 = (bf16[2,8,3200]{2,1,0:T(8,128)(2,1)S(1)}, bf16[2,8,3200]{2,1,0:T(8,128)(2,1)S(1)}, u32[]{:S(2)}, u32[]{:S(2)}) collective-permute-start(bf16[2,8,3200]{2,1,0:T(8,128)(2,1)S(1)} %pad_maximum_fusion.4), channel_id=1, source_target_pairs={{0,4},{1,5},{2,6},{3,7},{4,0},{5,1},{6,2},{7,3},{8,12},{9,13},{10,... | collective-permute-start | bytes 307208 | tf_op jit(solution)/shard_map/ppermute | solution.py:50
  12.5 10.2 %collective-permute-start.6 = (bf16[2,8,3200]{2,1,0:T(8,128)(2,1)S(1)}, bf16[2,8,3200]{2,1,0:T(8,128)(2,1)S(1)}, u32[]{:S(2)}, u32[]{:S(2)}) collective-permute-start(bf16[2,8,3200]{2,1,0:T(8,128)(2,1)S(1)} %pad_maximum_fusion.3), channel_id=1, source_target_pairs={{0,8},{1,9},{2,10},{3,11},{4,12},{5,13},{6,14},{7,15},{8,0},{9,1},... | collective-permute-start | bytes 307208 | tf_op jit(solution)/shard_map/ppermute | solution.py:50
  15.6 4.4 %collective-permute-start.11 = (f32[8,1536]{1,0:T(8,128)S(1)}, f32[8,1536]{1,0:T(8,128)S(1)}, u32[]{:S(2)}, u32[]{:S(2)}) collective-permute-start(f32[8,1536]{1,0:T(8,128)S(1)} %add.29), channel_id=1, source_target_pairs={{0,2},{1,3},{2,0},{3,1},{4,6},{5,7},{6,4},{7,5},{8,10},{9,11},{10,... | collective-permute-start | bytes 147464 | tf_op jit(solution)/shard_map/ppermute | solution.py:50
  17.2 4.2 %collective-permute-start.2 = (f32[8,1536]{1,0:T(8,128)S(1)}, f32[8,1536]{1,0:T(8,128)S(1)}, u32[]{:S(2)}, u32[]{:S(2)}) collective-permute-start(f32[8,1536]{1,0:T(8,128)S(1)} %add.25), channel_id=1, source_target_pairs={{0,2},{1,3},{2,0},{3,1},{4,6},{5,7},{6,4},{7,5},{8,10},{9,11},{10,... | collective-permute-start | bytes 147464 | tf_op jit(solution)/shard_map/ppermute | solution.py:50
  20.0 5.4 %collective-permute-start.12 = (f32[8,1536]{1,0:T(8,128)S(1)}, f32[8,1536]{1,0:T(8,128)S(1)}, u32[]{:S(2)}, u32[]{:S(2)}) collective-permute-start(f32[8,1536]{1,0:T(8,128)S(1)} %add.30), channel_id=1, source_target_pairs={{0,8},{1,9},{2,10},{3,11},{4,12},{5,13},{6,14},{7,15},{8,0},{9,1},... | collective-permute-start | bytes 147464 | tf_op jit(solution)/shard_map/ppermute | solution.py:50
  21.4 5.0 %collective-permute-start.3 = (f32[8,1536]{1,0:T(8,128)S(1)}, f32[8,1536]{1,0:T(8,128)S(1)}, u32[]{:S(2)}, u32[]{:S(2)}) collective-permute-start(f32[8,1536]{1,0:T(8,128)S(1)} %add.26), channel_id=1, source_target_pairs={{0,4},{1,5},{2,6},{3,7},{4,0},{5,1},{6,2},{7,3},{8,12},{9,13},{10,... | collective-permute-start | bytes 147464 | tf_op jit(solution)/shard_map/ppermute | solution.py:50
  21.8 6.8 %collective-permute-start.16 = (bf16[4,8,3200]{2,1,0:T(8,128)(2,1)S(1)}, bf16[4,8,3200]{2,1,0:T(8,128)(2,1)S(1)}, u32[]{:S(2)}, u32[]{:S(2)}) collective-permute-start(bf16[4,8,3200]{2,1,0:T(8,128)(2,1)S(1)} %get-tuple-element.25.got), channel_id=1, source_target_pairs={{0,2},{1,3},{2,0},{3,1},{4,6},{5,7},{6,4},{7,5},{8,10},{9,11},{10,... | collective-permute-start | bytes 614408 | tf_op jit(solution)/shard_map/ppermute | solution.py:50
  22.7 6.3 %collective-permute-start.7 = (bf16[4,8,3200]{2,1,0:T(8,128)(2,1)S(1)}, bf16[4,8,3200]{2,1,0:T(8,128)(2,1)S(1)}, u32[]{:S(2)}, u32[]{:S(2)}) collective-permute-start(bf16[4,8,3200]{2,1,0:T(8,128)(2,1)S(1)} %pad_maximum_fusion.2), channel_id=1, source_target_pairs={{0,4},{1,5},{2,6},{3,7},{4,0},{5,1},{6,2},{7,3},{8,12},{9,13},{10,... | collective-permute-start | bytes 614408 | tf_op jit(solution)/shard_map/ppermute | solution.py:50
  25.5 1.3 %collective-permute-start.13 = (f32[8,1536]{1,0:T(8,128)S(1)}, f32[8,1536]{1,0:T(8,128)S(1)}, u32[]{:S(2)}, u32[]{:S(2)}) collective-permute-start(f32[8,1536]{1,0:T(8,128)S(1)} %add.31.own), channel_id=1, source_target_pairs={{0,1},{1,0},{2,3},{3,2},{4,5},{5,4},{6,7},{7,6},{8,9},{9,8},{10,11... | collective-permute-start | bytes 147464 | tf_op jit(solution)/shard_map/ppermute | solution.py:50
  25.5 5.6 %slice-start.2 = ((s8[6291456]{0:T(1024)(128)(4,1)}), s8[4194304]{0:T(1024)(128)(4,1)S(1)}, s32[]{:S(2)}) async-start(s8[6291456]{0:T(1024)(128)(4,1)} %bitcast.2), calls=%async_computation.2 | async-start | bytes 8388608
  26.4 8.5 %collective-permute-start.4 = (f32[8,1536]{1,0:T(8,128)S(1)}, f32[8,1536]{1,0:T(8,128)S(1)}, u32[]{:S(2)}, u32[]{:S(2)}) collective-permute-start(f32[8,1536]{1,0:T(8,128)S(1)} %add.27.own), channel_id=1, source_target_pairs={{0,1},{1,0},{2,3},{3,2},{4,5},{5,4},{6,7},{7,6},{8,9},{9,8},{10,11... | collective-permute-start | bytes 147464 | tf_op jit(solution)/shard_map/ppermute | solution.py:50
  26.7 4.3 %slice-start.3 = ((s8[6291456]{0:T(1024)(128)(4,1)}), s8[2097152]{0:T(1024)(128)(4,1)S(1)}, s32[]{:S(2)}) async-start(s8[6291456]{0:T(1024)(128)(4,1)} %bitcast.2), calls=%async_computation.3 | async-start | bytes 4194304
  28.6 1.8 %collective-permute-start.17 = (bf16[8,8,3200]{2,1,0:T(8,128)(2,1)S(1)}, bf16[8,8,3200]{2,1,0:T(8,128)(2,1)S(1)}, u32[]{:S(2)}, u32[]{:S(2)}) collective-permute-start(bf16[8,8,3200]{2,1,0:T(8,128)(2,1)S(1)} %pad_maximum_fusion.1), channel_id=1, source_target_pairs={{0,1},{1,0},{2,3},{3,2},{4,5},{5,4},{6,7},{7,6},{8,9},{9,8},{10,11... | collective-permute-start | bytes 1228808 | tf_op jit(solution)/shard_map/ppermute | solution.py:50
  29.0 2.0 %collective-permute-start.8 = (bf16[8,8,3200]{2,1,0:T(8,128)(2,1)S(1)}, bf16[8,8,3200]{2,1,0:T(8,128)(2,1)S(1)}, u32[]{:S(2)}, u32[]{:S(2)}) collective-permute-start(bf16[8,8,3200]{2,1,0:T(8,128)(2,1)S(1)} %pad_maximum_fusion), channel_id=1, source_target_pairs={{0,1},{1,0},{2,3},{3,2},{4,5},{5,4},{6,7},{7,6},{8,9},{9,8},{10,11... | collective-permute-start | bytes 1228808 | tf_op jit(solution)/shard_map/ppermute | solution.py:50
  31.0 3.9 %slice-start = ((s8[6291456]{0:T(1024)(128)(4,1)}), s8[4194304]{0:T(1024)(128)(4,1)S(1)}, s32[]{:S(2)}) async-start(s8[6291456]{0:T(1024)(128)(4,1)} %bitcast), calls=%async_computation | async-start | bytes 8388608
  31.1 3.8 %slice-start.1 = ((s8[6291456]{0:T(1024)(128)(4,1)}), s8[2097152]{0:T(1024)(128)(4,1)S(1)}, s32[]{:S(2)}) async-start(s8[6291456]{0:T(1024)(128)(4,1)} %bitcast), calls=%async_computation.1 | async-start | bytes 4194304

commit v6 on v5

--- a/solution.py
+++ b/solution.py
@@ -14,7 +14,7 @@
 LAGW = 1024
 SMOOTH = 64
 LANES = 128
-UNROLL = 3
+UNROLL = 4
 PIECES = 4
 BEGIN = 3 * 10**9
 VMEM = pl.BlockSpec(memory_space=pltpu.VMEM)

time: 40.7 us -> 40.3 us (level)
  transfers between devices with their start and end apart: 18 -> 18, of which waited for: 7 -> 7; matrix products, arithmetic and copies ran while one was open for 1% -> 1% of each run, Pallas kernels for 16% -> 15%
where the time goes in v6:
time: 40.3 us; the launch traced here: 40.1 us
  starting transfers between devices  17.8 us (44%)
  Pallas kernels  11.7 us (29%)
  waiting for transfers between devices  7.44 us (18%)
  between operations  1.53 us (4%)
  local copies, waits for them, and re-layouts  1.34 us (3%)
    ppermute x18, starting transfers between devices, swap(): return lax.ppermute(value, 'chan', [(i, i ^ bit) for i in range(owners)])  17.8 us
    ppermute x18, waiting for transfers between devices, swap(): return lax.ppermute(value, 'chan', [(i, i ^ bit) for i in range(owners)])  7.44 us
    pallas_call x1, Pallas kernels, shards(): pl.pallas_call(functools.partial(correlate, 1, bins, row_order[1], row_or...  5.34 us
    pallas_call x1, Pallas kernels, shards(): pl.pallas_call(functools.partial(finish, 0, bins, first_count, moved, lat...  3.72 us
    pallas_call x1, Pallas kernels, shards(): pl.pallas_call(functools.partial(begin, h, bins, [(2 * receivers * i, m)...  1.66 us
    unnamed x17, local copies, waits for them, and re-layouts  1.25 us
    pallas_call x1, Pallas kernels, shards(): pl.pallas_call(functools.partial(pick_rows, bins), out_shape=(rows, rows,...  0.84 us
  transfers between devices with their start and end apart: 18, of which 7 were waited for; matrix products, arithmetic and copies ran while one was open for 1% of the time, Pallas kernels for 15%

profile of v6, /device:TPU:0, one launch (start us, length us, event | category | flops | bytes accessed | tf_op | source)
XLA Modules:
  0.0 40.1 jit_solution(9977130490167613762)
XLA Ops:
  0.0 0.0 copy-start
  0.0 1.1 %copy-done = bf16[8,8,6144]{2,1,0:T(8,128)(2,1)S(1)} copy-done((bf16[8,8,6144]{2,1,0:T(8,128)(2,1)S(1)}, bf16[8,8,6144]{2,1,0:T(8,128)(2,1)}, u32[]{:S(2)}) %copy-start) | copy-done | bytes 786456
  1.1 0.1 add_channels.1
  1.3 0.5 %collective-permute-start.9 = (f32[8,1536]{1,0:T(8,128)S(1)}, f32[8,1536]{1,0:T(8,128)S(1)}, u32[]{:S(2)}, u32[]{:S(2)}) collective-permute-start(f32[8,1536]{1,0:T(8,128)S(1)} %get-tuple-element.21), channel_id=1, source_target_pairs={{0,1},{1,0},{2,3},{3,2},{4,5},{5,4},{6,7},{7,6},{8,9},{9,8},{10,11... | collective-permute-start | bytes 147464 | tf_op jit(solution)/shard_map/ppermute | solution.py:50
  3.1 0.8 %pick_rows.1 = (bf16[1,8,3200]{2,1,0:T(8,128)(2,1)S(1)}, bf16[1,8,3200]{2,1,0:T(8,128)(2,1)S(1)}, f32[8,8,128]{2,1,0:T(8,128)S(1)}) custom-call(s32[1]{0:T(128)S(6)} %copy.17.source_pick, s32[1]{0:T(128)S(6)} %copy.18.lag_start, s32[8]{0:T(128)} %bad_flag.1, bf16[8,8,6144]{2,1,0:T(8,128)(2,1)} %spectra.3), custom_call_target="tpu_custom_call" | custom-call | tf_op jit(solution)/shard_map/pick_rows/pallas_call | solution.py:368
  3.9 3.7 %collective-permute-start.14 = (bf16[1,8,3200]{2,1,0:T(8,128)(2,1)S(1)}, bf16[1,8,3200]{2,1,0:T(8,128)(2,1)S(1)}, u32[]{:S(2)}, u32[]{:S(2)}) collective-permute-start(bf16[1,8,3200]{2,1,0:T(8,128)(2,1)S(1)} %get-tuple-element.22), channel_id=1, source_target_pairs={{0,8},{1,9},{2,10},{3,11},{4,12},{5,13},{6,14},{7,15},{8,0},{9,1},... | collective-permute-start | bytes 153608 | tf_op jit(solution)/shard_map/ppermute | solution.py:50
  7.6 1.5 %collective-permute-start.5 = (bf16[1,8,3200]{2,1,0:T(8,128)(2,1)S(1)}, bf16[1,8,3200]{2,1,0:T(8,128)(2,1)S(1)}, u32[]{:S(2)}, u32[]{:S(2)}) collective-permute-start(bf16[1,8,3200]{2,1,0:T(8,128)(2,1)S(1)} %get-tuple-element.19), channel_id=1, source_target_pairs={{0,2},{1,3},{2,0},{3,1},{4,6},{5,7},{6,4},{7,5},{8,10},{9,11},{10,... | collective-permute-start | bytes 153608 | tf_op jit(solution)/shard_map/ppermute | solution.py:50
  9.1 0.0 collective-permute-start
  9.2 0.0 collective-permute-done.9
  9.2 1.6 %collective-permute-start.10 = (f32[8,1536]{1,0:T(8,128)S(1)}, f32[8,1536]{1,0:T(8,128)S(1)}, u32[]{:S(2)}, u32[]{:S(2)}) collective-permute-start(f32[8,1536]{1,0:T(8,128)S(1)} %add.28), channel_id=1, source_target_pairs={{0,4},{1,5},{2,6},{3,7},{4,0},{5,1},{6,2},{7,3},{8,12},{9,13},{10,... | collective-permute-start | bytes 147464 | tf_op jit(solution)/shard_map/ppermute | solution.py:50
  10.8 0.0 collective-permute-done
  10.8 0.4 %collective-permute-start.1 = (f32[8,1536]{1,0:T(8,128)S(1)}, f32[8,1536]{1,0:T(8,128)S(1)}, u32[]{:S(2)}, u32[]{:S(2)}) collective-permute-start(f32[8,1536]{1,0:T(8,128)S(1)} %add.24), channel_id=1, source_target_pairs={{0,8},{1,9},{2,10},{3,11},{4,12},{5,13},{6,14},{7,15},{8,0},{9,1},... | collective-permute-start | bytes 147464 | tf_op jit(solution)/shard_map/ppermute | solution.py:50
  11.2 0.0 collective-permute-done.14
  11.3 1.2 %collective-permute-start.15 = (bf16[2,8,3200]{2,1,0:T(8,128)(2,1)S(1)}, bf16[2,8,3200]{2,1,0:T(8,128)(2,1)S(1)}, u32[]{:S(2)}, u32[]{:S(2)}) collective-permute-start(bf16[2,8,3200]{2,1,0:T(8,128)(2,1)S(1)} %pad_maximum_fusion.4), channel_id=1, source_target_pairs={{0,4},{1,5},{2,6},{3,7},{4,0},{5,1},{6,2},{7,3},{8,12},{9,13},{10,... | collective-permute-start | bytes 307208 | tf_op jit(solution)/shard_map/ppermute | solution.py:50
  12.4 0.0 collective-permute-done.5
  12.5 3.1 %collective-permute-start.6 = (bf16[2,8,3200]{2,1,0:T(8,128)(2,1)S(1)}, bf16[2,8,3200]{2,1,0:T(8,128)(2,1)S(1)}, u32[]{:S(2)}, u32[]{:S(2)}) collective-permute-start(bf16[2,8,3200]{2,1,0:T(8,128)(2,1)S(1)} %pad_maximum_fusion.3), channel_id=1, source_target_pairs={{0,8},{1,9},{2,10},{3,11},{4,12},{5,13},{6,14},{7,15},{8,0},{9,1},... | collective-permute-start | bytes 307208 | tf_op jit(solution)/shard_map/ppermute | solution.py:50
  15.6 0.0 collective-permute-done.10
  15.6 1.6 %collective-permute-start.11 = (f32[8,1536]{1,0:T(8,128)S(1)}, f32[8,1536]{1,0:T(8,128)S(1)}, u32[]{:S(2)}, u32[]{:S(2)}) collective-permute-start(f32[8,1536]{1,0:T(8,128)S(1)} %add.29), channel_id=1, source_target_pairs={{0,2},{1,3},{2,0},{3,1},{4,6},{5,7},{6,4},{7,5},{8,10},{9,11},{10,... | collective-permute-start | bytes 147464 | tf_op jit(solution)/shard_map/ppermute | solution.py:50
  17.2 0.0 collective-permute-done.1
  17.2 0.5 %collective-permute-start.2 = (f32[8,1536]{1,0:T(8,128)S(1)}, f32[8,1536]{1,0:T(8,128)S(1)}, u32[]{:S(2)}, u32[]{:S(2)}) collective-permute-start(f32[8,1536]{1,0:T(8,128)S(1)} %add.25), channel_id=1, source_target_pairs={{0,2},{1,3},{2,0},{3,1},{4,6},{5,7},{6,4},{7,5},{8,10},{9,11},{10,... | collective-permute-start | bytes 147464 | tf_op jit(solution)/shard_map/ppermute | solution.py:50
  17.8 2.3 %collective-permute-done.11 = f32[8,1536]{1,0:T(8,128)S(1)} collective-permute-done((f32[8,1536]{1,0:T(8,128)S(1)}, f32[8,1536]{1,0:T(8,128)S(1)}, u32[]{:S(2)}, u32[]{:S(2)}) %collective-permute-start.11) | collective-permute-done | bytes 49184 | tf_op jit(solution)/shard_map/ppermute | solution.py:50
  20.0 0.2 collective-permute-start.12
  20.2 1.1 %collective-permute-done.2 = f32[8,1536]{1,0:T(8,128)S(1)} collective-permute-done((f32[8,1536]{1,0:T(8,128)S(1)}, f32[8,1536]{1,0:T(8,128)S(1)}, u32[]{:S(2)}, u32[]{:S(2)}) %collective-permute-start.2) | collective-permute-done | bytes 49184 | tf_op jit(solution)/shard_map/ppermute | solution.py:50
  21.4 0.4 collective-permute-start.3
  21.7 0.0 collective-permute-done.15
  21.8 0.9 %collective-permute-start.16 = (bf16[4,8,3200]{2,1,0:T(8,128)(2,1)S(1)}, bf16[4,8,3200]{2,1,0:T(8,128)(2,1)S(1)}, u32[]{:S(2)}, u32[]{:S(2)}) collective-permute-start(bf16[4,8,3200]{2,1,0:T(8,128)(2,1)S(1)} %get-tuple-element.25.got), channel_id=1, source_target_pairs={{0,2},{1,3},{2,0},{3,1},{4,6},{5,7},{6,4},{7,5},{8,10},{9,11},{10,... | collective-permute-start | bytes 614408 | tf_op jit(solution)/shard_map/ppermute | solution.py:50
  22.7 0.0 collective-permute-done.6
  22.7 1.4 %collective-permute-start.7 = (bf16[4,8,3200]{2,1,0:T(8,128)(2,1)S(1)}, bf16[4,8,3200]{2,1,0:T(8,128)(2,1)S(1)}, u32[]{:S(2)}, u32[]{:S(2)}) collective-permute-start(bf16[4,8,3200]{2,1,0:T(8,128)(2,1)S(1)} %pad_maximum_fusion.2), channel_id=1, source_target_pairs={{0,4},{1,5},{2,6},{3,7},{4,0},{5,1},{6,2},{7,3},{8,12},{9,13},{10,... | collective-permute-start | bytes 614408 | tf_op jit(solution)/shard_map/ppermute | solution.py:50
  24.1 1.3 %collective-permute-done.12 = f32[8,1536]{1,0:T(8,128)S(1)} collective-permute-done((f32[8,1536]{1,0:T(8,128)S(1)}, f32[8,1536]{1,0:T(8,128)S(1)}, u32[]{:S(2)}, u32[]{:S(2)}) %collective-permute-start.12) | collective-permute-done | bytes 49184 | tf_op jit(solution)/shard_map/ppermute | solution.py:50
  25.5 0.1 collective-permute-start.13
  25.5 0.0 slice-start.2
  25.6 0.9 %collective-permute-done.3 = f32[8,1536]{1,0:T(8,128)S(1)} collective-permute-done((f32[8,1536]{1,0:T(8,128)S(1)}, f32[8,1536]{1,0:T(8,128)S(1)}, u32[]{:S(2)}, u32[]{:S(2)}) %collective-permute-start.3) | collective-permute-done | bytes 49184 | tf_op jit(solution)/shard_map/ppermute | solution.py:50
  26.4 0.1 collective-permute-start.4
  26.5 0.2 collective-permute-done.13.other
  26.7 0.0 slice-start.3
  26.7 1.7 %begin.1 = (f32[12,2,8,8,128]{4,3,2,1,0:T(8,128)S(1)}, bf16[32,3072]{1,0:T(8,128)(2,1)S(1)}) custom-call(f32[8,8,128]{2,1,0:T(8,128)S(1)} %get-tuple-element.15.keep, bf16[8,8,6144]{2,1,0:T(8,128)(2,1)S(1)} %get-tuple-element.16.spectra, f32[8,1536]{1,0:T(8,128)S(1)} %add.31.own, f32[8,1536]{1,0:T(8,128)S(1)} %collective-permute-done.13.other, ...), custom_call_target="tpu_custom_call" | custom-call | flops 3000000000 | bytes 4194304 | tf_op jit(solution)/shard_map/begin/pallas_call | solution.py:415
  28.4 0.0 collective-permute-done.16
  28.4 0.1 pad_maximum_fusion.1
  28.5 0.3 collective-permute-start.17
  28.8 0.0 collective-permute-done.7
  28.8 0.1 pad_maximum_fusion
  28.9 0.3 collective-permute-start.8
  29.2 1.1 %collective-permute-done.17 = bf16[8,8,3200]{2,1,0:T(8,128)(2,1)S(1)} collective-permute-done((bf16[8,8,3200]{2,1,0:T(8,128)(2,1)S(1)}, bf16[8,8,3200]{2,1,0:T(8,128)(2,1)S(1)}, u32[]{:S(2)}, u32[]{:S(2)}) %collective-permute-start.17) | collective-permute-done | bytes 409632 | tf_op jit(solution)/shard_map/ppermute | solution.py:50
  30.3 0.5 %collective-permute-done.8 = bf16[8,8,3200]{2,1,0:T(8,128)(2,1)S(1)} collective-permute-done((bf16[8,8,3200]{2,1,0:T(8,128)(2,1)S(1)}, bf16[8,8,3200]{2,1,0:T(8,128)(2,1)S(1)}, u32[]{:S(2)}, u32[]{:S(2)}) %collective-permute-start.8) | collective-permute-done | bytes 409632 | tf_op jit(solution)/shard_map/ppermute | solution.py:50
  30.9 0.0 slice-start
  30.9 0.0 slice-done.2
  30.9 0.0 slice-done.3
  31.0 0.0 slice-start.1
  31.0 3.7 %finish.1.rest_0_ = f32[128,1024]{1,0:T(8,128)S(1)} custom-call(f32[8,1536]{1,0:T(8,128)S(1)} %add.31.own, f32[8,1536]{1,0:T(8,128)S(1)} %collective-permute-done.13.other, bf16[16,8,3200]{2,1,0:T(8,128)(2,1)S(1)} %constant_dynamic-update-slice_fusion.8.got, f32[12,2,8,8,128]{4,3,2,1,0:T(8,128)S(1)} %get-tuple-element.23.white, ...), custom_call_target="tpu_custom_call" | custom-call | flops 4000000000 | bytes 10485760 | tf_op jit(solution)/shard_map/finish/pallas_call | solution.py:440
  34.7 0.0 collective-permute-done.4.other
  34.7 0.0 slice-done
  34.7 0.0 slice-done.1
  34.7 5.3 %correlate.1 = f32[16,8,1024]{2,1,0:T(8,128)} custom-call(f32[8,8,128]{2,1,0:T(8,128)S(1)} %get-tuple-element.15.keep, bf16[8,8,6144]{2,1,0:T(8,128)(2,1)S(1)} %get-tuple-element.16.spectra, f32[8,1536]{1,0:T(8,128)S(1)} %add.27.own, f32[8,1536]{1,0:T(8,128)S(1)} %collective-permute-done.4.other, ...), custom_call_target="tpu_custom_call" | custom-call | flops 5000000000 | bytes 10485760 | tf_op jit(solution)/shard_map/correlate/pallas_call | solution.py:455
  (23 shorter events, 0.3 us)
Async XLA Ops:
  0.0 1.1 %copy-start = (bf16[8,8,6144]{2,1,0:T(8,128)(2,1)S(1)}, bf16[8,8,6144]{2,1,0:T(8,128)(2,1)}, u32[]{:S(2)}) copy-start(bf16[8,8,6144]{2,1,0:T(8,128)(2,1)} %spectra.3) | copy-start | bytes 2359300
  1.3 7.9 %collective-permute-start.9 = (f32[8,1536]{1,0:T(8,128)S(1)}, f32[8,1536]{1,0:T(8,128)S(1)}, u32[]{:S(2)}, u32[]{:S(2)}) collective-permute-start(f32[8,1536]{1,0:T(8,128)S(1)} %get-tuple-element.21), channel_id=1, source_target_pairs={{0,1},{1,0},{2,3},{3,2},{4,5},{5,4},{6,7},{7,6},{8,9},{9,8},{10,11... | collective-permute-start | bytes 147464 | tf_op jit(solution)/shard_map/ppermute | solution.py:50
  3.9 7.3 %collective-permute-start.14 = (bf16[1,8,3200]{2,1,0:T(8,128)(2,1)S(1)}, bf16[1,8,3200]{2,1,0:T(8,128)(2,1)S(1)}, u32[]{:S(2)}, u32[]{:S(2)}) collective-permute-start(bf16[1,8,3200]{2,1,0:T(8,128)(2,1)S(1)} %get-tuple-element.22), channel_id=1, source_target_pairs={{0,8},{1,9},{2,10},{3,11},{4,12},{5,13},{6,14},{7,15},{8,0},{9,1},... | collective-permute-start | bytes 153608 | tf_op jit(solution)/shard_map/ppermute | solution.py:50
  7.6 4.8 %collective-permute-start.5 = (bf16[1,8,3200]{2,1,0:T(8,128)(2,1)S(1)}, bf16[1,8,3200]{2,1,0:T(8,128)(2,1)S(1)}, u32[]{:S(2)}, u32[]{:S(2)}) collective-permute-start(bf16[1,8,3200]{2,1,0:T(8,128)(2,1)S(1)} %get-tuple-element.19), channel_id=1, source_target_pairs={{0,2},{1,3},{2,0},{3,1},{4,6},{5,7},{6,4},{7,5},{8,10},{9,11},{10,... | collective-permute-start | bytes 153608 | tf_op jit(solution)/shard_map/ppermute | solution.py:50
  9.1 1.7 %collective-permute-start = (f32[8,1536]{1,0:T(8,128)S(1)}, f32[8,1536]{1,0:T(8,128)S(1)}, u32[]{:S(2)}, u32[]{:S(2)}) collective-permute-start(f32[8,1536]{1,0:T(8,128)S(1)} %get-tuple-element.18), channel_id=1, source_target_pairs={{0,1},{1,0},{2,3},{3,2},{4,5},{5,4},{6,7},{7,6},{8,9},{9,8},{10,11... | collective-permute-start | bytes 147464 | tf_op jit(solution)/shard_map/ppermute | solution.py:50
  9.2 6.4 %collective-permute-start.10 = (f32[8,1536]{1,0:T(8,128)S(1)}, f32[8,1536]{1,0:T(8,128)S(1)}, u32[]{:S(2)}, u32[]{:S(2)}) collective-permute-start(f32[8,1536]{1,0:T(8,128)S(1)} %add.28), channel_id=1, source_target_pairs={{0,4},{1,5},{2,6},{3,7},{4,0},{5,1},{6,2},{7,3},{8,12},{9,13},{10,... | collective-permute-start | bytes 147464 | tf_op jit(solution)/shard_map/ppermute | solution.py:50
  10.8 6.4 %collective-permute-start.1 = (f32[8,1536]{1,0:T(8,128)S(1)}, f32[8,1536]{1,0:T(8,128)S(1)}, u32[]{:S(2)}, u32[]{:S(2)}) collective-permute-start(f32[8,1536]{1,0:T(8,128)S(1)} %add.24), channel_id=1, source_target_pairs={{0,8},{1,9},{2,10},{3,11},{4,12},{5,13},{6,14},{7,15},{8,0},{9,1},... | collective-permute-start | bytes 147464 | tf_op jit(solution)/shard_map/ppermute | solution.py:50
  11.3 10.5 %collective-permute-start.15 = (bf16[2,8,3200]{2,1,0:T(8,128)(2,1)S(1)}, bf16[2,8,3200]{2,1,0:T(8,128)(2,1)S(1)}, u32[]{:S(2)}, u32[]{:S(2)}) collective-permute-start(bf16[2,8,3200]{2,1,0:T(8,128)(2,1)S(1)} %pad_maximum_fusion.4), channel_id=1, source_target_pairs={{0,4},{1,5},{2,6},{3,7},{4,0},{5,1},{6,2},{7,3},{8,12},{9,13},{10,... | collective-permute-start | bytes 307208 | tf_op jit(solution)/shard_map/ppermute | solution.py:50
  12.5 10.2 %collective-permute-start.6 = (bf16[2,8,3200]{2,1,0:T(8,128)(2,1)S(1)}, bf16[2,8,3200]{2,1,0:T(8,128)(2,1)S(1)}, u32[]{:S(2)}, u32[]{:S(2)}) collective-permute-start(bf16[2,8,3200]{2,1,0:T(8,128)(2,1)S(1)} %pad_maximum_fusion.3), channel_id=1, source_target_pairs={{0,8},{1,9},{2,10},{3,11},{4,12},{5,13},{6,14},{7,15},{8,0},{9,1},... | collective-permute-start | bytes 307208 | tf_op jit(solution)/shard_map/ppermute | solution.py:50
  15.6 4.4 %collective-permute-start.11 = (f32[8,1536]{1,0:T(8,128)S(1)}, f32[8,1536]{1,0:T(8,128)S(1)}, u32[]{:S(2)}, u32[]{:S(2)}) collective-permute-start(f32[8,1536]{1,0:T(8,128)S(1)} %add.29), channel_id=1, source_target_pairs={{0,2},{1,3},{2,0},{3,1},{4,6},{5,7},{6,4},{7,5},{8,10},{9,11},{10,... | collective-permute-start | bytes 147464 | tf_op jit(solution)/shard_map/ppermute | solution.py:50
  17.2 4.2 %collective-permute-start.2 = (f32[8,1536]{1,0:T(8,128)S(1)}, f32[8,1536]{1,0:T(8,128)S(1)}, u32[]{:S(2)}, u32[]{:S(2)}) collective-permute-start(f32[8,1536]{1,0:T(8,128)S(1)} %add.25), channel_id=1, source_target_pairs={{0,2},{1,3},{2,0},{3,1},{4,6},{5,7},{6,4},{7,5},{8,10},{9,11},{10,... | collective-permute-start | bytes 147464 | tf_op jit(solution)/shard_map/ppermute | solution.py:50
  20.0 5.4 %collective-permute-start.12 = (f32[8,1536]{1,0:T(8,128)S(1)}, f32[8,1536]{1,0:T(8,128)S(1)}, u32[]{:S(2)}, u32[]{:S(2)}) collective-permute-start(f32[8,1536]{1,0:T(8,128)S(1)} %add.30), channel_id=1, source_target_pairs={{0,8},{1,9},{2,10},{3,11},{4,12},{5,13},{6,14},{7,15},{8,0},{9,1},... | collective-permute-start | bytes 147464 | tf_op jit(solution)/shard_map/ppermute | solution.py:50
  21.4 5.0 %collective-permute-start.3 = (f32[8,1536]{1,0:T(8,128)S(1)}, f32[8,1536]{1,0:T(8,128)S(1)}, u32[]{:S(2)}, u32[]{:S(2)}) collective-permute-start(f32[8,1536]{1,0:T(8,128)S(1)} %add.26), channel_id=1, source_target_pairs={{0,4},{1,5},{2,6},{3,7},{4,0},{5,1},{6,2},{7,3},{8,12},{9,13},{10,... | collective-permute-start | bytes 147464 | tf_op jit(solution)/shard_map/ppermute | solution.py:50
  21.8 6.6 %collective-permute-start.16 = (bf16[4,8,3200]{2,1,0:T(8,128)(2,1)S(1)}, bf16[4,8,3200]{2,1,0:T(8,128)(2,1)S(1)}, u32[]{:S(2)}, u32[]{:S(2)}) collective-permute-start(bf16[4,8,3200]{2,1,0:T(8,128)(2,1)S(1)} %get-tuple-element.25.got), channel_id=1, source_target_pairs={{0,2},{1,3},{2,0},{3,1},{4,6},{5,7},{6,4},{7,5},{8,10},{9,11},{10,... | collective-permute-start | bytes 614408 | tf_op jit(solution)/shard_map/ppermute | solution.py:50
  22.7 6.1 %collective-permute-start.7 = (bf16[4,8,3200]{2,1,0:T(8,128)(2,1)S(1)}, bf16[4,8,3200]{2,1,0:T(8,128)(2,1)S(1)}, u32[]{:S(2)}, u32[]{:S(2)}) collective-permute-start(bf16[4,8,3200]{2,1,0:T(8,128)(2,1)S(1)} %pad_maximum_fusion.2), channel_id=1, source_target_pairs={{0,4},{1,5},{2,6},{3,7},{4,0},{5,1},{6,2},{7,3},{8,12},{9,13},{10,... | collective-permute-start | bytes 614408 | tf_op jit(solution)/shard_map/ppermute | solution.py:50
  25.5 1.3 %collective-permute-start.13 = (f32[8,1536]{1,0:T(8,128)S(1)}, f32[8,1536]{1,0:T(8,128)S(1)}, u32[]{:S(2)}, u32[]{:S(2)}) collective-permute-start(f32[8,1536]{1,0:T(8,128)S(1)} %add.31.own), channel_id=1, source_target_pairs={{0,1},{1,0},{2,3},{3,2},{4,5},{5,4},{6,7},{7,6},{8,9},{9,8},{10,11... | collective-permute-start | bytes 147464 | tf_op jit(solution)/shard_map/ppermute | solution.py:50
  25.5 5.4 %slice-start.2 = ((s8[6291456]{0:T(1024)(128)(4,1)}), s8[4194304]{0:T(1024)(128)(4,1)S(1)}, s32[]{:S(2)}) async-start(s8[6291456]{0:T(1024)(128)(4,1)} %bitcast.2), calls=%async_computation.2 | async-start | bytes 8388608
  26.4 8.3 %collective-permute-start.4 = (f32[8,1536]{1,0:T(8,128)S(1)}, f32[8,1536]{1,0:T(8,128)S(1)}, u32[]{:S(2)}, u32[]{:S(2)}) collective-permute-start(f32[8,1536]{1,0:T(8,128)S(1)} %add.27.own), channel_id=1, source_target_pairs={{0,1},{1,0},{2,3},{3,2},{4,5},{5,4},{6,7},{7,6},{8,9},{9,8},{10,11... | collective-permute-start | bytes 147464 | tf_op jit(solution)/shard_map/ppermute | solution.py:50
  26.7 4.2 %slice-start.3 = ((s8[6291456]{0:T(1024)(128)(4,1)}), s8[2097152]{0:T(1024)(128)(4,1)S(1)}, s32[]{:S(2)}) async-start(s8[6291456]{0:T(1024)(128)(4,1)} %bitcast.2), calls=%async_computation.3 | async-start | bytes 4194304
  28.5 1.8 %collective-permute-start.17 = (bf16[8,8,3200]{2,1,0:T(8,128)(2,1)S(1)}, bf16[8,8,3200]{2,1,0:T(8,128)(2,1)S(1)}, u32[]{:S(2)}, u32[]{:S(2)}) collective-permute-start(bf16[8,8,3200]{2,1,0:T(8,128)(2,1)S(1)} %pad_maximum_fusion.1), channel_id=1, source_target_pairs={{0,1},{1,0},{2,3},{3,2},{4,5},{5,4},{6,7},{7,6},{8,9},{9,8},{10,11... | collective-permute-start | bytes 1228808 | tf_op jit(solution)/shard_map/ppermute | solution.py:50
  28.9 2.0 %collective-permute-start.8 = (bf16[8,8,3200]{2,1,0:T(8,128)(2,1)S(1)}, bf16[8,8,3200]{2,1,0:T(8,128)(2,1)S(1)}, u32[]{:S(2)}, u32[]{:S(2)}) collective-permute-start(bf16[8,8,3200]{2,1,0:T(8,128)(2,1)S(1)} %pad_maximum_fusion), channel_id=1, source_target_pairs={{0,1},{1,0},{2,3},{3,2},{4,5},{5,4},{6,7},{7,6},{8,9},{9,8},{10,11... | collective-permute-start | bytes 1228808 | tf_op jit(solution)/shard_map/ppermute | solution.py:50
  30.9 3.8 %slice-start = ((s8[6291456]{0:T(1024)(128)(4,1)}), s8[4194304]{0:T(1024)(128)(4,1)S(1)}, s32[]{:S(2)}) async-start(s8[6291456]{0:T(1024)(128)(4,1)} %bitcast), calls=%async_computation | async-start | bytes 8388608
  31.0 3.8 %slice-start.1 = ((s8[6291456]{0:T(1024)(128)(4,1)}), s8[2097152]{0:T(1024)(128)(4,1)S(1)}, s32[]{:S(2)}) async-start(s8[6291456]{0:T(1024)(128)(4,1)} %bitcast), calls=%async_computation.1 | async-start | bytes 4194304

commit v7 on v6

--- a/solution.py
+++ b/solution.py
@@ -14,7 +14,7 @@
 LAGW = 1024
 SMOOTH = 64
 LANES = 128
-UNROLL = 4
+UNROLL = 6
 PIECES = 4
 BEGIN = 3 * 10**9
 VMEM = pl.BlockSpec(memory_space=pltpu.VMEM)

time: 40.3 us -> 40.4 us (level)
  no operation moved by 1% of the time
where the time goes in v7:
time: 40.4 us; the launch traced here: 40.1 us
  starting transfers between devices  17.8 us (44%)
  Pallas kernels  11.8 us (29%)
  waiting for transfers between devices  7.44 us (18%)
  between operations  1.53 us (4%)
  local copies, waits for them, and re-layouts  1.34 us (3%)
    ppermute x18, starting transfers between devices, swap(): return lax.ppermute(value, 'chan', [(i, i ^ bit) for i in range(owners)])  17.8 us
    ppermute x18, waiting for transfers between devices, swap(): return lax.ppermute(value, 'chan', [(i, i ^ bit) for i in range(owners)])  7.44 us
    pallas_call x1, Pallas kernels, shards(): pl.pallas_call(functools.partial(correlate, 1, bins, row_order[1], row_or...  5.43 us
    pallas_call x1, Pallas kernels, shards(): pl.pallas_call(functools.partial(finish, 0, bins, first_count, moved, lat...  3.73 us
    pallas_call x1, Pallas kernels, shards(): pl.pallas_call(functools.partial(begin, h, bins, [(2 * receivers * i, m)...  1.61 us
    unnamed x17, local copies, waits for them, and re-layouts  1.25 us
    pallas_call x1, Pallas kernels, shards(): pl.pallas_call(functools.partial(pick_rows, bins), out_shape=(rows, rows,...  0.84 us
  transfers between devices with their start and end apart: 18, of which 7 were waited for; matrix products, arithmetic and copies ran while one was open for 1% of the time, Pallas kernels for 15%

profile of v7, /device:TPU:0, one launch (start us, length us, event | category | flops | bytes accessed | tf_op | source)
XLA Modules:
  0.0 40.1 jit_solution(4127349098718524318)
XLA Ops:
  0.0 0.0 copy-start
  0.0 1.1 %copy-done = bf16[8,8,6144]{2,1,0:T(8,128)(2,1)S(1)} copy-done((bf16[8,8,6144]{2,1,0:T(8,128)(2,1)S(1)}, bf16[8,8,6144]{2,1,0:T(8,128)(2,1)}, u32[]{:S(2)}) %copy-start) | copy-done | bytes 786456
  1.1 0.1 add_channels.1
  1.3 0.5 %collective-permute-start.9 = (f32[8,1536]{1,0:T(8,128)S(1)}, f32[8,1536]{1,0:T(8,128)S(1)}, u32[]{:S(2)}, u32[]{:S(2)}) collective-permute-start(f32[8,1536]{1,0:T(8,128)S(1)} %get-tuple-element.21), channel_id=1, source_target_pairs={{0,1},{1,0},{2,3},{3,2},{4,5},{5,4},{6,7},{7,6},{8,9},{9,8},{10,11... | collective-permute-start | bytes 147464 | tf_op jit(solution)/shard_map/ppermute | solution.py:50
  3.1 0.8 %pick_rows.1 = (bf16[1,8,3200]{2,1,0:T(8,128)(2,1)S(1)}, bf16[1,8,3200]{2,1,0:T(8,128)(2,1)S(1)}, f32[8,8,128]{2,1,0:T(8,128)S(1)}) custom-call(s32[1]{0:T(128)S(6)} %copy.17.source_pick, s32[1]{0:T(128)S(6)} %copy.18.lag_start, s32[8]{0:T(128)} %bad_flag.1, bf16[8,8,6144]{2,1,0:T(8,128)(2,1)} %spectra.3), custom_call_target="tpu_custom_call" | custom-call | tf_op jit(solution)/shard_map/pick_rows/pallas_call | solution.py:368
  3.9 3.7 %collective-permute-start.14 = (bf16[1,8,3200]{2,1,0:T(8,128)(2,1)S(1)}, bf16[1,8,3200]{2,1,0:T(8,128)(2,1)S(1)}, u32[]{:S(2)}, u32[]{:S(2)}) collective-permute-start(bf16[1,8,3200]{2,1,0:T(8,128)(2,1)S(1)} %get-tuple-element.22), channel_id=1, source_target_pairs={{0,8},{1,9},{2,10},{3,11},{4,12},{5,13},{6,14},{7,15},{8,0},{9,1},... | collective-permute-start | bytes 153608 | tf_op jit(solution)/shard_map/ppermute | solution.py:50
  7.6 1.5 %collective-permute-start.5 = (bf16[1,8,3200]{2,1,0:T(8,128)(2,1)S(1)}, bf16[1,8,3200]{2,1,0:T(8,128)(2,1)S(1)}, u32[]{:S(2)}, u32[]{:S(2)}) collective-permute-start(bf16[1,8,3200]{2,1,0:T(8,128)(2,1)S(1)} %get-tuple-element.19), channel_id=1, source_target_pairs={{0,2},{1,3},{2,0},{3,1},{4,6},{5,7},{6,4},{7,5},{8,10},{9,11},{10,... | collective-permute-start | bytes 153608 | tf_op jit(solution)/shard_map/ppermute | solution.py:50
  9.1 0.0 collective-permute-start
  9.2 0.0 collective-permute-done.9
  9.2 1.6 %collective-permute-start.10 = (f32[8,1536]{1,0:T(8,128)S(1)}, f32[8,1536]{1,0:T(8,128)S(1)}, u32[]{:S(2)}, u32[]{:S(2)}) collective-permute-start(f32[8,1536]{1,0:T(8,128)S(1)} %add.28), channel_id=1, source_target_pairs={{0,4},{1,5},{2,6},{3,7},{4,0},{5,1},{6,2},{7,3},{8,12},{9,13},{10,... | collective-permute-start | bytes 147464 | tf_op jit(solution)/shard_map/ppermute | solution.py:50
  10.8 0.0 collective-permute-done
  10.8 0.4 collective-permute-start.1
  11.2 0.0 collective-permute-done.14
  11.3 1.2 %collective-permute-start.15 = (bf16[2,8,3200]{2,1,0:T(8,128)(2,1)S(1)}, bf16[2,8,3200]{2,1,0:T(8,128)(2,1)S(1)}, u32[]{:S(2)}, u32[]{:S(2)}) collective-permute-start(bf16[2,8,3200]{2,1,0:T(8,128)(2,1)S(1)} %pad_maximum_fusion.4), channel_id=1, source_target_pairs={{0,4},{1,5},{2,6},{3,7},{4,0},{5,1},{6,2},{7,3},{8,12},{9,13},{10,... | collective-permute-start | bytes 307208 | tf_op jit(solution)/shard_map/ppermute | solution.py:50
  12.4 0.0 collective-permute-done.5
  12.5 3.1 %collective-permute-start.6 = (bf16[2,8,3200]{2,1,0:T(8,128)(2,1)S(1)}, bf16[2,8,3200]{2,1,0:T(8,128)(2,1)S(1)}, u32[]{:S(2)}, u32[]{:S(2)}) collective-permute-start(bf16[2,8,3200]{2,1,0:T(8,128)(2,1)S(1)} %pad_maximum_fusion.3), channel_id=1, source_target_pairs={{0,8},{1,9},{2,10},{3,11},{4,12},{5,13},{6,14},{7,15},{8,0},{9,1},... | collective-permute-start | bytes 307208 | tf_op jit(solution)/shard_map/ppermute | solution.py:50
  15.6 0.0 collective-permute-done.10
  15.6 1.6 %collective-permute-start.11 = (f32[8,1536]{1,0:T(8,128)S(1)}, f32[8,1536]{1,0:T(8,128)S(1)}, u32[]{:S(2)}, u32[]{:S(2)}) collective-permute-start(f32[8,1536]{1,0:T(8,128)S(1)} %add.29), channel_id=1, source_target_pairs={{0,2},{1,3},{2,0},{3,1},{4,6},{5,7},{6,4},{7,5},{8,10},{9,11},{10,... | collective-permute-start | bytes 147464 | tf_op jit(solution)/shard_map/ppermute | solution.py:50
  17.2 0.0 collective-permute-done.1
  17.2 0.5 %collective-permute-start.2 = (f32[8,1536]{1,0:T(8,128)S(1)}, f32[8,1536]{1,0:T(8,128)S(1)}, u32[]{:S(2)}, u32[]{:S(2)}) collective-permute-start(f32[8,1536]{1,0:T(8,128)S(1)} %add.25), channel_id=1, source_target_pairs={{0,2},{1,3},{2,0},{3,1},{4,6},{5,7},{6,4},{7,5},{8,10},{9,11},{10,... | collective-permute-start | bytes 147464 | tf_op jit(solution)/shard_map/ppermute | solution.py:50
  17.8 2.3 %collective-permute-done.11 = f32[8,1536]{1,0:T(8,128)S(1)} collective-permute-done((f32[8,1536]{1,0:T(8,128)S(1)}, f32[8,1536]{1,0:T(8,128)S(1)}, u32[]{:S(2)}, u32[]{:S(2)}) %collective-permute-start.11) | collective-permute-done | bytes 49184 | tf_op jit(solution)/shard_map/ppermute | solution.py:50
  20.0 0.2 collective-permute-start.12
  20.2 1.1 %collective-permute-done.2 = f32[8,1536]{1,0:T(8,128)S(1)} collective-permute-done((f32[8,1536]{1,0:T(8,128)S(1)}, f32[8,1536]{1,0:T(8,128)S(1)}, u32[]{:S(2)}, u32[]{:S(2)}) %collective-permute-start.2) | collective-permute-done | bytes 49184 | tf_op jit(solution)/shard_map/ppermute | solution.py:50
  21.4 0.4 collective-permute-start.3
  21.7 0.0 collective-permute-done.15
  21.8 0.9 %collective-permute-start.16 = (bf16[4,8,3200]{2,1,0:T(8,128)(2,1)S(1)}, bf16[4,8,3200]{2,1,0:T(8,128)(2,1)S(1)}, u32[]{:S(2)}, u32[]{:S(2)}) collective-permute-start(bf16[4,8,3200]{2,1,0:T(8,128)(2,1)S(1)} %get-tuple-element.25.got), channel_id=1, source_target_pairs={{0,2},{1,3},{2,0},{3,1},{4,6},{5,7},{6,4},{7,5},{8,10},{9,11},{10,... | collective-permute-start | bytes 614408 | tf_op jit(solution)/shard_map/ppermute | solution.py:50
  22.7 0.0 collective-permute-done.6
  22.7 1.4 %collective-permute-start.7 = (bf16[4,8,3200]{2,1,0:T(8,128)(2,1)S(1)}, bf16[4,8,3200]{2,1,0:T(8,128)(2,1)S(1)}, u32[]{:S(2)}, u32[]{:S(2)}) collective-permute-start(bf16[4,8,3200]{2,1,0:T(8,128)(2,1)S(1)} %pad_maximum_fusion.2), channel_id=1, source_target_pairs={{0,4},{1,5},{2,6},{3,7},{4,0},{5,1},{6,2},{7,3},{8,12},{9,13},{10,... | collective-permute-start | bytes 614408 | tf_op jit(solution)/shard_map/ppermute | solution.py:50
  24.1 1.3 %collective-permute-done.12 = f32[8,1536]{1,0:T(8,128)S(1)} collective-permute-done((f32[8,1536]{1,0:T(8,128)S(1)}, f32[8,1536]{1,0:T(8,128)S(1)}, u32[]{:S(2)}, u32[]{:S(2)}) %collective-permute-start.12) | collective-permute-done | bytes 49184 | tf_op jit(solution)/shard_map/ppermute | solution.py:50
  25.5 0.1 collective-permute-start.13
  25.5 0.0 slice-start.2
  25.6 0.9 %collective-permute-done.3 = f32[8,1536]{1,0:T(8,128)S(1)} collective-permute-done((f32[8,1536]{1,0:T(8,128)S(1)}, f32[8,1536]{1,0:T(8,128)S(1)}, u32[]{:S(2)}, u32[]{:S(2)}) %collective-permute-start.3) | collective-permute-done | bytes 49184 | tf_op jit(solution)/shard_map/ppermute | solution.py:50
  26.4 0.1 collective-permute-start.4
  26.5 0.2 collective-permute-done.13.other
  26.7 0.0 slice-start.3
  26.7 1.6 %begin.1 = (f32[12,2,8,8,128]{4,3,2,1,0:T(8,128)S(1)}, bf16[32,3072]{1,0:T(8,128)(2,1)S(1)}) custom-call(f32[8,8,128]{2,1,0:T(8,128)S(1)} %get-tuple-element.15.keep, bf16[8,8,6144]{2,1,0:T(8,128)(2,1)S(1)} %get-tuple-element.16.spectra, f32[8,1536]{1,0:T(8,128)S(1)} %add.31.own, f32[8,1536]{1,0:T(8,128)S(1)} %collective-permute-done.13.other, ...), custom_call_target="tpu_custom_call" | custom-call | flops 3000000000 | bytes 4194304 | tf_op jit(solution)/shard_map/begin/pallas_call | solution.py:415
  28.4 0.0 collective-permute-done.16
  28.4 0.1 pad_maximum_fusion.1
  28.4 0.3 collective-permute-start.17
  28.8 0.0 collective-permute-done.7
  28.8 0.1 pad_maximum_fusion
  28.8 0.3 collective-permute-start.8
  29.2 1.1 %collective-permute-done.17 = bf16[8,8,3200]{2,1,0:T(8,128)(2,1)S(1)} collective-permute-done((bf16[8,8,3200]{2,1,0:T(8,128)(2,1)S(1)}, bf16[8,8,3200]{2,1,0:T(8,128)(2,1)S(1)}, u32[]{:S(2)}, u32[]{:S(2)}) %collective-permute-start.17) | collective-permute-done | bytes 409632 | tf_op jit(solution)/shard_map/ppermute | solution.py:50
  30.3 0.5 %collective-permute-done.8 = bf16[8,8,3200]{2,1,0:T(8,128)(2,1)S(1)} collective-permute-done((bf16[8,8,3200]{2,1,0:T(8,128)(2,1)S(1)}, bf16[8,8,3200]{2,1,0:T(8,128)(2,1)S(1)}, u32[]{:S(2)}, u32[]{:S(2)}) %collective-permute-start.8) | collective-permute-done | bytes 409632 | tf_op jit(solution)/shard_map/ppermute | solution.py:50
  30.8 0.0 slice-start
  30.9 0.0 slice-done.2
  30.9 0.0 slice-done.3
  30.9 0.0 slice-start.1
  30.9 3.7 %finish.1.rest_0_ = f32[128,1024]{1,0:T(8,128)S(1)} custom-call(f32[8,1536]{1,0:T(8,128)S(1)} %add.31.own, f32[8,1536]{1,0:T(8,128)S(1)} %collective-permute-done.13.other, bf16[16,8,3200]{2,1,0:T(8,128)(2,1)S(1)} %constant_dynamic-update-slice_fusion.8.got, f32[12,2,8,8,128]{4,3,2,1,0:T(8,128)S(1)} %get-tuple-element.23.white, ...), custom_call_target="tpu_custom_call" | custom-call | flops 4000000000 | bytes 10485760 | tf_op jit(solution)/shard_map/finish/pallas_call | solution.py:440
  34.7 0.0 collective-permute-done.4.other
  34.7 0.0 slice-done
  34.7 0.0 slice-done.1
  34.7 5.4 %correlate.1 = f32[16,8,1024]{2,1,0:T(8,128)} custom-call(f32[8,8,128]{2,1,0:T(8,128)S(1)} %get-tuple-element.15.keep, bf16[8,8,6144]{2,1,0:T(8,128)(2,1)S(1)} %get-tuple-element.16.spectra, f32[8,1536]{1,0:T(8,128)S(1)} %add.27.own, f32[8,1536]{1,0:T(8,128)S(1)} %collective-permute-done.4.other, ...), custom_call_target="tpu_custom_call" | custom-call | flops 5000000000 | bytes 10485760 | tf_op jit(solution)/shard_map/correlate/pallas_call | solution.py:455
  (23 shorter events, 0.3 us)
Async XLA Ops:
  0.0 1.1 %copy-start = (bf16[8,8,6144]{2,1,0:T(8,128)(2,1)S(1)}, bf16[8,8,6144]{2,1,0:T(8,128)(2,1)}, u32[]{:S(2)}) copy-start(bf16[8,8,6144]{2,1,0:T(8,128)(2,1)} %spectra.3) | copy-start | bytes 2359300
  1.3 7.9 %collective-permute-start.9 = (f32[8,1536]{1,0:T(8,128)S(1)}, f32[8,1536]{1,0:T(8,128)S(1)}, u32[]{:S(2)}, u32[]{:S(2)}) collective-permute-start(f32[8,1536]{1,0:T(8,128)S(1)} %get-tuple-element.21), channel_id=1, source_target_pairs={{0,1},{1,0},{2,3},{3,2},{4,5},{5,4},{6,7},{7,6},{8,9},{9,8},{10,11... | collective-permute-start | bytes 147464 | tf_op jit(solution)/shard_map/ppermute | solution.py:50
  3.9 7.3 %collective-permute-start.14 = (bf16[1,8,3200]{2,1,0:T(8,128)(2,1)S(1)}, bf16[1,8,3200]{2,1,0:T(8,128)(2,1)S(1)}, u32[]{:S(2)}, u32[]{:S(2)}) collective-permute-start(bf16[1,8,3200]{2,1,0:T(8,128)(2,1)S(1)} %get-tuple-element.22), channel_id=1, source_target_pairs={{0,8},{1,9},{2,10},{3,11},{4,12},{5,13},{6,14},{7,15},{8,0},{9,1},... | collective-permute-start | bytes 153608 | tf_op jit(solution)/shard_map/ppermute | solution.py:50
  7.6 4.8 %collective-permute-start.5 = (bf16[1,8,3200]{2,1,0:T(8,128)(2,1)S(1)}, bf16[1,8,3200]{2,1,0:T(8,128)(2,1)S(1)}, u32[]{:S(2)}, u32[]{:S(2)}) collective-permute-start(bf16[1,8,3200]{2,1,0:T(8,128)(2,1)S(1)} %get-tuple-element.19), channel_id=1, source_target_pairs={{0,2},{1,3},{2,0},{3,1},{4,6},{5,7},{6,4},{7,5},{8,10},{9,11},{10,... | collective-permute-start | bytes 153608 | tf_op jit(solution)/shard_map/ppermute | solution.py:50
  9.1 1.7 %collective-permute-start = (f32[8,1536]{1,0:T(8,128)S(1)}, f32[8,1536]{1,0:T(8,128)S(1)}, u32[]{:S(2)}, u32[]{:S(2)}) collective-permute-start(f32[8,1536]{1,0:T(8,128)S(1)} %get-tuple-element.18), channel_id=1, source_target_pairs={{0,1},{1,0},{2,3},{3,2},{4,5},{5,4},{6,7},{7,6},{8,9},{9,8},{10,11... | collective-permute-start | bytes 147464 | tf_op jit(solution)/shard_map/ppermute | solution.py:50
  9.2 6.4 %collective-permute-start.10 = (f32[8,1536]{1,0:T(8,128)S(1)}, f32[8,1536]{1,0:T(8,128)S(1)}, u32[]{:S(2)}, u32[]{:S(2)}) collective-permute-start(f32[8,1536]{1,0:T(8,128)S(1)} %add.28), channel_id=1, source_target_pairs={{0,4},{1,5},{2,6},{3,7},{4,0},{5,1},{6,2},{7,3},{8,12},{9,13},{10,... | collective-permute-start | bytes 147464 | tf_op jit(solution)/shard_map/ppermute | solution.py:50
  10.8 6.4 %collective-permute-start.1 = (f32[8,1536]{1,0:T(8,128)S(1)}, f32[8,1536]{1,0:T(8,128)S(1)}, u32[]{:S(2)}, u32[]{:S(2)}) collective-permute-start(f32[8,1536]{1,0:T(8,128)S(1)} %add.24), channel_id=1, source_target_pairs={{0,8},{1,9},{2,10},{3,11},{4,12},{5,13},{6,14},{7,15},{8,0},{9,1},... | collective-permute-start | bytes 147464 | tf_op jit(solution)/shard_map/ppermute | solution.py:50
  11.3 10.5 %collective-permute-start.15 = (bf16[2,8,3200]{2,1,0:T(8,128)(2,1)S(1)}, bf16[2,8,3200]{2,1,0:T(8,128)(2,1)S(1)}, u32[]{:S(2)}, u32[]{:S(2)}) collective-permute-start(bf16[2,8,3200]{2,1,0:T(8,128)(2,1)S(1)} %pad_maximum_fusion.4), channel_id=1, source_target_pairs={{0,4},{1,5},{2,6},{3,7},{4,0},{5,1},{6,2},{7,3},{8,12},{9,13},{10,... | collective-permute-start | bytes 307208 | tf_op jit(solution)/shard_map/ppermute | solution.py:50
  12.5 10.2 %collective-permute-start.6 = (bf16[2,8,3200]{2,1,0:T(8,128)(2,1)S(1)}, bf16[2,8,3200]{2,1,0:T(8,128)(2,1)S(1)}, u32[]{:S(2)}, u32[]{:S(2)}) collective-permute-start(bf16[2,8,3200]{2,1,0:T(8,128)(2,1)S(1)} %pad_maximum_fusion.3), channel_id=1, source_target_pairs={{0,8},{1,9},{2,10},{3,11},{4,12},{5,13},{6,14},{7,15},{8,0},{9,1},... | collective-permute-start | bytes 307208 | tf_op jit(solution)/shard_map/ppermute | solution.py:50
  15.6 4.4 %collective-permute-start.11 = (f32[8,1536]{1,0:T(8,128)S(1)}, f32[8,1536]{1,0:T(8,128)S(1)}, u32[]{:S(2)}, u32[]{:S(2)}) collective-permute-start(f32[8,1536]{1,0:T(8,128)S(1)} %add.29), channel_id=1, source_target_pairs={{0,2},{1,3},{2,0},{3,1},{4,6},{5,7},{6,4},{7,5},{8,10},{9,11},{10,... | collective-permute-start | bytes 147464 | tf_op jit(solution)/shard_map/ppermute | solution.py:50
  17.2 4.2 %collective-permute-start.2 = (f32[8,1536]{1,0:T(8,128)S(1)}, f32[8,1536]{1,0:T(8,128)S(1)}, u32[]{:S(2)}, u32[]{:S(2)}) collective-permute-start(f32[8,1536]{1,0:T(8,128)S(1)} %add.25), channel_id=1, source_target_pairs={{0,2},{1,3},{2,0},{3,1},{4,6},{5,7},{6,4},{7,5},{8,10},{9,11},{10,... | collective-permute-start | bytes 147464 | tf_op jit(solution)/shard_map/ppermute | solution.py:50
  20.0 5.4 %collective-permute-start.12 = (f32[8,1536]{1,0:T(8,128)S(1)}, f32[8,1536]{1,0:T(8,128)S(1)}, u32[]{:S(2)}, u32[]{:S(2)}) collective-permute-start(f32[8,1536]{1,0:T(8,128)S(1)} %add.30), channel_id=1, source_target_pairs={{0,8},{1,9},{2,10},{3,11},{4,12},{5,13},{6,14},{7,15},{8,0},{9,1},... | collective-permute-start | bytes 147464 | tf_op jit(solution)/shard_map/ppermute | solution.py:50
  21.4 5.0 %collective-permute-start.3 = (f32[8,1536]{1,0:T(8,128)S(1)}, f32[8,1536]{1,0:T(8,128)S(1)}, u32[]{:S(2)}, u32[]{:S(2)}) collective-permute-start(f32[8,1536]{1,0:T(8,128)S(1)} %add.26), channel_id=1, source_target_pairs={{0,4},{1,5},{2,6},{3,7},{4,0},{5,1},{6,2},{7,3},{8,12},{9,13},{10,... | collective-permute-start | bytes 147464 | tf_op jit(solution)/shard_map/ppermute | solution.py:50
  21.8 6.6 %collective-permute-start.16 = (bf16[4,8,3200]{2,1,0:T(8,128)(2,1)S(1)}, bf16[4,8,3200]{2,1,0:T(8,128)(2,1)S(1)}, u32[]{:S(2)}, u32[]{:S(2)}) collective-permute-start(bf16[4,8,3200]{2,1,0:T(8,128)(2,1)S(1)} %get-tuple-element.25.got), channel_id=1, source_target_pairs={{0,2},{1,3},{2,0},{3,1},{4,6},{5,7},{6,4},{7,5},{8,10},{9,11},{10,... | collective-permute-start | bytes 614408 | tf_op jit(solution)/shard_map/ppermute | solution.py:50
  22.7 6.0 %collective-permute-start.7 = (bf16[4,8,3200]{2,1,0:T(8,128)(2,1)S(1)}, bf16[4,8,3200]{2,1,0:T(8,128)(2,1)S(1)}, u32[]{:S(2)}, u32[]{:S(2)}) collective-permute-start(bf16[4,8,3200]{2,1,0:T(8,128)(2,1)S(1)} %pad_maximum_fusion.2), channel_id=1, source_target_pairs={{0,4},{1,5},{2,6},{3,7},{4,0},{5,1},{6,2},{7,3},{8,12},{9,13},{10,... | collective-permute-start | bytes 614408 | tf_op jit(solution)/shard_map/ppermute | solution.py:50
  25.5 1.3 %collective-permute-start.13 = (f32[8,1536]{1,0:T(8,128)S(1)}, f32[8,1536]{1,0:T(8,128)S(1)}, u32[]{:S(2)}, u32[]{:S(2)}) collective-permute-start(f32[8,1536]{1,0:T(8,128)S(1)} %add.31.own), channel_id=1, source_target_pairs={{0,1},{1,0},{2,3},{3,2},{4,5},{5,4},{6,7},{7,6},{8,9},{9,8},{10,11... | collective-permute-start | bytes 147464 | tf_op jit(solution)/shard_map/ppermute | solution.py:50
  25.5 5.4 %slice-start.2 = ((s8[6291456]{0:T(1024)(128)(4,1)}), s8[4194304]{0:T(1024)(128)(4,1)S(1)}, s32[]{:S(2)}) async-start(s8[6291456]{0:T(1024)(128)(4,1)} %bitcast.2), calls=%async_computation.2 | async-start | bytes 8388608
  26.4 8.2 %collective-permute-start.4 = (f32[8,1536]{1,0:T(8,128)S(1)}, f32[8,1536]{1,0:T(8,128)S(1)}, u32[]{:S(2)}, u32[]{:S(2)}) collective-permute-start(f32[8,1536]{1,0:T(8,128)S(1)} %add.27.own), channel_id=1, source_target_pairs={{0,1},{1,0},{2,3},{3,2},{4,5},{5,4},{6,7},{7,6},{8,9},{9,8},{10,11... | collective-permute-start | bytes 147464 | tf_op jit(solution)/shard_map/ppermute | solution.py:50
  26.7 4.1 %slice-start.3 = ((s8[6291456]{0:T(1024)(128)(4,1)}), s8[2097152]{0:T(1024)(128)(4,1)S(1)}, s32[]{:S(2)}) async-start(s8[6291456]{0:T(1024)(128)(4,1)} %bitcast.2), calls=%async_computation.3 | async-start | bytes 4194304
  28.4 1.8 %collective-permute-start.17 = (bf16[8,8,3200]{2,1,0:T(8,128)(2,1)S(1)}, bf16[8,8,3200]{2,1,0:T(8,128)(2,1)S(1)}, u32[]{:S(2)}, u32[]{:S(2)}) collective-permute-start(bf16[8,8,3200]{2,1,0:T(8,128)(2,1)S(1)} %pad_maximum_fusion.1), channel_id=1, source_target_pairs={{0,1},{1,0},{2,3},{3,2},{4,5},{5,4},{6,7},{7,6},{8,9},{9,8},{10,11... | collective-permute-start | bytes 1228808 | tf_op jit(solution)/shard_map/ppermute | solution.py:50
  28.8 2.0 %collective-permute-start.8 = (bf16[8,8,3200]{2,1,0:T(8,128)(2,1)S(1)}, bf16[8,8,3200]{2,1,0:T(8,128)(2,1)S(1)}, u32[]{:S(2)}, u32[]{:S(2)}) collective-permute-start(bf16[8,8,3200]{2,1,0:T(8,128)(2,1)S(1)} %pad_maximum_fusion), channel_id=1, source_target_pairs={{0,1},{1,0},{2,3},{3,2},{4,5},{5,4},{6,7},{7,6},{8,9},{9,8},{10,11... | collective-permute-start | bytes 1228808 | tf_op jit(solution)/shard_map/ppermute | solution.py:50
  30.8 3.8 %slice-start = ((s8[6291456]{0:T(1024)(128)(4,1)}), s8[4194304]{0:T(1024)(128)(4,1)S(1)}, s32[]{:S(2)}) async-start(s8[6291456]{0:T(1024)(128)(4,1)} %bitcast), calls=%async_computation | async-start | bytes 8388608
  30.9 3.8 %slice-start.1 = ((s8[6291456]{0:T(1024)(128)(4,1)}), s8[2097152]{0:T(1024)(128)(4,1)S(1)}, s32[]{:S(2)}) async-start(s8[6291456]{0:T(1024)(128)(4,1)} %bitcast), calls=%async_computation.1 | async-start | bytes 4194304
